TPU v7x, 32 devices: a whole 2x2x4 slice. The times are simulated.
32 devices in a mesh: fsdp: 4 (over x, core), ctx: 4 (over z), tp: 2 (over y).
Axes of the slice: x: 2, y: 2, z: 4, core: 2. Of those that a mesh axis runs over, the one named last changes fastest.
Arguments:
- tokens: bfloat16 [8, 4096, 768], P('fsdp', 'ctx'), may hold values from -6 to 6
- qkv_weight: bfloat16 [768, 3, 768], P(('fsdp', 'ctx'), None, 'tp'), may hold values from -0.21875 to 0.21875
- qv_bias: bfloat16 [2, 768], P(None, 'tp'), may hold values from -3 to 3
- out_weight: bfloat16 [768, 768], P(('fsdp', 'ctx'), 'tp'), may hold values from -8 to 8
- up_weight: bfloat16 [768, 3072], P(('fsdp', 'ctx'), 'tp'), may hold values from -0.21875 to 0.21875
- up_bias: bfloat16 [3072], P('tp'), may hold values from -3 to 3
- down_weight: bfloat16 [768, 3072], P(('fsdp', 'ctx'), 'tp'), may hold values from -0.109375 to 0.109375
- norm_gains: bfloat16 [768, 2], P(('fsdp', 'ctx')), may hold values from 0.5 to 1.5
- row_biases: bfloat16 [768, 4], P(('fsdp', 'ctx')), may hold values from -3 to 3
- cotangent: bfloat16 [8, 4096, 768], P('fsdp', 'ctx'), may hold values from -6 to 6
Outputs:
- output: bfloat16 [8, 4096, 768], P('fsdp', ('ctx', 'tp'))
- tokens_grad: bfloat16 [8, 4096, 768], P('fsdp', ('ctx', 'tp'))
- qkv_weight_grad: float32 [768, 3, 768], P(('fsdp', 'ctx'), None, 'tp')
- qv_bias_grad: float32 [2, 768], P(None, 'tp')
- out_weight_grad: float32 [768, 768], P(('fsdp', 'ctx'), 'tp')
- up_weight_grad: float32 [768, 3072], P(('fsdp', 'ctx'), 'tp')
- up_bias_grad: float32 [3072], P('tp')
- down_weight_grad: float32 [768, 3072], P(('fsdp', 'ctx'), 'tp')
- norm_gains_grad: float32 [768, 2], P(('fsdp', 'ctx'))
- row_biases_grad: float32 [768, 4], P(('fsdp', 'ctx'))
All inputs are finite; a program needn't handle non-finite values.
Results may differ from a plain program's by a relative error of at most 0.02.
Values may be sent and summed in bfloat16 or wider, within the bound.
No kernel may reach another device: no remote copies, remote signals or barrier semaphores. Data moves between devices by JAX's collectives and lax.ppermute only.
A program may use at most 256 MiB of HBM per device.

v0:
```python
import jax
import jax.numpy as jnp
from jax import lax
from jax.sharding import PartitionSpec as P

HD = 64


epsilon = 1e-12
score_scale = 0.125
highest = lax.Precision.HIGHEST


def contract_last(left, right):
    return lax.dot_general(
        left, right, (((1,), (1,)), ((), ())), preferred_element_type=jnp.float32
    )


def contract_first(left, right):
    return lax.dot_general(
        left, right, (((0,), (0,)), ((), ())), preferred_element_type=jnp.float32
    )


def norm_forward(hidden, gain, shift):
    center = hidden - jnp.mean(hidden, axis=-1, keepdims=True)
    inv_scale = lax.rsqrt(jnp.mean(center * center, axis=-1, keepdims=True) + epsilon)
    normed = center * inv_scale
    return (normed * gain + shift, normed, inv_scale)


def norm_backward(grad_out, normed, inv_scale, gain):
    grad_norm = grad_out * gain
    return inv_scale * (
        grad_norm
        - jnp.mean(grad_norm, axis=-1, keepdims=True)
        - normed * jnp.mean(grad_norm * normed, axis=-1, keepdims=True)
    )


def gelu_exact(values):
    return jax.nn.gelu(values, approximate=False)


def split_heads(array, first_row, row_count, head_count):
    piece = lax.dynamic_slice_in_dim(array, first_row, row_count, 1)
    return piece.reshape(piece.shape[0], row_count, head_count, piece.shape[2] // head_count)


def block_scores(query_four, key_four):
    return (
        jnp.einsum("sqhd,skhd->shqk", query_four, key_four, preferred_element_type=jnp.float32)
        * score_scale
    )


def softmax_rows(scores, row_max, row_total):
    return jnp.exp(scores - row_max[..., None]) / row_total[..., None]


def score_grads(scores, row_max, row_total, row_delta, grad_four, value_four):
    prob_full = softmax_rows(scores, row_max, row_total)
    prob_grad = jnp.einsum(
        "sqhd,skhd->shqk", grad_four, value_four, preferred_element_type=jnp.float32
    )
    score_low = (prob_full * (prob_grad - row_delta[..., None])).astype(jnp.bfloat16)
    return (prob_full.astype(jnp.bfloat16), score_low)


def body(
    tokens,
    qkv_weight,
    qv_bias,
    out_weight,
    up_weight,
    up_bias,
    down_weight,
    norm_gains,
    row_biases,
    cotangent,
):
    seq_count, local_len, width = tokens.shape
    row_count = seq_count * local_len
    tp_count = lax.axis_size("tp")
    share_len = local_len // tp_count
    share_start = lax.axis_index("tp") * share_len

    def own_rows(array_three):
        return lax.dynamic_slice_in_dim(array_three, share_start, share_len, 1)

    def to_three(array_two):
        return array_two.reshape(seq_count, array_two.shape[0] // seq_count, array_two.shape[1])

    gathered = (
        lax.all_gather(qkv_weight, ("fsdp", "ctx"), axis=0, tiled=True),
        lax.all_gather(out_weight, ("fsdp", "ctx"), axis=0, tiled=True),
        lax.all_gather(up_weight, ("fsdp", "ctx"), axis=0, tiled=True),
        lax.all_gather(down_weight, ("fsdp", "ctx"), axis=0, tiled=True),
        lax.all_gather(norm_gains, ("fsdp", "ctx"), axis=0, tiled=True),
        lax.all_gather(row_biases, ("fsdp", "ctx"), axis=0, tiled=True),
    )
    w_qkv, w_out, w_up, w_down, gains_all, biases_all = gathered
    gains_f = gains_all.astype(jnp.float32)
    biases_f = biases_all.astype(jnp.float32)
    head_width = w_qkv.shape[2]
    head_count = head_width // HD
    flat_tokens = tokens.reshape(row_count, width)
    projected = jnp.dot(
        flat_tokens, w_qkv.reshape(width, 3 * head_width), preferred_element_type=jnp.float32
    )
    projected = projected.reshape(row_count, 3, head_width)
    bias_f = qv_bias.astype(jnp.float32)
    query_low = (projected[:, 0] + bias_f[0]).astype(jnp.bfloat16)
    key_low = projected[:, 1].astype(jnp.bfloat16)
    value_low = (projected[:, 2] + bias_f[1]).astype(jnp.bfloat16)
    keys_full, values_full = (
        lax.all_gather(
            key_low.reshape(seq_count, local_len, head_width), "ctx", axis=1, tiled=True
        ),
        lax.all_gather(
            value_low.reshape(seq_count, local_len, head_width), "ctx", axis=1, tiled=True
        ),
    )
    full_len = keys_full.shape[1]
    block_len = min(512, full_len)
    block_count = full_len // block_len
    query_four = query_low.reshape(seq_count, local_len, head_count, HD)
    stat_shape = (seq_count, head_count, local_len)
    four_shape = (seq_count, local_len, head_count, HD)

    def stats_step(block_idx, running):
        row_max, row_total = running
        scores = block_scores(
            query_four, split_heads(keys_full, block_idx * block_len, block_len, head_count)
        )
        new_max = jnp.maximum(row_max, jnp.max(scores, axis=-1))
        row_total = row_total * jnp.exp(row_max - new_max) + jnp.sum(
            jnp.exp(scores - new_max[..., None]), axis=-1
        )
        return (new_max, row_total)

    row_max, row_total = lax.fori_loop(
        0,
        block_count,
        stats_step,
        (jnp.full(stat_shape, -jnp.inf, jnp.float32), jnp.zeros(stat_shape, jnp.float32)),
    )

    def value_step(block_idx, attn_mixed):
        first_row = block_idx * block_len
        value_four = split_heads(values_full, first_row, block_len, head_count)
        prob_full = softmax_rows(
            block_scores(query_four, split_heads(keys_full, first_row, block_len, head_count)),
            row_max,
            row_total,
        )
        return attn_mixed + jnp.einsum(
            "shqk,skhd->sqhd",
            prob_full.astype(jnp.bfloat16),
            value_four,
            preferred_element_type=jnp.float32,
        )

    zero_four = jnp.zeros(four_shape, jnp.float32)
    attn_mixed = lax.fori_loop(0, block_count, value_step, zero_four)
    mixed_low = attn_mixed.reshape(row_count, head_width).astype(jnp.bfloat16)
    attn_part = contract_last(mixed_low, w_out)
    attn_out = lax.psum(attn_part.astype(jnp.bfloat16), "tp").astype(jnp.float32) + biases_f[:, 0]
    first_out, first_norm, first_scale = norm_forward(
        flat_tokens.astype(jnp.float32) + attn_out, gains_f[:, 0], biases_f[:, 1]
    )
    first_low = first_out.astype(jnp.bfloat16)
    inner_pre = jnp.dot(first_low, w_up, preferred_element_type=jnp.float32) + up_bias.astype(
        jnp.float32
    )
    activated, gelu_back = jax.vjp(gelu_exact, inner_pre)
    act_low = activated.astype(jnp.bfloat16)
    ffn_part = contract_last(act_low, w_down)
    ffn_out = lax.psum(ffn_part.astype(jnp.bfloat16), "tp").astype(jnp.float32) + biases_f[:, 2]
    grad_final = cotangent.reshape(row_count, width).astype(jnp.float32)
    final_out, final_norm, final_scale = norm_forward(
        first_out + ffn_out, gains_f[:, 1], biases_f[:, 3]
    )
    gain2_grad = jnp.sum(grad_final * final_norm, axis=0)
    shift2_grad = jnp.sum(grad_final, axis=0)
    grad_second = norm_backward(grad_final, final_norm, final_scale, gains_f[:, 1])
    ffn_grad_low = grad_second.astype(jnp.bfloat16)
    down_grad = contract_first(ffn_grad_low, act_low)
    down_bias_grad = jnp.sum(ffn_grad_low.astype(jnp.float32), axis=0)
    act_grad = jnp.dot(ffn_grad_low, w_down, preferred_element_type=jnp.float32)
    inner_low = gelu_back(act_grad)[0].astype(jnp.bfloat16)
    up_grad = contract_first(first_low, inner_low)
    up_bias_grad = jnp.sum(inner_low.astype(jnp.float32), axis=0)
    back_part = contract_last(inner_low, w_up)
    first_grad = grad_second + lax.psum(back_part.astype(jnp.bfloat16), "tp").astype(jnp.float32)
    gain1_grad = jnp.sum(first_grad * first_norm, axis=0)
    shift1_grad = jnp.sum(first_grad, axis=0)
    resid_grad = norm_backward(first_grad, first_norm, first_scale, gains_f[:, 0])
    attn_grad_low = resid_grad.astype(jnp.bfloat16)
    out_grad = contract_first(attn_grad_low, mixed_low)
    out_bias_grad = jnp.sum(attn_grad_low.astype(jnp.float32), axis=0)
    mixed_grad_low = jnp.dot(attn_grad_low, w_out, preferred_element_type=jnp.float32).astype(
        jnp.bfloat16
    )
    grad_four = mixed_grad_low.reshape(four_shape)
    row_delta = jnp.einsum(
        "sqhd,sqhd->shq", grad_four.astype(jnp.float32), attn_mixed, precision=highest
    )

    def grad_step(block_idx, running):
        query_grad, key_all, value_all = running
        first_row = block_idx * block_len
        key_four = split_heads(keys_full, first_row, block_len, head_count)
        value_four = split_heads(values_full, first_row, block_len, head_count)
        scores = block_scores(query_four, key_four)
        prob_low, score_low = score_grads(
            scores, row_max, row_total, row_delta, grad_four, value_four
        )
        query_grad = query_grad + jnp.einsum(
            "shqk,skhd->sqhd", score_low, key_four, preferred_element_type=jnp.float32
        )
        key_part = (
            jnp.einsum("shqk,sqhd->skhd", score_low, query_four, preferred_element_type=jnp.float32)
            * score_scale
        )
        value_part = jnp.einsum(
            "shqk,sqhd->skhd", prob_low, grad_four, preferred_element_type=jnp.float32
        )
        key_all = lax.dynamic_update_slice_in_dim(
            key_all, key_part.reshape(seq_count, block_len, head_width), first_row, 1
        )
        value_all = lax.dynamic_update_slice_in_dim(
            value_all, value_part.reshape(seq_count, block_len, head_width), first_row, 1
        )
        return (query_grad, key_all, value_all)

    zeros_full = jnp.zeros((seq_count, full_len, head_width), jnp.float32)
    query_grad, key_all, value_all = lax.fori_loop(
        0, block_count, grad_step, (zero_four, zeros_full, zeros_full)
    )
    key_grad, value_grad = (
        lax.psum_scatter(
            key_all.astype(jnp.bfloat16), "ctx", scatter_dimension=1, tiled=True
        ).astype(jnp.float32),
        lax.psum_scatter(
            value_all.astype(jnp.bfloat16), "ctx", scatter_dimension=1, tiled=True
        ).astype(jnp.float32),
    )
    query_grad_low = (query_grad * score_scale).reshape(row_count, head_width).astype(jnp.bfloat16)
    key_grad_low = key_grad.reshape(row_count, head_width).astype(jnp.bfloat16)
    value_grad_low = value_grad.reshape(row_count, head_width).astype(jnp.bfloat16)
    grad_cat = jnp.stack([query_grad_low, key_grad_low, value_grad_low], axis=1)
    qkv_grad = jnp.einsum("td,tcj->dcj", flat_tokens, grad_cat, preferred_element_type=jnp.float32)
    qv_grad = jnp.stack(
        [
            jnp.sum(query_grad_low.astype(jnp.float32), axis=0),
            jnp.sum(value_grad_low.astype(jnp.float32), axis=0),
        ]
    )
    input_part = contract_last(
        grad_cat.reshape(row_count, 3 * head_width), w_qkv.reshape(width, 3 * head_width)
    )
    gains_grad = jnp.stack([gain1_grad, gain2_grad], axis=1)
    shifts_grad = jnp.stack([shift1_grad, shift2_grad], axis=1)
    tokens_full = resid_grad + lax.psum(input_part.astype(jnp.bfloat16), "tp").astype(jnp.float32)
    tokens_share = own_rows(to_three(tokens_full))
    output_share = own_rows(to_three(final_out))
    biases_grad = jnp.stack(
        [out_bias_grad, shifts_grad[:, 0], down_bias_grad, shifts_grad[:, 1]], axis=1
    )
    shards = (
        lax.psum_scatter(qkv_grad, ("fsdp", "ctx"), scatter_dimension=0, tiled=True),
        lax.psum_scatter(out_grad, ("fsdp", "ctx"), scatter_dimension=0, tiled=True),
        lax.psum_scatter(up_grad, ("fsdp", "ctx"), scatter_dimension=0, tiled=True),
        lax.psum_scatter(down_grad, ("fsdp", "ctx"), scatter_dimension=0, tiled=True),
        lax.psum_scatter(gains_grad, ("fsdp", "ctx"), scatter_dimension=0, tiled=True),
        lax.psum_scatter(biases_grad, ("fsdp", "ctx"), scatter_dimension=0, tiled=True),
    )
    qv_total, up_total = lax.psum((qv_grad, up_bias_grad), ("fsdp", "ctx"))
    output = output_share.astype(jnp.bfloat16)
    tokens_out = tokens_share.astype(jnp.bfloat16)
    return (
        output,
        tokens_out,
        shards[0],
        qv_total,
        shards[1],
        shards[2],
        up_total,
        shards[3],
        shards[4],
        shards[5],
    )


def solution(mesh):
    in_specs = (
        P("fsdp", "ctx", None),
        P(("fsdp", "ctx"), None, "tp"),
        P(None, "tp"),
        P(("fsdp", "ctx"), "tp"),
        P(("fsdp", "ctx"), "tp"),
        P("tp"),
        P(("fsdp", "ctx"), "tp"),
        P(("fsdp", "ctx"), None),
        P(("fsdp", "ctx"), None),
        P("fsdp", "ctx", None),
    )
    out_specs = (
        P("fsdp", ("ctx", "tp"), None),
        P("fsdp", ("ctx", "tp"), None),
        P(("fsdp", "ctx"), None, "tp"),
        P(None, "tp"),
        P(("fsdp", "ctx"), "tp"),
        P(("fsdp", "ctx"), "tp"),
        P("tp"),
        P(("fsdp", "ctx"), "tp"),
        P(("fsdp", "ctx"), None),
        P(("fsdp", "ctx"), None),
    )
    return jax.shard_map(body, mesh=mesh, in_specs=in_specs, out_specs=out_specs, check_vma=False)
```

profile of v0, /device:TPU:0, one launch (start us, length us, event | category | flops | bytes accessed | tf_op | source)
XLA Modules:
  0.0 2091.1 jit_solution(9542823779875088038)
XLA Ops:
  8.0 45.5 %all-gather.8.cloned.1.call-done = bf16[768,3,384]{2,0,1:T(8,128)(2,1)} async-done(((bf16[48,3,384]{2,0,1:T(8,128)(2,1)}), bf16[768,3,384]{2,0,1:T(8,128)(2,1)}) %all-gather.8.cloned.1.call-update) | async-done | bytes 1769488 | tf_op jit(solution)/shard_map/all_gather | solution.py:96
  67.9 53.5 %all_gather.27 = bf16[768,384]{1,0:T(8,128)(2,1)} all-gather(bf16[48,384]{1,0:T(8,128)(2,1)S(1)} %copy-done.33), channel_id=1, replica_groups=mesh['fsdp'=4,'ctx'=4,'tp'=2] {'fsdp','ctx'}, dimensions={0}, use_global_device_ids=true | all-gather | bytes 626688 | tf_op jit(solution)/shard_map/all_gather | solution.py:97
  142.4 48.0 %all-gather.12.cloned.1.call-done = bf16[2,4096,384]{1,2,0:T(8,128)(2,1)} async-done(((bf16[2,1024,384]{1,2,0:T(8,128)(2,1)}), bf16[2,4096,384]{1,2,0:T(8,128)(2,1)}) %all-gather.12.cloned.1.call-update) | async-done | bytes 6291472 | tf_op jit(solution)/shard_map/all_gather | solution.py:118
  190.4 93.1 %while.48 = (s32[]{:T(128)}, f32[2,6,1024]{2,1,0:T(8,128)S(1)}, f32[2,6,1024]{2,1,0:T(8,128)S(1)}, bf16[2,4096,384]{1,2,0:T(8,128)(2,1)}, bf16[2,1024,6,64]{1,3,...) while((s32[]{:T(128)}, f32[2,6,1024]{2,1,0:T(8,128)S(1)}, ...), condition=%wide.region_3.0_spmd.clone, body=%wide.region_0.0_spmd.clone.sunk | while | flops 836825088 | bytes 54902944 | solution.py:143
  283.5 22.7 %all-gather.10.cloned.1.call-done = bf16[2,4096,384]{1,2,0:T(8,128)(2,1)} async-done(((bf16[2,1024,384]{1,2,0:T(8,128)(2,1)}), bf16[2,4096,384]{1,2,0:T(8,128)(2,1)}) %all-gather.10.cloned.1.call-update) | async-done | bytes 6291472 | tf_op jit(solution)/shard_map/all_gather | solution.py:121
  306.2 88.7 %while.49 = (s32[]{:T(128)}, f32[2,1024,6,64]{1,3,2,0:T(8,128)}, bf16[2,4096,384]{1,2,0:T(8,128)(2,1)}, bf16[2,4096,384]{1,2,0:T(8,128)(2,1)}, bf16[2,1024,6,64]...) while((s32[]{:T(128)}, f32[2,1024,6,64]{1,3,2,0:T(8,128)}, ...), condition=%wide.region_5.0_spmd.clone, body=%wide.region_4.0_spmd.clone.sunk | while | flops 1637351424 | bytes 12681393 | solution.py:166
  405.1 29.4 %all-gather.1 = bf16[16,48,2]{1,2,0:T(2,128)(2,1)S(1)} all-gather(bf16[1,48,2]{1,2,0:T(2,128)(2,1)S(1)} %bitcast.191), channel_id=1, replica_groups=mesh['fsdp'=4,'ctx'=4,'tp'=2] {'fsdp','ctx'}, dimensions={0}, use_global_device_ids=true | all-gather | bytes 3264 | tf_op jit(solution)/shard_map/all_gather | solution.py:100
  434.7 29.8 %all-gather = bf16[16,48,4]{1,2,0:T(4,128)(2,1)S(1)} all-gather(bf16[1,48,4]{1,2,0:T(4,128)(2,1)S(1)} %bitcast.190), channel_id=1, replica_groups=mesh['fsdp'=4,'ctx'=4,'tp'=2] {'fsdp','ctx'}, dimensions={0}, use_global_device_ids=true | all-gather | bytes 6528 | tf_op jit(solution)/shard_map/all_gather | solution.py:101
  465.2 22.8 %all-reduce.8.cloned.1.call-done = bf16[2048,768]{1,0:T(8,128)(2,1)} async-done(((bf16[2048,768]{1,0:T(8,128)(2,1)}), bf16[2048,768]{1,0:T(8,128)(2,1)}) %all-reduce.8.cloned.1.call-update) | async-done | bytes 3145744 | tf_op jit(solution)/shard_map/psum | solution.py:169
  496.9 35.6 %all-gather.14.cloned.1.call-done = bf16[768,1536]{1,0:T(8,128)(2,1)} async-done(((bf16[48,1536]{1,0:T(8,128)(2,1)}), bf16[768,1536]{1,0:T(8,128)(2,1)}) %all-gather.14.cloned.1.call-update) | async-done | bytes 2359312 | tf_op jit(solution)/shard_map/all_gather | solution.py:98
  532.5 35.1 %multiply_convert_fusion.1 = (bf16[2048,1536]{1,0:T(8,128)(2,1)}, f32[2048,1536]{1,0:T(8,128)}, f32[2048,1536]{1,0:T(8,128)}) fusion(f32[1536]{0:T(1024)S(1)} %convert_element_type.186, bf16[768,1536]{1,0:T(8,128)(2,1)} %all-gather.14.cloned.1.call-done, f32[2048,768]{1,0:T(8,128)} %subtract_multiply_fusion.2, f32[768]{0:T(1024)S(1)} %get-tuple-element.637, ...), kind=kOutput, calls=%fused_computation.29 | convolution fusion | flops 5044174848 | bytes 40120320 | tf_op jit(solution)/shard_map/dot_general | solution.py:174
  587.0 82.7 %all-reduce.10.cloned.1.call-done = bf16[2048,768]{1,0:T(8,128)(2,1)} async-done(((bf16[2048,768]{1,0:T(8,128)(2,1)}), bf16[2048,768]{1,0:T(8,128)(2,1)}) %all-reduce.10.cloned.1.call-update) | async-done | bytes 3145744 | tf_op jit(solution)/shard_map/psum | solution.py:180
  681.2 18.9 convert_reduce_fusion
  709.2 85.9 %all-reduce.12.cloned.1.call-done = bf16[2048,768]{1,0:T(8,128)(2,1)} async-done(((bf16[2048,768]{1,0:T(8,128)(2,1)}), bf16[2048,768]{1,0:T(8,128)(2,1)}) %all-reduce.12.cloned.1.call-update) | async-done | bytes 3145744 | tf_op jit(solution)/shard_map/psum | solution.py:196
  830.3 482.0 %while.50 = (s32[]{:T(128)}, f32[2,1024,6,64]{1,3,2,0:T(8,128)}, bf16[2,4096,384]{1,2,0:T(8,128)(2,1)}, bf16[2,4096,384]{1,2,0:T(8,128)(2,1)}, bf16[2,4096,384]{...) while((s32[]{:T(128)}, f32[2,1024,6,64]{1,3,2,0:T(8,128)}, ...), condition=%wide.region_18.0_spmd.clone, body=%wide.region_17.0_spmd.clone.sunk | while | flops 4072931328 | bytes 139346160 | solution.py:239
  1327.7 95.6 %reduce-scatter.12.cloned.1.call-done = bf16[2,1024,384]{1,2,0:T(8,128)(2,1)} async-done(((bf16[2,4096,384]{1,2,0:T(8,128)(2,1)}), bf16[2,1024,384]{1,2,0:T(8,128)(2,1)}) %reduce-scatter.12.cloned.1.call-update) | async-done | bytes 1572880 | tf_op jit(solution)/shard_map/reduce_scatter | solution.py:243
  1425.9 110.9 %reduce-scatter.14.cloned.1.call-done = bf16[2,1024,384]{1,2,0:T(8,128)(2,1)} async-done(((bf16[2,4096,384]{1,2,0:T(8,128)(2,1)}), bf16[2,1024,384]{1,2,0:T(8,128)(2,1)}) %reduce-scatter.14.cloned.1.call-update) | async-done | bytes 1572880 | tf_op jit(solution)/shard_map/reduce_scatter | solution.py:246
  1598.1 57.0 %reduce-scatter.24.cloned.1.call-done = f32[48,4]{1,0:T(8,128)} async-done(((f32[768,4]{1,0:T(8,128)}), f32[48,4]{1,0:T(8,128)}) %reduce-scatter.24.cloned.1.call-update) | async-done | bytes 784
  1656.9 61.1 %all-reduce.1 = (f32[2,384]{1,0:T(2,128)}, f32[1536]{0:T(1024)}) all-reduce(f32[2,384]{1,0:T(2,128)S(1)} %pad_maximum_fusion.5, f32[1536]{0:T(1024)S(1)} %copy-done.43), channel_id=1, replica_groups=mesh['fsdp'=4,'ctx'=4,'tp'=2] {'fsdp','ctx'}, use_global_device_ids=true, to_apply=%region_25.0 | all-reduce | flops 2304 | bytes 18432 | tf_op jit(solution)/shard_map/psum | solution.py:280
  1718.0 58.1 %all-reduce.16.cloned.1.call-done = f32[768,3,384]{2,1,0:T(4,128)} async-done(((f32[768,3,384]{2,1,0:T(4,128)}), f32[768,3,384]{2,1,0:T(4,128)}) %all-reduce.16.cloned.1.call-update) | async-done | bytes 3538960
  1777.8 86.1 %all-reduce.14.cloned.1.call-done = bf16[2048,768]{1,0:T(8,128)(2,1)} async-done(((bf16[2048,768]{1,0:T(8,128)(2,1)}), bf16[2048,768]{1,0:T(8,128)(2,1)}) %all-reduce.14.cloned.1.call-update) | async-done | bytes 3145744 | tf_op jit(solution)/shard_map/psum | solution.py:266
  1869.5 56.6 %reduce-scatter.16.cloned.1.call-done = f32[48,384]{1,0:T(8,128)} async-done(((f32[768,384]{1,0:T(8,128)}), f32[48,384]{1,0:T(8,128)}) %reduce-scatter.16.cloned.1.call-update) | async-done | bytes 73744 | tf_op jit(solution)/shard_map/reduce_scatter | solution.py:274
  1926.1 78.9 %reduce-scatter.20.cloned.1.call-done = f32[48,1536]{1,0:T(8,128)} async-done(((f32[768,1536]{1,0:T(8,128)}), f32[48,1536]{1,0:T(8,128)}) %reduce-scatter.20.cloned.1.call-update) | async-done | bytes 294928 | tf_op jit(solution)/shard_map/reduce_scatter | solution.py:276
  2005.0 79.2 %reduce-scatter.18.cloned.1.call-done = f32[48,1536]{1,0:T(8,128)} async-done(((f32[768,1536]{1,0:T(8,128)}), f32[48,1536]{1,0:T(8,128)}) %reduce-scatter.18.cloned.1.call-update) | async-done | bytes 294928 | tf_op jit(solution)/shard_map/reduce_scatter | solution.py:275
  (368 shorter events, 881.1 us)
Async XLA Ops:
  7.2 46.2 %all-gather.8.cloned.1.call-start = ((), (), s32[]{:S(2)}) async-start(), calls=%async_computation.7 | async-start | bytes 1880064 | tf_op jit(solution)/shard_map/all_gather | solution.py:96
  7.9 182.5 %all-gather.12.cloned.1.call-start = ((), (), s32[]{:S(2)}) async-start(), calls=%async_computation.9 | async-start | bytes 7864320 | tf_op jit(solution)/shard_map/all_gather | solution.py:118
  67.7 238.5 %all-gather.10.cloned.1.call-start = ((), (), s32[]{:S(2)}) async-start(), calls=%async_computation.8 | async-start | bytes 7864320 | tf_op jit(solution)/shard_map/all_gather | solution.py:121
  141.9 346.1 %all-reduce.8.cloned.1.call-start = ((), (), s32[]{:S(2)}) async-start(), calls=%async_computation.10 | async-start | bytes 6291456 | tf_op jit(solution)/shard_map/psum | solution.py:169
  400.4 87.7 %copy-start.7 = (bf16[2,1024,768]{2,1,0:T(8,128)(2,1)S(1)}, bf16[2,1024,768]{2,1,0:T(8,128)(2,1)}, u32[]{:S(2)}) copy-start(bf16[2,1024,768]{2,1,0:T(8,128)(2,1)} %param.16) | copy-start | bytes 9437188
  403.9 128.7 %all-gather.14.cloned.1.call-start = ((), (), s32[]{:S(2)}) async-start(), calls=%async_computation.11 | async-start | bytes 2506752 | tf_op jit(solution)/shard_map/all_gather | solution.py:98
  404.4 171.3 %all-gather.16.cloned.1.call-start = ((), (), s32[]{:S(2)}) async-start(), calls=%async_computation.12 | async-start | bytes 2506752 | tf_op jit(solution)/shard_map/all_gather | solution.py:99
  405.0 264.7 %all-reduce.10.cloned.1.call-start = ((), (), s32[]{:S(2)}) async-start(), calls=%async_computation.13 | async-start | bytes 6291456 | tf_op jit(solution)/shard_map/psum | solution.py:180
  434.6 244.3 %copy-start.27 = (f32[768]{0:T(1024)}, f32[768]{0:T(1024)S(1)}, u32[]{:S(2)}) copy-start(f32[768]{0:T(1024)S(1)} %get-tuple-element.639) | copy-start | bytes 9220
  434.7 370.4 %copy-start.31 = (f32[768]{0:T(1024)}, f32[768]{0:T(1024)S(1)}, u32[]{:S(2)}) copy-start(f32[768]{0:T(1024)S(1)} %get-tuple-element.640) | copy-start | bytes 9220
  465.2 204.5 %copy-start.35 = (f32[768]{0:T(1024)}, f32[768]{0:T(1024)S(1)}, u32[]{:S(2)}) copy-start(f32[768]{0:T(1024)S(1)} %get-tuple-element.637) | copy-start | bytes 9220
  585.0 210.2 %all-reduce.12.cloned.1.call-start = ((), (), s32[]{:S(2)}) async-start(), calls=%async_computation.14 | async-start | bytes 6291456 | tf_op jit(solution)/shard_map/psum | solution.py:196
  709.2 714.1 %reduce-scatter.12.cloned.1.call-start = ((), (), s32[]{:S(2)}) async-start(), calls=%async_computation.15 | async-start | bytes 7864320 | tf_op jit(solution)/shard_map/reduce_scatter | solution.py:243
  709.2 95.8 %copy-start.30 = (f32[2048]{0:T(1024)S(1)}, f32[2048]{0:T(1024)}, u32[]{:S(2)}) copy-start(f32[2048]{0:T(1024)} %copy-done.29) | copy-start | bytes 24580
  1312.4 224.4 %reduce-scatter.14.cloned.1.call-start = ((), (), s32[]{:S(2)}) async-start(), calls=%async_computation.16 | async-start | bytes 7864320 | tf_op jit(solution)/shard_map/reduce_scatter | solution.py:246
  1312.9 283.8 %reduce-scatter.22.cloned.1.call-start = ((), (), s32[]{:S(2)}) async-start(), calls=%async_computation.21 | async-start | bytes 417792
  1315.7 339.5 %reduce-scatter.24.cloned.1.call-start = ((), (), s32[]{:S(2)}) async-start(), calls=%async_computation.22 | async-start | bytes 417792
  1321.1 218.3 %copy-start.8 = (bf16[2,1024,768]{2,1,0:T(8,128)(2,1)S(1)}, bf16[2,1024,768]{2,1,0:T(8,128)(2,1)}, u32[]{:S(2)}) copy-start(bf16[2,1024,768]{2,1,0:T(8,128)(2,1)} %param.16) | copy-start | bytes 9437188
  1327.7 448.4 %all-reduce.16.cloned.1.call-start = ((), (), s32[]{:S(2)}) async-start(), calls=%async_computation.23 | async-start | bytes 9437184
  1553.9 310.0 %all-reduce.14.cloned.1.call-start = ((), (), s32[]{:S(2)}) async-start(), calls=%async_computation.17 | async-start | bytes 6291456 | tf_op jit(solution)/shard_map/psum | solution.py:266
  1562.6 363.5 %reduce-scatter.16.cloned.1.call-start = ((), (), s32[]{:S(2)}) async-start(), calls=%async_computation.18 | async-start | bytes 1253376 | tf_op jit(solution)/shard_map/reduce_scatter | solution.py:274
  1568.6 436.4 %reduce-scatter.20.cloned.1.call-start = ((), (), s32[]{:S(2)}) async-start(), calls=%async_computation.20 | async-start | bytes 5013504 | tf_op jit(solution)/shard_map/reduce_scatter | solution.py:276
  1579.1 505.0 %reduce-scatter.18.cloned.1.call-start = ((), (), s32[]{:S(2)}) async-start(), calls=%async_computation.19 | async-start | bytes 5013504 | tf_op jit(solution)/shard_map/reduce_scatter | solution.py:275
  1591.1 65.8 %copy-start.43 = (f32[1536]{0:T(1024)S(1)}, f32[1536]{0:T(1024)}, u32[]{:S(2)}) copy-start(f32[1536]{0:T(1024)} %get-tuple-element.708) | copy-start | bytes 18436
  (49 other events, 407.1 us)
Sparse Core Ops, SparseCore 0:
  10.2 43.1 all-gather.7
  67.8 122.5 all-gather.11
  192.5 113.6 all-gather.9
  404.0 83.9 all-reduce.7
  490.2 42.3 all-gather.13
  534.7 41.0 all-gather.15
  585.1 84.5 all-reduce.9
  709.3 85.8 all-reduce.11
  1312.5 110.7 reduce-scatter.11
  1425.4 111.2 reduce-scatter.13
  1540.3 56.4 reduce-scatter.21
  1600.1 55.0 reduce-scatter.23
  1658.8 117.2 all-reduce.15
  1778.2 85.5 all-reduce.13
  1867.9 58.1 reduce-scatter.15
  1930.4 74.5 reduce-scatter.19
  2009.3 74.8 reduce-scatter.17
where the time goes:
time: 2100 us; the launch traced here: 2090 us
  waiting for transfers between devices  977 us (47%)
  matrix products  697 us (33%)
  blocking collectives  174 us (8%)
  local copies, waits for them, and re-layouts  134 us (6%)
  other arithmetic  92 us (4%)
    dot_general x16, matrix products, block_scores(): jnp.einsum('sqhd,skhd->shqk', query_four, key_four, preferred_element_typ...  141 us
    unnamed x20, waiting for transfers between devices  118 us
    dot_general x8, matrix products, score_grads(): jnp.einsum('sqhd,skhd->shqk', grad_four, value_four, preferred_element_ty...  116 us
    reduce_scatter x1, waiting for transfers between devices, body(): lax.psum_scatter(value_all.astype(jnp.bfloat16), 'ctx', scatter_dimension...  111 us
    reduce_scatter x1, waiting for transfers between devices, body(): lax.psum_scatter(key_all.astype(jnp.bfloat16), 'ctx', scatter_dimension=1...  95.6 us
    dot_general x8, matrix products, grad_step(): jnp.einsum('shqk,sqhd->skhd', prob_low, grad_four, preferred_element_type...  89.2 us
    psum x1, waiting for transfers between devices, body(): lax.psum(input_part.astype(jnp.bfloat16), 'tp').astype(jnp.float32)  86.1 us
    psum x1, waiting for transfers between devices, body(): lax.psum(back_part.astype(jnp.bfloat16), 'tp').astype(jnp.float32)  85.9 us
  transfers between devices with their start and end apart: 17, of which 17 were waited for; matrix products, arithmetic and copies ran while one was open for 12% of the time, Pallas kernels for 0%

commit v1 on v0

v1 whole, which is shorter than its diff:
```python
import jax
import jax.numpy as jnp
from jax import lax
from jax.experimental import pallas as pl
from jax.experimental.pallas import tpu as pltpu
from jax.sharding import PartitionSpec as P

HD = 64
B = jnp.bfloat16
F = jnp.float32
epsilon = 1e-12
score_scale = 0.125
LOG2E = 1.4426950408889634
WEIGHT_AXES = ("tp", "fsdp", "ctx")


def dot(left, right, left_dim, right_dim):
    return lax.dot_general(
        left, right, (((left_dim,), (right_dim,)), ((), ())), preferred_element_type=F
    )


def split_low(value, count):
    parts = []
    for _ in range(count):
        part = value.astype(B)
        parts.append(part)
        value = value - part.astype(F)
    return parts


def pick_block(size, wanted):
    while size % wanted:
        wanted //= 2
    return wanted


def forward_kernel(q_ref, kv_ref, o_ref, lse_ref, qx, kx, vx, *, bk):
    rows = q_ref.shape[-1]
    keys = kv_ref.shape[-1]
    scaled = q_ref[0].astype(F) * (score_scale * LOG2E)
    high, rest = split_low(scaled, 2)
    qx[0:HD, :] = high
    qx[HD : 2 * HD, :] = rest
    kx[0:HD, :] = kv_ref[0, 0]
    kx[HD : 2 * HD, :] = kv_ref[0, 0]
    vx[0:HD, :] = kv_ref[0, 1]
    vx[HD : HD + 16, :] = jnp.ones((16, keys), B)

    def step(i, carry):
        row_max, mixed = carry
        off = pl.multiple_of(i * bk, bk)
        scores = dot(kx[:, pl.ds(off, bk)], qx[...], 0, 0)
        new_max = jnp.maximum(row_max, jnp.max(scores, axis=0, keepdims=True))
        probs = jnp.exp2(scores - new_max).astype(B)
        mixed = mixed * jnp.exp2(row_max - new_max) + dot(vx[:, pl.ds(off, bk)], probs, 1, 0)
        return new_max, mixed

    start = (jnp.full((1, rows), -jnp.inf, F), jnp.zeros((HD + 16, rows), F))
    row_max, mixed = lax.fori_loop(0, keys // bk, step, start)
    total = mixed[HD : HD + 1, :]
    o_ref[0] = mixed[0:HD, :] / total
    lse_ref[0, 0] = row_max + jnp.log2(total)


def attention_forward(q_t, kv_t, bk):
    parts, width, rows = q_t.shape
    keys = kv_t.shape[3]
    heads = width // HD
    bk = pick_block(keys, bk)
    return pl.pallas_call(
        lambda *refs: forward_kernel(*refs, bk=bk),
        grid=(parts, heads),
        in_specs=[
            pl.BlockSpec((1, HD, rows), lambda t, h: (t, h, 0)),
            pl.BlockSpec((1, 2, HD, keys), lambda t, h: (t, 0, h, 0)),
        ],
        out_specs=[
            pl.BlockSpec((1, HD, rows), lambda t, h: (t, h, 0)),
            pl.BlockSpec((1, 1, 1, rows), lambda t, h: (t, h, 0, 0)),
        ],
        out_shape=[
            jax.ShapeDtypeStruct((parts, width, rows), F),
            jax.ShapeDtypeStruct((parts, heads, 1, rows), F),
        ],
        scratch_shapes=[
            pltpu.VMEM((2 * HD, rows), B),
            pltpu.VMEM((2 * HD, keys), B),
            pltpu.VMEM((HD + 16, keys), B),
        ],
        compiler_params=pltpu.CompilerParams(
            vmem_limit_bytes=56 << 20, dimension_semantics=("arbitrary", "arbitrary")
        ),
        name="attn_forward",
    )(q_t, kv_t)


def backward_kernel(
    q_ref, kv_ref, do_ref, lse_ref, delta_ref, dq_ref, dkv_ref, qx, kx, dx, vx, dq_acc, *, bk, bq
):
    rows = q_ref.shape[-1]
    keys = kv_ref.shape[-1]
    scaled = q_ref[0].astype(F) * (score_scale * LOG2E)
    high, rest = split_low(scaled, 2)
    sub = lax.broadcasted_iota(jnp.int32, (16, rows), 0)

    def stacked(value):
        block = jnp.zeros((16, rows), F)
        for j, part in enumerate(split_low(value, 3)):
            block = jnp.where(sub == j, jnp.broadcast_to(part.astype(F), (16, rows)), block)
        return block.astype(B)

    qx[0:HD, :] = high
    qx[HD : 2 * HD, :] = rest
    qx[2 * HD : 2 * HD + 16, :] = stacked(lse_ref[0, 0])
    dx[0:HD, :] = do_ref[0]
    dx[HD : HD + 16, :] = stacked(delta_ref[0, 0])
    kx[0:HD, :] = kv_ref[0, 0]
    kx[HD : 2 * HD, :] = kv_ref[0, 0]
    kx[2 * HD : 2 * HD + 16, :] = jnp.full((16, keys), -1.0, B)
    vx[0:HD, :] = kv_ref[0, 1]
    vx[HD : HD + 16, :] = jnp.full((16, keys), -1.0, B)
    dq_acc[...] = jnp.zeros_like(dq_acc)

    def step(i, carry):
        off = pl.multiple_of(i * bk, bk)
        k_part = kx[:, pl.ds(off, bk)]
        v_part = vx[:, pl.ds(off, bk)]
        dk_part = jnp.zeros((HD, bk), F)
        dv_part = jnp.zeros((HD, bk), F)
        for j in range(0, rows, bq):
            probs = jnp.exp2(dot(qx[:, j : j + bq], k_part, 0, 0))
            prob_grad = dot(dx[:, j : j + bq], v_part, 0, 0)
            score_low = (probs * prob_grad).astype(B)
            prob_low = probs.astype(B)
            dv_part = dv_part + dot(dx[0:HD, j : j + bq], prob_low, 1, 0)
            dk_part = dk_part + dot(q_ref[0, :, j : j + bq], score_low, 1, 0)
            dq_acc[j : j + bq, :] += dot(score_low, k_part[0:HD, :], 1, 1)
        dkv_ref[0, 0, :, pl.ds(off, bk)] = (dk_part * score_scale).astype(B)
        dkv_ref[0, 1, :, pl.ds(off, bk)] = dv_part.astype(B)
        return carry

    lax.fori_loop(0, keys // bk, step, 0)
    dq_ref[0] = jnp.transpose(dq_acc[...] * score_scale).astype(dq_ref.dtype)


def attention_backward(q_t, kv_t, do_t, lse, delta, bk, bq, dq_type):
    parts, width, rows = q_t.shape
    keys = kv_t.shape[3]
    heads = width // HD
    bk = pick_block(keys, bk)
    bq = pick_block(rows, bq)
    row_spec = pl.BlockSpec((1, HD, rows), lambda t, h: (t, h, 0))
    stat_spec = pl.BlockSpec((1, 1, 1, rows), lambda t, h: (t, h, 0, 0))
    key_spec = pl.BlockSpec((1, 2, HD, keys), lambda t, h: (t, 0, h, 0))
    return pl.pallas_call(
        lambda *refs: backward_kernel(*refs, bk=bk, bq=bq),
        grid=(parts, heads),
        in_specs=[row_spec, key_spec, row_spec, stat_spec, stat_spec],
        out_specs=[row_spec, key_spec],
        out_shape=[
            jax.ShapeDtypeStruct((parts, width, rows), dq_type),
            jax.ShapeDtypeStruct((parts, 2, width, keys), B),
        ],
        scratch_shapes=[
            pltpu.VMEM((2 * HD + 16, rows), B),
            pltpu.VMEM((2 * HD + 16, keys), B),
            pltpu.VMEM((HD + 16, rows), B),
            pltpu.VMEM((HD + 16, keys), B),
            pltpu.VMEM((rows, HD), F),
        ],
        compiler_params=pltpu.CompilerParams(
            vmem_limit_bytes=56 << 20, dimension_semantics=("arbitrary", "arbitrary")
        ),
        name="attn_backward",
    )(q_t, kv_t, do_t, lse, delta)


def ring_gather(block):
    count = lax.axis_size("ctx")
    up = [(i, (i + 1) % count) for i in range(count)]
    down = [((i + 1) % count, i) for i in range(count)]
    half = block.shape[0] // 2
    first, second = block[:half], block[half:]
    pieces = []
    for _ in range(count - 1):
        first = lax.ppermute(first, "ctx", up)
        second = lax.ppermute(second, "ctx", down)
        pieces.append((first, second))
    return pieces


def ring_reduce(pieces):
    count = lax.axis_size("ctx")
    up = [(i, (i + 1) % count) for i in range(count)]
    down = [((i + 1) % count, i) for i in range(count)]
    first = second = None
    for one, two in reversed(pieces):
        if first is not None:
            one = one + first.astype(F)
            two = two + second.astype(F)
        first = lax.ppermute(one.astype(B), "ctx", down)
        second = lax.ppermute(two.astype(B), "ctx", up)
    return jnp.concatenate([first, second], axis=0).astype(F)


def sum_all(vector):
    for axis in ("fsdp", "tp", "ctx"):
        size = lax.axis_size(axis)
        bit = 1
        while bit < size:
            vector = vector + lax.ppermute(vector, axis, [(i, i ^ bit) for i in range(size)])
            bit *= 2
    return vector


def tp_gather(vector):
    size = lax.axis_size("tp")
    own = lax.axis_index("tp")
    out = jnp.zeros((size,) + vector.shape, vector.dtype)
    out = lax.dynamic_update_index_in_dim(out, vector, own, 0)
    for shift in range(1, size):
        got = lax.ppermute(vector, "tp", [(i, (i + shift) % size) for i in range(size)])
        out = lax.dynamic_update_index_in_dim(out, got, (own - shift) % size, 0)
    return out


def tp_exchange(rows):
    size = lax.axis_size("tp")
    own = lax.axis_index("tp")
    seqs, length, width = rows.shape
    split = rows.reshape(seqs, size, length // size, width)
    out = jnp.zeros((size, seqs, length // size, width), rows.dtype)
    kept = lax.dynamic_index_in_dim(split, own, 1, keepdims=False)
    out = lax.dynamic_update_index_in_dim(out, kept, own, 0)
    for shift in range(1, size):
        sent = lax.dynamic_index_in_dim(split, (own + shift) % size, 1, keepdims=False)
        got = lax.ppermute(sent, "tp", [(i, (i + shift) % size) for i in range(size)])
        out = lax.dynamic_update_index_in_dim(out, got, (own - shift) % size, 0)
    return out.reshape(size * seqs, length // size, width)


def norm_forward(hidden, gain, shift):
    center = hidden - jnp.mean(hidden, axis=-1, keepdims=True)
    inv_scale = lax.rsqrt(jnp.mean(center * center, axis=-1, keepdims=True) + epsilon)
    normed = center * inv_scale
    return (normed * gain + shift, normed, inv_scale)


def norm_backward(grad_out, normed, inv_scale, gain):
    grad_norm = grad_out * gain
    return inv_scale * (
        grad_norm
        - jnp.mean(grad_norm, axis=-1, keepdims=True)
        - normed * jnp.mean(grad_norm * normed, axis=-1, keepdims=True)
    )


def gelu_exact(values):
    return jax.nn.gelu(values, approximate=False)


def body(
    tokens,
    qkv_weight,
    qv_bias,
    out_weight,
    up_weight,
    up_bias,
    down_weight,
    norm_gains,
    row_biases,
    cotangent,
):
    seq_count, local_len, width = tokens.shape
    tp_count = lax.axis_size("tp")
    own_seqs = seq_count // tp_count
    first_seq = lax.axis_index("tp") * own_seqs
    own_tokens = lax.dynamic_slice_in_dim(tokens, first_seq, own_seqs, 0)
    own_cotangent = lax.dynamic_slice_in_dim(cotangent, first_seq, own_seqs, 0)
    rows = own_seqs * local_len
    x_own = own_tokens.reshape(rows, width)
    shard_rows = qkv_weight.shape[0]
    head_width = qkv_weight.shape[2]
    ff_width = up_weight.shape[1]
    pad = 128 - norm_gains.shape[1] - row_biases.shape[1]

    first_shard = jnp.concatenate(
        [
            qkv_weight.reshape(shard_rows, 3 * head_width),
            norm_gains,
            row_biases,
            jnp.zeros((shard_rows, pad), B),
        ],
        axis=1,
    )
    first_all = lax.all_gather(first_shard, WEIGHT_AXES, axis=0, tiled=True)
    first_all = first_all.reshape(tp_count, width, first_shard.shape[1])
    x_pieces = [ring_gather(own_tokens[s]) for s in range(own_seqs)]
    second_shard = jnp.concatenate([out_weight, up_weight, down_weight], axis=1)
    second_all = lax.all_gather(second_shard, WEIGHT_AXES, axis=0, tiled=True)
    second_all = second_all.reshape(tp_count, width, second_shard.shape[1])
    w_q = first_all[:, :, :head_width]
    w_kv = first_all[:, :, head_width : 3 * head_width]
    rows_all = jnp.transpose(first_all[0, :, 3 * head_width :]).astype(F)
    gain1, gain2 = rows_all[0], rows_all[1]
    out_bias, shift1, down_bias, shift2 = (rows_all[2 + i] for i in range(4))
    w_out = second_all[:, :, :head_width]
    w_up = second_all[:, :, head_width : head_width + ff_width]
    w_down = second_all[:, :, head_width + ff_width :]
    bias_all = tp_gather(jnp.concatenate([qv_bias.reshape(-1), up_bias]))
    q_bias = bias_all[:, :head_width].astype(F)
    v_bias = bias_all[:, head_width : 2 * head_width].astype(F)
    u_bias = bias_all[:, 2 * head_width :].astype(F)
    kv_bias = jnp.concatenate([jnp.zeros_like(v_bias), v_bias], axis=1)

    x_full = [
        jnp.concatenate([own_tokens[s]] + [p for pair in x_pieces[s] for p in pair], axis=0)
        for s in range(own_seqs)
    ]
    q_t = [
        (dot(w_q, own_tokens[s], 1, 1) + q_bias[:, :, None]).astype(B) for s in range(own_seqs)
    ]
    kv_t = [
        (dot(w_kv, x_full[s], 1, 1) + kv_bias[:, :, None])
        .astype(B)
        .reshape(tp_count, 2, head_width, x_full[s].shape[0])
        for s in range(own_seqs)
    ]
    attended = [attention_forward(q_t[s], kv_t[s], 2048) for s in range(own_seqs)]
    om_t = [one[0] for one in attended]
    lse = [one[1] for one in attended]
    mixed_t = jnp.concatenate([one.astype(B) for one in om_t], axis=2)
    attn_part = sum(dot(mixed_t[t], w_out[t], 0, 1) for t in range(tp_count))
    x_float = x_own.astype(F)
    first_out, first_norm, first_scale = norm_forward(
        x_float + attn_part + out_bias, gain1, shift1
    )
    first_low = first_out.astype(B)

    act_low, gelu_back = [], []
    for t in range(tp_count):
        inner = dot(first_low, w_up[t], 1, 0) + u_bias[t]
        activated, back = jax.vjp(gelu_exact, inner)
        act_low.append(activated.astype(B))
        gelu_back.append(back)
    ffn_out = sum(dot(act_low[t], w_down[t], 1, 1) for t in range(tp_count)) + down_bias
    grad_final = own_cotangent.reshape(rows, width).astype(F)
    final_out, final_norm, final_scale = norm_forward(first_out + ffn_out, gain2, shift2)
    output = tp_exchange(final_out.astype(B).reshape(own_seqs, local_len, width))
    gain2_grad = jnp.sum(grad_final * final_norm, axis=0)
    shift2_grad = jnp.sum(grad_final, axis=0)
    grad_second = norm_backward(grad_final, final_norm, final_scale, gain2)
    df = grad_second.astype(B)
    down_bias_grad = jnp.sum(df.astype(F), axis=0)
    inner_low = [
        gelu_back[t](dot(df, w_down[t], 1, 0))[0].astype(B) for t in range(tp_count)
    ]
    up_bias_grad = [jnp.sum(inner_low[t].astype(F), axis=0) for t in range(tp_count)]
    first_grad = grad_second + sum(dot(inner_low[t], w_up[t], 1, 1) for t in range(tp_count))
    gain1_grad = jnp.sum(first_grad * first_norm, axis=0)
    shift1_grad = jnp.sum(first_grad, axis=0)
    resid_grad = norm_backward(first_grad, first_norm, first_scale, gain1)
    da = resid_grad.astype(B)
    out_bias_grad = jnp.sum(da.astype(F), axis=0)
    second_grad = jnp.stack(
        [
            jnp.concatenate(
                [
                    dot(da, mixed_t[t], 0, 1).astype(B),
                    dot(first_low, inner_low[t], 0, 0).astype(B),
                    dot(df, act_low[t], 0, 0).astype(B),
                ],
                axis=1,
            )
            for t in range(tp_count)
        ]
    )
    second_grad = lax.psum_scatter(
        second_grad.reshape(tp_count * width, second_shard.shape[1]),
        WEIGHT_AXES,
        scatter_dimension=0,
        tiled=True,
    ).astype(F)

    do_t = dot(w_out, da, 1, 1).astype(B)
    v_bias_grad = jnp.sum(do_t.astype(F), axis=2)
    early = sum_all(
        jnp.concatenate(
            [gain1_grad, gain2_grad, out_bias_grad, shift1_grad, down_bias_grad, shift2_grad]
            + up_bias_grad
            + [v_bias_grad.reshape(-1)]
        )
    )
    dq_t, dkv_t = [], []
    for s in range(own_seqs):
        do_s = do_t[:, :, s * local_len : (s + 1) * local_len]
        delta = (om_t[s] * do_s.astype(F)).reshape(tp_count, head_width // HD, HD, local_len)
        delta = jnp.sum(delta, axis=2, keepdims=True)
        one_dq, one_dkv = attention_backward(q_t[s], kv_t[s], do_s, lse[s], delta, 1024, 512, B)
        dq_t.append(one_dq)
        dkv_t.append(one_dkv.reshape(tp_count, 2 * head_width, one_dkv.shape[3]))
    q_bias_grad = sum_all(sum(jnp.sum(one.astype(F), axis=2) for one in dq_t).reshape(-1))

    own_grads = []
    half = local_len // 2
    for s in range(own_seqs):
        full = sum(dot(dkv_t[s][t], w_kv[t], 0, 1) for t in range(tp_count))
        pieces = []
        for i in range(len(x_pieces[s])):
            at = local_len + i * local_len
            pieces.append((full[at : at + half], full[at + half : at + local_len]))
        own = full[:local_len] + sum(dot(dq_t[s][t], w_q[t], 0, 1) for t in range(tp_count))
        own_grads.append(own + ring_reduce(pieces))
    tokens_grad = resid_grad.reshape(own_seqs, local_len, width) + jnp.stack(own_grads)
    tokens_out = tp_exchange(tokens_grad.astype(B))
    qkv_grad = jnp.stack(
        [
            jnp.concatenate(
                [
                    sum(dot(own_tokens[s], dq_t[s][t], 0, 1) for s in range(own_seqs)).astype(B),
                    sum(dot(x_full[s], dkv_t[s][t], 0, 1) for s in range(own_seqs)).astype(B),
                ],
                axis=1,
            )
            for t in range(tp_count)
        ]
    )
    qkv_grad = lax.psum_scatter(
        qkv_grad.reshape(tp_count * width, 3 * head_width),
        WEIGHT_AXES,
        scatter_dimension=0,
        tiled=True,
    ).astype(F)

    member = lax.axis_index("fsdp") * lax.axis_size("ctx") + lax.axis_index("ctx")
    own_tp = lax.axis_index("tp")
    six = lax.dynamic_slice_in_dim(
        early[: 6 * width].reshape(6, width), member * shard_rows, shard_rows, 1
    )
    six = jnp.transpose(six)
    up_total = lax.dynamic_slice_in_dim(early, 6 * width + own_tp * ff_width, ff_width, 0)
    v_total = lax.dynamic_slice_in_dim(
        early, 6 * width + tp_count * ff_width + own_tp * head_width, head_width, 0
    )
    q_total = lax.dynamic_slice_in_dim(q_bias_grad, own_tp * head_width, head_width, 0)
    return (
        output,
        tokens_out,
        qkv_grad.reshape(shard_rows, 3, head_width),
        jnp.stack([q_total, v_total]),
        second_grad[:, :head_width],
        second_grad[:, head_width : head_width + ff_width],
        up_total,
        second_grad[:, head_width + ff_width :],
        six[:, :2],
        six[:, 2:],
    )


def solution(mesh):
    in_specs = (
        P("fsdp", "ctx", None),
        P(("fsdp", "ctx"), None, "tp"),
        P(None, "tp"),
        P(("fsdp", "ctx"), "tp"),
        P(("fsdp", "ctx"), "tp"),
        P("tp"),
        P(("fsdp", "ctx"), "tp"),
        P(("fsdp", "ctx"), None),
        P(("fsdp", "ctx"), None),
        P("fsdp", "ctx", None),
    )
    out_specs = (
        P("fsdp", ("ctx", "tp"), None),
        P("fsdp", ("ctx", "tp"), None),
        P(("fsdp", "ctx"), None, "tp"),
        P(None, "tp"),
        P(("fsdp", "ctx"), "tp"),
        P(("fsdp", "ctx"), "tp"),
        P("tp"),
        P(("fsdp", "ctx"), "tp"),
        P(("fsdp", "ctx"), None),
        P(("fsdp", "ctx"), None),
    )
    return jax.shard_map(body, mesh=mesh, in_specs=in_specs, out_specs=out_specs, check_vma=False)
```

time: 2100 us -> 787 us (0.37)
  waiting for transfers between devices: 977 us -> 239 us
  matrix products: 697 us -> 159 us
  Pallas kernels: 0 us -> 200 us
  blocking collectives: 174 us -> 0 us
  starting transfers between devices: 1.62 us -> 85.7 us
  local copies, waits for them, and re-layouts: 134 us -> 54.8 us
  other arithmetic: 92 us -> 27.2 us
    dot_general x68 -> x27, matrix products: 697 us -> 159 us  [dot(): lax.dot_general(left, right, (((left_dim,), (right_dim,)), ((), ())), pre...]
    reduce_scatter x5 -> x2, waiting for transfers between devices: 421 us -> 41.8 us  [the longest x1 41.8 us: body(): lax.psum_scatter(second_grad.reshape(tp_count * width, second_shard.shape...]
    psum x4 -> x0, waiting for transfers between devices: 277 us -> none  [the longest x1 86.1 us: body(): lax.psum(input_part.astype(jnp.bfloat16), 'tp').astype(jnp.float32)]
    pallas_call x0 -> x2, Pallas kernels: none -> 200 us  [the longest x1 131 us: attention_backward(): pl.pallas_call(lambda *refs: backward_kernel(*refs, bk=bk, bq=bq), grid=(...]
    ppermute x0 -> x25, waiting for transfers between devices: none -> 197 us  [the longest x3 66.6 us: ring_reduce(): first = lax.ppermute(one.astype(B), 'ctx', down)]
    all_gather x5 -> x2, waiting for transfers between devices: 160 us -> 0.02 us  [the longest x1 0.02 us: body(): second_all = lax.all_gather(second_shard, WEIGHT_AXES, axis=0, tiled=True)]
    unnamed x20 -> x4, waiting for transfers between devices: 118 us -> 0.07 us
    all_gather x3 -> x0, blocking collectives: 113 us -> none  [the longest x1 53.5 us: body(): lax.all_gather(out_weight, ('fsdp', 'ctx'), axis=0, tiled=True)]
  transfers between devices with their start and end apart: 17 -> 29, of which waited for: 17 -> 19; matrix products, arithmetic and copies ran while one was open for 12% -> 14% of each run, Pallas kernels for 0% -> 9%
where the time goes in v1:
time: 787 us; the launch traced here: 782 us
  waiting for transfers between devices  239 us (30%)
  Pallas kernels  200 us (25%)
  matrix products  159 us (20%)
  starting transfers between devices  85.7 us (11%)
  local copies, waits for them, and re-layouts  54.8 us (7%)
  other arithmetic  27.2 us (3%)
  between operations  14.9 us (2%)
    dot_general x27, matrix products, dot(): lax.dot_general(left, right, (((left_dim,), (right_dim,)), ((), ())), pre...  159 us
    pallas_call x1, Pallas kernels, attention_backward(): pl.pallas_call(lambda *refs: backward_kernel(*refs, bk=bk, bq=bq), grid=(...  131 us
    pallas_call x1, Pallas kernels, attention_forward(): pl.pallas_call(lambda *refs: forward_kernel(*refs, bk=bk), grid=(parts, h...  69.8 us
    ppermute x3, waiting for transfers between devices, ring_reduce(): first = lax.ppermute(one.astype(B), 'ctx', down)  66.6 us
    ppermute x3, waiting for transfers between devices, ring_gather(): first = lax.ppermute(first, 'ctx', up)  53.1 us
    reduce_scatter x1, waiting for transfers between devices, body(): lax.psum_scatter(second_grad.reshape(tp_count * width, second_shard.shape...  41.8 us
    ppermute x10, starting transfers between devices, sum_all(): lax.ppermute(vector, axis, [(i, i ^ bit) for i in range(size)])  38 us
    ppermute x3, starting transfers between devices, ring_gather(): first = lax.ppermute(first, 'ctx', up)  32.2 us
  transfers between devices with their start and end apart: 29, of which 19 were waited for; matrix products, arithmetic and copies ran while one was open for 14% of the time, Pallas kernels for 9%

profile of v1, /device:TPU:0, one launch (start us, length us, event | category | flops | bytes accessed | tf_op | source)
XLA Modules:
  0.0 781.6 jit_solution(15609122622170484977)
XLA Ops:
  19.9 21.2 %collective-permute-done.1 = bf16[512,768]{1,0:T(8,128)(2,1)} collective-permute-done((bf16[512,768]{1,0:T(8,128)(2,1)S(1)}, bf16[512,768]{1,0:T(8,128)(2,1)}, u32[]{:S(2)}, u32[]{:S(2)}) %collective-permute-start.1) | collective-permute-done | bytes 786464 | tf_op jit(solution)/shard_map/ppermute | solution.py:187
  41.1 10.3 %collective-permute-start.3 = (bf16[512,768]{1,0:T(8,128)(2,1)}, bf16[512,768]{1,0:T(8,128)(2,1)}, u32[]{:S(2)}, u32[]{:S(2)}) collective-permute-start(bf16[512,768]{1,0:T(8,128)(2,1)} %collective-permute-done.1), channel_id=1, source_target_pairs={{0,2},{2,4},{4,6},{6,0},{1,3},{3,5},{5,7},{7,1},{8,10},{10,12},{12... | collective-permute-start | bytes 2359304 | tf_op jit(solution)/shard_map/ppermute | solution.py:187
  53.7 11.1 %collective-permute-done.2 = bf16[512,768]{1,0:T(8,128)(2,1)} collective-permute-done((bf16[512,768]{1,0:T(8,128)(2,1)}, bf16[512,768]{1,0:T(8,128)(2,1)}, u32[]{:S(2)}, u32[]{:S(2)}) %collective-permute-start.2) | collective-permute-done | bytes 786464 | tf_op jit(solution)/shard_map/ppermute | solution.py:188
  66.5 19.6 %collective-permute-done.3 = bf16[512,768]{1,0:T(8,128)(2,1)} collective-permute-done((bf16[512,768]{1,0:T(8,128)(2,1)}, bf16[512,768]{1,0:T(8,128)(2,1)}, u32[]{:S(2)}, u32[]{:S(2)}) %collective-permute-start.3) | collective-permute-done | bytes 786464 | tf_op jit(solution)/shard_map/ppermute | solution.py:187
  86.0 18.8 %collective-permute-start.5 = (bf16[512,768]{1,0:T(8,128)(2,1)}, bf16[512,768]{1,0:T(8,128)(2,1)S(1)}, u32[]{:S(2)}, u32[]{:S(2)}) collective-permute-start(bf16[512,768]{1,0:T(8,128)(2,1)} %collective-permute-done.3), channel_id=1, source_target_pairs={{0,2},{2,4},{4,6},{6,0},{1,3},{3,5},{5,7},{7,1},{8,10},{10,12},{12... | collective-permute-start | bytes 2359304 | tf_op jit(solution)/shard_map/ppermute | solution.py:187
  117.6 12.4 %collective-permute-done.5 = bf16[512,768]{1,0:T(8,128)(2,1)S(1)} collective-permute-done((bf16[512,768]{1,0:T(8,128)(2,1)}, bf16[512,768]{1,0:T(8,128)(2,1)S(1)}, u32[]{:S(2)}, u32[]{:S(2)}) %collective-permute-start.5) | collective-permute-done | bytes 786464 | tf_op jit(solution)/shard_map/ppermute | solution.py:187
  131.0 16.4 %collective-permute-done.6 = bf16[512,768]{1,0:T(8,128)(2,1)S(1)} collective-permute-done((bf16[512,768]{1,0:T(8,128)(2,1)}, bf16[512,768]{1,0:T(8,128)(2,1)S(1)}, u32[]{:S(2)}, u32[]{:S(2)}) %collective-permute-start.6) | collective-permute-done | bytes 786464 | tf_op jit(solution)/shard_map/ppermute | solution.py:188
  152.4 16.5 %add_convert_fusion = bf16[2,768,4096]{2,1,0:T(8,128)(2,1)} fusion(f32[2,768]{1,0:T(2,128)S(1)} %pad_convert_fusion, bf16[4096,768]{1,0:T(8,128)(2,1)} %constant_dynamic-update-slice_fusion, bf16[2,768,1280]{2,1,0:T(8,128)(2,1)S(1)} %bitcast.217), kind=kOutput, calls=%fused_computation | convolution fusion | flops 9676259328 | bytes 21239808 | tf_op jit(solution)/shard_map/dot_general | solution.py:18
  168.9 69.8 %attn_forward.1 = (f32[2,384,1024]{2,1,0:T(8,128)}, f32[2,6,1,1024]{3,2,1,0:T(1,128)}) custom-call(bf16[2,384,1024]{2,1,0:T(8,128)(2,1)} %add_convert_fusion.4.refs_0_, bf16[2,2,384,4096]{3,2,1,0:T(8,128)(2,1)} %bitcast.199), custom_call_target="tpu_custom_call" | custom-call | tf_op jit(solution)/shard_map/attn_forward/pallas_call | solution.py:71
  249.9 17.4 %multiply_convert_fusion.1 = (bf16[1024,1536]{1,0:T(8,128)(2,1)S(1)}, f32[1024,1536]{1,0:T(8,128)}, f32[1024,1536]{1,0:T(8,128)}) fusion(f32[1536]{0:T(1024)S(1)} %get-tuple-element.62, bf16[1024,768]{1,0:T(8,128)(2,1)S(1)} %fusion.25, bf16[2,768,3456]{2,1,0:T(8,128)(2,1)S(1)} %bitcast.224), kind=kOutput, calls=%fused_computation.24 | convolution fusion | flops 2519728128 | bytes 19668992 | tf_op jit(solution)/shard_map/dot_general | solution.py:18
  270.0 17.1 %multiply_convert_fusion = (bf16[1024,1536]{1,0:T(8,128)(2,1)S(1)}, f32[1024,1536]{1,0:T(8,128)}, f32[1024,1536]{1,0:T(8,128)}) fusion(f32[1536]{0:T(1024)S(1)} %get-tuple-element.61, bf16[1024,768]{1,0:T(8,128)(2,1)S(1)} %fusion.25, bf16[2,768,3456]{2,1,0:T(8,128)(2,1)S(1)} %bitcast.226), kind=kOutput, calls=%fused_computation.11 | convolution fusion | flops 2519728128 | bytes 19668992 | tf_op jit(solution)/shard_map/dot_general | solution.py:18
  296.0 8.4 %convert_reduce_fusion.1 = (f32[1536]{0:T(1024)}, bf16[1024,1536]{1,0:T(8,128)(2,1)S(1)}) fusion(f32[1024,1536]{1,0:T(8,128)} %get-tuple-element.71, bf16[1024,768]{1,0:T(8,128)(2,1)S(1)} %get-tuple-element.64, bf16[2,768,3456]{2,1,0:T(8,128)(2,1)S(1)} %bitcast.228, f32[1024,1536]{1,0:T(8,128)} %get-tuple-element.89, f32[1536]{0:T(1024)S(1)} %get-tuple-element.62), kind=kOutput, calls=%fused_computation.8 | convolution fusion | flops 2442656256 | bytes 19675136 | tf_op jit(solution)/shard_map/dot_general | solution.py:18
  308.7 7.9 %convert_reduce_fusion = (f32[1536]{0:T(1024)}, bf16[1024,1536]{1,0:T(8,128)(2,1)S(1)}) fusion(f32[1024,1536]{1,0:T(8,128)} %get-tuple-element.69, bf16[1024,768]{1,0:T(8,128)(2,1)S(1)} %get-tuple-element.64, bf16[2,768,3456]{2,1,0:T(8,128)(2,1)S(1)} %bitcast.230, f32[1024,1536]{1,0:T(8,128)} %get-tuple-element.90, f32[1536]{0:T(1024)S(1)} %get-tuple-element.61), kind=kOutput, calls=%fused_computation.7 | convolution fusion | flops 2442656256 | bytes 19675136 | tf_op jit(solution)/shard_map/dot_general | solution.py:18
  332.6 130.6 %attn_backward.1 = (bf16[2,384,1024]{2,1,0:T(8,128)(2,1)}, bf16[2,2,384,4096]{3,2,1,0:T(8,128)(2,1)}) custom-call(bf16[2,384,1024]{2,1,0:T(8,128)(2,1)} %add_convert_fusion.4.refs_0_, bf16[2,2,384,4096]{3,2,1,0:T(8,128)(2,1)} %bitcast.200, bf16[2,384,1024]{2,1,0:T(8,128)(2,1)} %get-tuple-element.94.refs_2_, f32[2,6,1,1024]{3,2,1,0:T(1,128)} %get-tuple-element.15.refs_3_, ...), custom_call_target="tpu_custom_call" | custom-call | tf_op jit(solution)/shard_map/attn_backward/pallas_call | solution.py:156
  473.2 12.2 %convolution_convert_fusion.6 = bf16[768,768]{0,1:T(8,128)(2,1)S(1)} fusion(bf16[768,4096]{1,0:T(8,128)(2,1)S(1)} %bitcast.208, bf16[4096,768]{1,0:T(8,128)(2,1)} %constant_dynamic-update-slice_fusion), kind=kOutput, calls=%fused_computation.115 | convolution fusion | flops 4832428032 | bytes 13762560 | tf_op jit(solution)/shard_map/dot_general | solution.py:18
  518.6 10.3 %fusion.52 = f32[4096,768]{1,0:T(8,128)} fusion(bf16[768,4096]{1,0:T(8,128)(2,1)} %bitcast.209, bf16[2,768,1280]{2,1,0:T(8,128)(2,1)} %bitcast.213), kind=kOutput, calls=%fused_computation.122 | convolution fusion | flops 4831838208 | bytes 20054016 | tf_op jit(solution)/shard_map/dot_general | solution.py:18
  529.0 11.5 %fusion.88 = (bf16[4096,768]{1,0:T(8,128)(2,1)}, f32[4096,768]{1,0:T(8,128)S(1)}) fusion(f32[4096,768]{1,0:T(8,128)} %fusion.52, bf16[768,4096]{1,0:T(8,128)(2,1)} %bitcast.203, bf16[2,768,1280]{2,1,0:T(8,128)(2,1)} %bitcast.214), kind=kOutput, calls=%fused_computation.203 | convolution fusion | flops 4838129664 | bytes 38928384 | tf_op jit(solution)/shard_map/dot_general | solution.py:18
  546.3 45.0 %collective-permute-done.8 = bf16[512,768]{1,0:T(8,128)(2,1)S(1)} collective-permute-done((bf16[512,768]{1,0:T(8,128)(2,1)S(1)}, bf16[512,768]{1,0:T(8,128)(2,1)S(1)}, u32[]{:S(2)}, u32[]{:S(2)}) %collective-permute-start.8) | collective-permute-done | bytes 786464 | tf_op jit(solution)/shard_map/ppermute | solution.py:202
  591.6 21.6 %collective-permute-done.9 = bf16[512,768]{1,0:T(8,128)(2,1)S(1)} collective-permute-done((bf16[512,768]{1,0:T(8,128)(2,1)S(1)}, bf16[512,768]{1,0:T(8,128)(2,1)S(1)}, u32[]{:S(2)}, u32[]{:S(2)}) %collective-permute-start.9) | collective-permute-done | bytes 786464 | tf_op jit(solution)/shard_map/ppermute | solution.py:202
  620.2 16.6 %collective-permute-done.12 = bf16[512,768]{1,0:T(8,128)(2,1)S(1)} collective-permute-done((bf16[512,768]{1,0:T(8,128)(2,1)S(1)}, bf16[512,768]{1,0:T(8,128)(2,1)S(1)}, u32[]{:S(2)}, u32[]{:S(2)}) %collective-permute-start.12) | collective-permute-done | bytes 786464 | tf_op jit(solution)/shard_map/ppermute | solution.py:203
  649.1 15.7 %collective-permute-start.23 = (f32[8448]{0:T(1024)S(1)}, f32[8448]{0:T(1024)S(1)}, u32[]{:S(2)}, u32[]{:S(2)}) collective-permute-start(f32[8448]{0:T(1024)S(1)} %add.282), channel_id=1, source_target_pairs={{0,2},{2,0},{4,6},{6,4},{1,3},{3,1},{5,7},{7,5},{8,10},{10,8},{12,... | collective-permute-start | bytes 101384 | tf_op jit(solution)/shard_map/ppermute | solution.py:212
  682.3 16.7 %collective-permute-done.17 = f32[768]{0:T(1024)S(1)} collective-permute-done((f32[768]{0:T(1024)S(1)}, f32[768]{0:T(1024)S(1)}, u32[]{:S(2)}, u32[]{:S(2)}) %collective-permute-start.17) | collective-permute-done | bytes 3104 | tf_op jit(solution)/shard_map/ppermute | solution.py:212
  699.1 11.1 %collective-permute-start.18 = (f32[768]{0:T(1024)S(1)}, f32[768]{0:T(1024)S(1)}, u32[]{:S(2)}, u32[]{:S(2)}) collective-permute-start(f32[768]{0:T(1024)S(1)} %add.276), channel_id=1, source_target_pairs={{0,2},{2,0},{4,6},{6,4},{1,3},{3,1},{5,7},{7,5},{8,10},{10,8},{12,... | collective-permute-start | bytes 9224 | tf_op jit(solution)/shard_map/ppermute | solution.py:212
  729.7 41.8 %reduce-scatter.5.cloned.1.call-done = bf16[48,3456]{1,0:T(8,128)(2,1)} async-done(((bf16[1536,3456]{1,0:T(8,128)(2,1)}), bf16[48,3456]{1,0:T(8,128)(2,1)}) %reduce-scatter.5.cloned.1.call-update) | async-done | bytes 331792 | tf_op jit(solution)/shard_map/reduce_scatter | solution.py:379
  (268 shorter events, 186.6 us)
Async XLA Ops:
  7.2 141.1 %all-gather.3.cloned.1.call-start = ((), (), s32[]{:S(2)}) async-start(), calls=%async_computation.2 | async-start | bytes 4055040 | tf_op jit(solution)/shard_map/all_gather | solution.py:297
  10.6 232.6 %all-gather.5.cloned.1.call-start = ((), (), s32[]{:S(2)}) async-start(), calls=%async_computation.3 | async-start | bytes 10948608 | tf_op jit(solution)/shard_map/all_gather | solution.py:301
  12.4 715.5 %reduce-scatter.3.cloned.1.call-start = ((), (), s32[]{:S(2)}) async-start(), calls=%async_computation.4 | async-start | bytes 3649536 | tf_op jit(solution)/shard_map/reduce_scatter | solution.py:429
  14.9 26.2 %collective-permute-start.1 = (bf16[512,768]{1,0:T(8,128)(2,1)S(1)}, bf16[512,768]{1,0:T(8,128)(2,1)}, u32[]{:S(2)}, u32[]{:S(2)}) collective-permute-start(bf16[512,768]{1,0:T(8,128)(2,1)S(1)} %get-tuple-element.80), channel_id=1, source_target_pairs={{0,2},{2,4},{4,6},{6,0},{1,3},{3,5},{5,7},{7,1},{8,10},{10,12},{12... | collective-permute-start | bytes 2359304 | tf_op jit(solution)/shard_map/ppermute | solution.py:187
  17.9 46.9 %collective-permute-start.2 = (bf16[512,768]{1,0:T(8,128)(2,1)}, bf16[512,768]{1,0:T(8,128)(2,1)}, u32[]{:S(2)}, u32[]{:S(2)}) collective-permute-start(bf16[512,768]{1,0:T(8,128)(2,1)} %get-tuple-element.79), channel_id=1, source_target_pairs={{2,0},{4,2},{6,4},{0,6},{3,1},{5,3},{7,5},{1,7},{10,8},{12,10},{14... | collective-permute-start | bytes 2359304 | tf_op jit(solution)/shard_map/ppermute | solution.py:188
  41.1 44.9 %collective-permute-start.3 = (bf16[512,768]{1,0:T(8,128)(2,1)}, bf16[512,768]{1,0:T(8,128)(2,1)}, u32[]{:S(2)}, u32[]{:S(2)}) collective-permute-start(bf16[512,768]{1,0:T(8,128)(2,1)} %collective-permute-done.1), channel_id=1, source_target_pairs={{0,2},{2,4},{4,6},{6,0},{1,3},{3,5},{5,7},{7,1},{8,10},{10,12},{12... | collective-permute-start | bytes 2359304 | tf_op jit(solution)/shard_map/ppermute | solution.py:187
  51.9 14.4 %collective-permute-start = (bf16[2304]{0:T(1024)(128)(2,1)S(1)}, bf16[2304]{0:T(1024)(128)(2,1)S(1)}, u32[]{:S(2)}, u32[]{:S(2)}) collective-permute-start(bf16[2304]{0:T(1024)(128)(2,1)S(1)} %dynamic-update-slice.17), channel_id=1, source_target_pairs={{0,1},{1,0},{2,3},{3,2},{4,5},{5,4},{6,7},{7,6},{8,9},{9,8},{10,11... | collective-permute-start | bytes 13832 | tf_op jit(solution)/shard_map/ppermute | solution.py:223
  64.8 42.7 %collective-permute-start.4 = (bf16[512,768]{1,0:T(8,128)(2,1)}, bf16[512,768]{1,0:T(8,128)(2,1)}, u32[]{:S(2)}, u32[]{:S(2)}) collective-permute-start(bf16[512,768]{1,0:T(8,128)(2,1)} %collective-permute-done.2), channel_id=1, source_target_pairs={{2,0},{4,2},{6,4},{0,6},{3,1},{5,3},{7,5},{1,7},{10,8},{12,10},{14... | collective-permute-start | bytes 2359304 | tf_op jit(solution)/shard_map/ppermute | solution.py:188
  86.0 44.0 %collective-permute-start.5 = (bf16[512,768]{1,0:T(8,128)(2,1)}, bf16[512,768]{1,0:T(8,128)(2,1)S(1)}, u32[]{:S(2)}, u32[]{:S(2)}) collective-permute-start(bf16[512,768]{1,0:T(8,128)(2,1)} %collective-permute-done.3), channel_id=1, source_target_pairs={{0,2},{2,4},{4,6},{6,0},{1,3},{3,5},{5,7},{7,1},{8,10},{10,12},{12... | collective-permute-start | bytes 2359304 | tf_op jit(solution)/shard_map/ppermute | solution.py:187
  107.5 39.9 %collective-permute-start.6 = (bf16[512,768]{1,0:T(8,128)(2,1)}, bf16[512,768]{1,0:T(8,128)(2,1)S(1)}, u32[]{:S(2)}, u32[]{:S(2)}) collective-permute-start(bf16[512,768]{1,0:T(8,128)(2,1)} %collective-permute-done.4), channel_id=1, source_target_pairs={{2,0},{4,2},{6,4},{0,6},{3,1},{5,3},{7,5},{1,7},{10,8},{12,10},{14... | collective-permute-start | bytes 2359304 | tf_op jit(solution)/shard_map/ppermute | solution.py:188
  495.0 276.6 %reduce-scatter.5.cloned.1.call-start = ((), (), s32[]{:S(2)}) async-start(), calls=%async_computation.5 | async-start | bytes 10948608 | tf_op jit(solution)/shard_map/reduce_scatter | solution.py:379
  543.1 48.2 %collective-permute-start.8 = (bf16[512,768]{1,0:T(8,128)(2,1)S(1)}, bf16[512,768]{1,0:T(8,128)(2,1)S(1)}, u32[]{:S(2)}, u32[]{:S(2)}) collective-permute-start(bf16[512,768]{1,0:T(8,128)(2,1)S(1)} %get-tuple-element.76), channel_id=1, source_target_pairs={{2,0},{4,2},{6,4},{0,6},{3,1},{5,3},{7,5},{1,7},{10,8},{12,10},{14... | collective-permute-start | bytes 2359304 | tf_op jit(solution)/shard_map/ppermute | solution.py:202
  546.3 45.3 %collective-permute-start.11 = (bf16[512,768]{1,0:T(8,128)(2,1)S(1)}, bf16[512,768]{1,0:T(8,128)(2,1)S(1)}, u32[]{:S(2)}, u32[]{:S(2)}) collective-permute-start(bf16[512,768]{1,0:T(8,128)(2,1)S(1)} %get-tuple-element.77), channel_id=1, source_target_pairs={{0,2},{2,4},{4,6},{6,0},{1,3},{3,5},{5,7},{7,1},{8,10},{10,12},{12... | collective-permute-start | bytes 2359304 | tf_op jit(solution)/shard_map/ppermute | solution.py:203
  591.5 21.6 %collective-permute-start.9 = (bf16[512,768]{1,0:T(8,128)(2,1)S(1)}, bf16[512,768]{1,0:T(8,128)(2,1)S(1)}, u32[]{:S(2)}, u32[]{:S(2)}) collective-permute-start(bf16[512,768]{1,0:T(8,128)(2,1)S(1)} %fusion.37), channel_id=1, source_target_pairs={{2,0},{4,2},{6,4},{0,6},{3,1},{5,3},{7,5},{1,7},{10,8},{12,10},{14... | collective-permute-start | bytes 2359304 | tf_op jit(solution)/shard_map/ppermute | solution.py:202
  614.5 22.3 %collective-permute-start.12 = (bf16[512,768]{1,0:T(8,128)(2,1)S(1)}, bf16[512,768]{1,0:T(8,128)(2,1)S(1)}, u32[]{:S(2)}, u32[]{:S(2)}) collective-permute-start(bf16[512,768]{1,0:T(8,128)(2,1)S(1)} %get-tuple-element.73), channel_id=1, source_target_pairs={{0,2},{2,4},{4,6},{6,0},{1,3},{3,5},{5,7},{7,1},{8,10},{10,12},{12... | collective-permute-start | bytes 2359304 | tf_op jit(solution)/shard_map/ppermute | solution.py:203
  617.3 47.6 %collective-permute-start.10 = (bf16[512,768]{1,0:T(8,128)(2,1)}, bf16[512,768]{1,0:T(8,128)(2,1)}, u32[]{:S(2)}, u32[]{:S(2)}) collective-permute-start(bf16[512,768]{1,0:T(8,128)(2,1)} %get-tuple-element.72), channel_id=1, source_target_pairs={{2,0},{4,2},{6,4},{0,6},{3,1},{5,3},{7,5},{1,7},{10,8},{12,10},{14... | collective-permute-start | bytes 2359304 | tf_op jit(solution)/shard_map/ppermute | solution.py:202
  639.3 29.5 %collective-permute-start.13 = (bf16[512,768]{1,0:T(8,128)(2,1)}, bf16[512,768]{1,0:T(8,128)(2,1)}, u32[]{:S(2)}, u32[]{:S(2)}) collective-permute-start(bf16[512,768]{1,0:T(8,128)(2,1)} %fusion.36), channel_id=1, source_target_pairs={{0,2},{2,4},{4,6},{6,0},{1,3},{3,5},{5,7},{7,1},{8,10},{10,12},{12... | collective-permute-start | bytes 2359304 | tf_op jit(solution)/shard_map/ppermute | solution.py:203
  647.4 77.1 %collective-permute-start.7 = (bf16[1,512,768]{2,1,0:T(8,128)(2,1)}, bf16[1,512,768]{2,1,0:T(8,128)(2,1)}, u32[]{:S(2)}, u32[]{:S(2)}) collective-permute-start(bf16[1,512,768]{2,1,0:T(8,128)(2,1)} %dynamic-slice_bitcast_fusion.3), channel_id=1, source_target_pairs={{0,1},{1,0},{2,3},{3,2},{4,5},{5,4},{6,7},{7,6},{8,9},{9,8},{10,11... | collective-permute-start | bytes 2359304 | tf_op jit(solution)/shard_map/ppermute | solution.py:238
  649.1 67.8 %collective-permute-start.23 = (f32[8448]{0:T(1024)S(1)}, f32[8448]{0:T(1024)S(1)}, u32[]{:S(2)}, u32[]{:S(2)}) collective-permute-start(f32[8448]{0:T(1024)S(1)} %add.282), channel_id=1, source_target_pairs={{0,2},{2,0},{4,6},{6,4},{1,3},{3,1},{5,7},{7,5},{8,10},{10,8},{12,... | collective-permute-start | bytes 101384 | tf_op jit(solution)/shard_map/ppermute | solution.py:212
  674.7 52.0 %collective-permute-start.14 = (bf16[1,512,768]{2,1,0:T(8,128)(2,1)}, bf16[1,512,768]{2,1,0:T(8,128)(2,1)}, u32[]{:S(2)}, u32[]{:S(2)}) collective-permute-start(bf16[1,512,768]{2,1,0:T(8,128)(2,1)} %dynamic-slice_bitcast_fusion.2), channel_id=1, source_target_pairs={{0,1},{1,0},{2,3},{3,2},{4,5},{5,4},{6,7},{7,6},{8,9},{9,8},{10,11... | collective-permute-start | bytes 2359304 | tf_op jit(solution)/shard_map/ppermute | solution.py:238
  682.3 16.7 %collective-permute-start.17 = (f32[768]{0:T(1024)S(1)}, f32[768]{0:T(1024)S(1)}, u32[]{:S(2)}, u32[]{:S(2)}) collective-permute-start(f32[768]{0:T(1024)S(1)} %add.275), channel_id=1, source_target_pairs={{0,1},{1,0},{2,3},{3,2},{4,5},{5,4},{6,7},{7,6},{8,9},{9,8},{10,11... | collective-permute-start | bytes 9224 | tf_op jit(solution)/shard_map/ppermute | solution.py:212
  699.1 12.8 %collective-permute-start.18 = (f32[768]{0:T(1024)S(1)}, f32[768]{0:T(1024)S(1)}, u32[]{:S(2)}, u32[]{:S(2)}) collective-permute-start(f32[768]{0:T(1024)S(1)} %add.276), channel_id=1, source_target_pairs={{0,2},{2,0},{4,6},{6,4},{1,3},{3,1},{5,7},{7,5},{8,10},{10,8},{12,... | collective-permute-start | bytes 9224 | tf_op jit(solution)/shard_map/ppermute | solution.py:212
  711.8 6.7 collective-permute-start.19
  717.0 4.9 collective-permute-start.24
  (52 other events, 836.8 us)
Sparse Core Ops, SparseCore 0:
  11.4 85.2 all-gather.2
  99.5 112.3 all-gather.4
  495.1 122.9 reduce-scatter.2
  624.0 147.4 reduce-scatter.4

commit v2 on v1

--- a/solution.py
+++ b/solution.py
@@ -35,68 +35,109 @@
     return wanted
 
 
-def forward_kernel(q_ref, kv_ref, o_ref, lse_ref, qx, kx, vx, *, bk):
+def forward_kernel(*refs, chunks, first, last, bk):
+    q_ref = refs[0]
+    kv_refs = refs[1 : 1 + chunks]
+    at = 1 + chunks
+    if not first:
+        o_in, stat_in = refs[at : at + 2]
+        at += 2
+    o_ref, stat_ref, qx, kx, vx = refs[at:]
     rows = q_ref.shape[-1]
-    keys = kv_ref.shape[-1]
+    keys = kx.shape[-1]
     scaled = q_ref[0].astype(F) * (score_scale * LOG2E)
     high, rest = split_low(scaled, 2)
     qx[0:HD, :] = high
     qx[HD : 2 * HD, :] = rest
-    kx[0:HD, :] = kv_ref[0, 0]
-    kx[HD : 2 * HD, :] = kv_ref[0, 0]
-    vx[0:HD, :] = kv_ref[0, 1]
+    size = keys // chunks
+    for c, kv_ref in enumerate(kv_refs):
+        at = c * size
+        kx[0:HD, at : at + size] = kv_ref[0, 0]
+        kx[HD : 2 * HD, at : at + size] = kv_ref[0, 0]
+        vx[0:HD, at : at + size] = kv_ref[0, 1]
     vx[HD : HD + 16, :] = jnp.ones((16, keys), B)
 
     def step(i, carry):
-        row_max, mixed = carry
+        row_max, mixed, total = carry
         off = pl.multiple_of(i * bk, bk)
         scores = dot(kx[:, pl.ds(off, bk)], qx[...], 0, 0)
         new_max = jnp.maximum(row_max, jnp.max(scores, axis=0, keepdims=True))
         probs = jnp.exp2(scores - new_max).astype(B)
-        mixed = mixed * jnp.exp2(row_max - new_max) + dot(vx[:, pl.ds(off, bk)], probs, 1, 0)
-        return new_max, mixed
-
-    start = (jnp.full((1, rows), -jnp.inf, F), jnp.zeros((HD + 16, rows), F))
-    row_max, mixed = lax.fori_loop(0, keys // bk, step, start)
-    total = mixed[HD : HD + 1, :]
-    o_ref[0] = mixed[0:HD, :] / total
-    lse_ref[0, 0] = row_max + jnp.log2(total)
-
-
-def attention_forward(q_t, kv_t, bk):
+        scale = jnp.exp2(row_max - new_max)
+        more = dot(vx[:, pl.ds(off, bk)], probs, 1, 0)
+        return new_max, mixed * scale + more[0:HD, :], total * scale + more[HD : HD + 1, :]
+
+    if first:
+        start = (
+            jnp.full((1, rows), -jnp.inf, F),
+            jnp.zeros((HD, rows), F),
+            jnp.zeros((1, rows), F),
+        )
+    else:
+        start = (stat_in[0, 0, 0:1, :], o_in[0], stat_in[0, 0, 1:2, :])
+    row_max, mixed, total = lax.fori_loop(0, keys // bk, step, start)
+    if last:
+        o_ref[0] = mixed / total
+        stat_ref[0, 0] = row_max + jnp.log2(total)
+    else:
+        o_ref[0] = mixed
+        stat_ref[0, 0, 0:1, :] = row_max
+        stat_ref[0, 0, 1:2, :] = total
+
+
+def attention_forward(q_t, kv_list, state, last, bk):
     parts, width, rows = q_t.shape
-    keys = kv_t.shape[3]
+    chunks = len(kv_list)
+    keys = kv_list[0].shape[3]
     heads = width // HD
-    bk = pick_block(keys, bk)
+    bk = pick_block(keys * chunks, bk)
+    first = state is None
+    row_spec = pl.BlockSpec((1, HD, rows), lambda t, h: (t, h, 0))
+    two_spec = pl.BlockSpec((1, 1, 2, rows), lambda t, h: (t, h, 0, 0))
+    one_spec = pl.BlockSpec((1, 1, 1, rows), lambda t, h: (t, h, 0, 0))
+    key_spec = pl.BlockSpec((1, 2, HD, keys), lambda t, h: (t, 0, h, 0))
+    total = parts * heads * rows * keys * chunks
     return pl.pallas_call(
-        lambda *refs: forward_kernel(*refs, bk=bk),
+        lambda *refs: forward_kernel(*refs, chunks=chunks, first=first, last=last, bk=bk),
         grid=(parts, heads),
-        in_specs=[
-            pl.BlockSpec((1, HD, rows), lambda t, h: (t, h, 0)),
-            pl.BlockSpec((1, 2, HD, keys), lambda t, h: (t, 0, h, 0)),
-        ],
-        out_specs=[
-            pl.BlockSpec((1, HD, rows), lambda t, h: (t, h, 0)),
-            pl.BlockSpec((1, 1, 1, rows), lambda t, h: (t, h, 0, 0)),
-        ],
+        in_specs=[row_spec] + [key_spec] * chunks + ([] if first else [row_spec, two_spec]),
+        out_specs=[row_spec, one_spec if last else two_spec],
         out_shape=[
             jax.ShapeDtypeStruct((parts, width, rows), F),
-            jax.ShapeDtypeStruct((parts, heads, 1, rows), F),
+            jax.ShapeDtypeStruct((parts, heads, 1 if last else 2, rows), F),
         ],
         scratch_shapes=[
             pltpu.VMEM((2 * HD, rows), B),
-            pltpu.VMEM((2 * HD, keys), B),
-            pltpu.VMEM((HD + 16, keys), B),
+            pltpu.VMEM((2 * HD, keys * chunks), B),
+            pltpu.VMEM((HD + 16, keys * chunks), B),
         ],
         compiler_params=pltpu.CompilerParams(
             vmem_limit_bytes=56 << 20, dimension_semantics=("arbitrary", "arbitrary")
         ),
+        cost_estimate=pl.CostEstimate(
+            flops=1024 * total, transcendentals=total, bytes_accessed=16 << 20
+        ),
         name="attn_forward",
-    )(q_t, kv_t)
+    )(q_t, *kv_list, *(() if first else state))
 
 
 def backward_kernel(
-    q_ref, kv_ref, do_ref, lse_ref, delta_ref, dq_ref, dkv_ref, qx, kx, dx, vx, dq_acc, *, bk, bq
+    q_ref,
+    kv_ref,
+    do_ref,
+    lse_ref,
+    delta_ref,
+    dq_in,
+    dq_ref,
+    dkv_ref,
+    qx,
+    kx,
+    dx,
+    vx,
+    dq_acc,
+    *,
+    bk,
+    bq,
 ):
     rows = q_ref.shape[-1]
     keys = kv_ref.shape[-1]
@@ -141,25 +182,26 @@
         return carry
 
     lax.fori_loop(0, keys // bk, step, 0)
-    dq_ref[0] = jnp.transpose(dq_acc[...] * score_scale).astype(dq_ref.dtype)
-
-
-def attention_backward(q_t, kv_t, do_t, lse, delta, bk, bq, dq_type):
+    dq_ref[0] = dq_in[0] + jnp.transpose(dq_acc[...] * score_scale)
+
+
+def attention_backward(q_t, kv_t, do_t, lse, delta, dq_t, bk, bq):
     parts, width, rows = q_t.shape
     keys = kv_t.shape[3]
     heads = width // HD
     bk = pick_block(keys, bk)
     bq = pick_block(rows, bq)
+    total = parts * heads * rows * keys
     row_spec = pl.BlockSpec((1, HD, rows), lambda t, h: (t, h, 0))
     stat_spec = pl.BlockSpec((1, 1, 1, rows), lambda t, h: (t, h, 0, 0))
     key_spec = pl.BlockSpec((1, 2, HD, keys), lambda t, h: (t, 0, h, 0))
     return pl.pallas_call(
         lambda *refs: backward_kernel(*refs, bk=bk, bq=bq),
         grid=(parts, heads),
-        in_specs=[row_spec, key_spec, row_spec, stat_spec, stat_spec],
+        in_specs=[row_spec, key_spec, row_spec, stat_spec, stat_spec, row_spec],
         out_specs=[row_spec, key_spec],
         out_shape=[
-            jax.ShapeDtypeStruct((parts, width, rows), dq_type),
+            jax.ShapeDtypeStruct((parts, width, rows), F),
             jax.ShapeDtypeStruct((parts, 2, width, keys), B),
         ],
         scratch_shapes=[
@@ -172,8 +214,12 @@
         compiler_params=pltpu.CompilerParams(
             vmem_limit_bytes=56 << 20, dimension_semantics=("arbitrary", "arbitrary")
         ),
+        cost_estimate=pl.CostEstimate(
+            flops=2048 * total, transcendentals=total, bytes_accessed=16 << 20
+        ),
+        input_output_aliases={5: 0},
         name="attn_backward",
-    )(q_t, kv_t, do_t, lse, delta)
+    )(q_t, kv_t, do_t, lse, delta, dq_t)
 
 
 def ring_gather(block):
@@ -190,18 +236,36 @@
     return pieces
 
 
-def ring_reduce(pieces):
+def ring_return(first, second):
     count = lax.axis_size("ctx")
     up = [(i, (i + 1) % count) for i in range(count)]
     down = [((i + 1) % count, i) for i in range(count)]
-    first = second = None
-    for one, two in reversed(pieces):
-        if first is not None:
-            one = one + first.astype(F)
-            two = two + second.astype(F)
-        first = lax.ppermute(one.astype(B), "ctx", down)
-        second = lax.ppermute(two.astype(B), "ctx", up)
-    return jnp.concatenate([first, second], axis=0).astype(F)
+    return lax.ppermute(first, "ctx", down), lax.ppermute(second, "ctx", up)
+
+
+def scatter_sum(blocks, order):
+    sizes = {axis: lax.axis_size(axis) for axis in WEIGHT_AXES}
+    bits = []
+    for axis in WEIGHT_AXES:
+        bit = sizes[axis] // 2
+        while bit:
+            bits.append((axis, bit))
+            bit //= 2
+    left = blocks.reshape((2,) * len(bits) + blocks.shape[2:])
+    todo = sorted(
+        bits,
+        key=lambda one: (one != ("fsdp", 1), order.index(one[0]), -one[1]),
+    )
+    for axis, bit in todo:
+        dim = bits.index((axis, bit))
+        bits.remove((axis, bit))
+        mine = (lax.axis_index(axis) // bit) % 2
+        sent = lax.dynamic_index_in_dim(left, 1 - mine, dim, keepdims=False)
+        kept = lax.dynamic_index_in_dim(left, mine, dim, keepdims=False)
+        got = lax.ppermute(sent, axis, [(i, i ^ bit) for i in range(sizes[axis])])
+        total = kept.astype(F) + got.astype(F)
+        left = total.astype(B) if bits else total
+    return left
 
 
 def sum_all(vector):
@@ -314,22 +378,31 @@
     u_bias = bias_all[:, 2 * head_width :].astype(F)
     kv_bias = jnp.concatenate([jnp.zeros_like(v_bias), v_bias], axis=1)
 
-    x_full = [
-        jnp.concatenate([own_tokens[s]] + [p for pair in x_pieces[s] for p in pair], axis=0)
+    def project(block):
+        got = (dot(w_kv, block, 1, 1) + kv_bias[:, :, None]).astype(B)
+        return got.reshape(tp_count, 2, head_width, block.shape[0])
+
+    x_chunks = [
+        [own_tokens[s]] + [jnp.concatenate(pair, axis=0) for pair in x_pieces[s]]
         for s in range(own_seqs)
     ]
-    q_t = [
-        (dot(w_q, own_tokens[s], 1, 1) + q_bias[:, :, None]).astype(B) for s in range(own_seqs)
-    ]
-    kv_t = [
-        (dot(w_kv, x_full[s], 1, 1) + kv_bias[:, :, None])
-        .astype(B)
-        .reshape(tp_count, 2, head_width, x_full[s].shape[0])
-        for s in range(own_seqs)
-    ]
-    attended = [attention_forward(q_t[s], kv_t[s], 2048) for s in range(own_seqs)]
-    om_t = [one[0] for one in attended]
-    lse = [one[1] for one in attended]
+    chunk_count = len(x_chunks[0])
+    near = (chunk_count + 1) // 2
+    q_t, kv_t, om_t, lse = [], [], [], []
+    for s in range(own_seqs):
+        q_s = (dot(w_q, own_tokens[s], 1, 1) + q_bias[:, :, None]).astype(B)
+        kv_s = [project(block) for block in x_chunks[s][:near]]
+        if near < chunk_count:
+            state = attention_forward(q_s, kv_s, None, False, 2048)
+            kv_far = [project(block) for block in x_chunks[s][near:]]
+            done = attention_forward(q_s, kv_far, state, True, 2048)
+            kv_s = kv_s + kv_far
+        else:
+            done = attention_forward(q_s, kv_s, None, True, 2048)
+        q_t.append(q_s)
+        kv_t.append(kv_s)
+        om_t.append(done[0])
+        lse.append(done[1])
     mixed_t = jnp.concatenate([one.astype(B) for one in om_t], axis=2)
     attn_part = sum(dot(mixed_t[t], w_out[t], 0, 1) for t in range(tp_count))
     x_float = x_own.astype(F)
@@ -376,6 +449,8 @@
             for t in range(tp_count)
         ]
     )
+    do_t = dot(w_out, da, 1, 1).astype(B)
+    do_t, second_grad = lax.optimization_barrier((do_t, second_grad))
     second_grad = lax.psum_scatter(
         second_grad.reshape(tp_count * width, second_shard.shape[1]),
         WEIGHT_AXES,
@@ -383,7 +458,6 @@
         tiled=True,
     ).astype(F)
 
-    do_t = dot(w_out, da, 1, 1).astype(B)
     v_bias_grad = jnp.sum(do_t.astype(F), axis=2)
     early = sum_all(
         jnp.concatenate(
@@ -392,46 +466,53 @@
             + [v_bias_grad.reshape(-1)]
         )
     )
-    dq_t, dkv_t = [], []
+    kv_grad = [0.0] * tp_count
+    q_grad = [0.0] * tp_count
+    q_bias_grad = 0.0
+    own_grads = []
+    half = local_len // 2
     for s in range(own_seqs):
         do_s = do_t[:, :, s * local_len : (s + 1) * local_len]
         delta = (om_t[s] * do_s.astype(F)).reshape(tp_count, head_width // HD, HD, local_len)
         delta = jnp.sum(delta, axis=2, keepdims=True)
-        one_dq, one_dkv = attention_backward(q_t[s], kv_t[s], do_s, lse[s], delta, 1024, 512, B)
-        dq_t.append(one_dq)
-        dkv_t.append(one_dkv.reshape(tp_count, 2 * head_width, one_dkv.shape[3]))
-    q_bias_grad = sum_all(sum(jnp.sum(one.astype(F), axis=2) for one in dq_t).reshape(-1))
-
-    own_grads = []
-    half = local_len // 2
-    for s in range(own_seqs):
-        full = sum(dot(dkv_t[s][t], w_kv[t], 0, 1) for t in range(tp_count))
-        pieces = []
-        for i in range(len(x_pieces[s])):
-            at = local_len + i * local_len
-            pieces.append((full[at : at + half], full[at + half : at + local_len]))
-        own = full[:local_len] + sum(dot(dq_t[s][t], w_q[t], 0, 1) for t in range(tp_count))
-        own_grads.append(own + ring_reduce(pieces))
+        dq = jnp.zeros(om_t[s].shape, F)
+        got = None
+        for c in reversed(range(chunk_count)):
+            dq, dkv = attention_backward(q_t[s], kv_t[s][c], do_s, lse[s], delta, dq, 1024, 512)
+            dkv = dkv.reshape(tp_count, 2 * head_width, dkv.shape[3])
+            part = sum(dot(dkv[t], w_kv[t], 0, 1) for t in range(tp_count))
+            kv_grad = [kv_grad[t] + dot(x_chunks[s][c], dkv[t], 0, 1) for t in range(tp_count)]
+            if c:
+                one, two = part[:half], part[half:]
+                if got is not None:
+                    one = one + got[0].astype(F)
+                    two = two + got[1].astype(F)
+                one, two, dq, *kv_grad = lax.optimization_barrier(
+                    (one.astype(B), two.astype(B), dq, *kv_grad)
+                )
+                got = ring_return(one, two)
+        dq_low = dq.astype(B)
+        q_bias_grad = q_bias_grad + jnp.sum(dq_low.astype(F), axis=2)
+        q_grad = [q_grad[t] + dot(own_tokens[s], dq_low[t], 0, 1) for t in range(tp_count)]
+        part = part + sum(dot(dq_low[t], w_q[t], 0, 1) for t in range(tp_count))
+        if got is not None:
+            part = part + jnp.concatenate(got, axis=0).astype(F)
+        own_grads.append(part)
+    q_bias_grad = sum_all(q_bias_grad.reshape(-1))
+    qkv_grad = jnp.stack(
+        [jnp.concatenate([q_grad[t], kv_grad[t]], axis=1).astype(B) for t in range(tp_count)]
+    )
+    qkv_grad = qkv_grad.reshape(tp_count, width // shard_rows, shard_rows, 3 * head_width)
+    cut = (3 * head_width // 256) * 128
+    qkv_grad = jnp.concatenate(
+        [
+            scatter_sum(qkv_grad[..., :cut], ("tp", "fsdp", "ctx")),
+            scatter_sum(qkv_grad[..., cut:], ("fsdp", "tp", "ctx")),
+        ],
+        axis=1,
+    )
     tokens_grad = resid_grad.reshape(own_seqs, local_len, width) + jnp.stack(own_grads)
     tokens_out = tp_exchange(tokens_grad.astype(B))
-    qkv_grad = jnp.stack(
-        [
-            jnp.concatenate(
-                [
-                    sum(dot(own_tokens[s], dq_t[s][t], 0, 1) for s in range(own_seqs)).astype(B),
-                    sum(dot(x_full[s], dkv_t[s][t], 0, 1) for s in range(own_seqs)).astype(B),
-                ],
-                axis=1,
-            )
-            for t in range(tp_count)
-        ]
-    )
-    qkv_grad = lax.psum_scatter(
-        qkv_grad.reshape(tp_count * width, 3 * head_width),
-        WEIGHT_AXES,
-        scatter_dimension=0,
-        tiled=True,
-    ).astype(F)
 
     member = lax.axis_index("fsdp") * lax.axis_size("ctx") + lax.axis_index("ctx")
     own_tp = lax.axis_index("tp")

time: 787 us -> 757 us (0.962)
  waiting for transfers between devices: 239 us -> 200 us
  Pallas kernels: 200 us -> 221 us
  starting transfers between devices: 85.7 us -> 66.8 us
  other arithmetic: 27.2 us -> 38.4 us
    reduce_scatter x1, waiting for transfers between devices: 41.8 us -> 0.01 us  [body(): lax.psum_scatter(second_grad.reshape(tp_count * width, second_shard.shape...]
    ppermute x10, starting transfers between devices: 38 us -> 6.4 us  [sum_all(): lax.ppermute(vector, axis, [(i, i ^ bit) for i in range(size)])]
    ppermute x10, waiting for transfers between devices: 27 us -> 55.2 us  [sum_all(): lax.ppermute(vector, axis, [(i, i ^ bit) for i in range(size)])]
    ppermute x6 -> x16, waiting for transfers between devices: 87.1 us -> 61.1 us  [the longest x6 35.2 us: ring_return(): return (lax.ppermute(first, 'ctx', down), lax.ppermute(second, 'ctx', up))]
    pallas_call x1 -> x4, Pallas kernels: 131 us -> 145 us  [attention_backward(): pl.pallas_call(lambda *refs: backward_kernel(*refs, bk=bk, bq=bq), grid=(...]
    ppermute x6 -> x16, starting transfers between devices: 7.19 us -> 21.3 us  [the longest x10 13.6 us: scatter_sum(): got = lax.ppermute(sent, axis, [(i, i ^ bit) for i in range(sizes[axis])])]
    pallas_call x1 -> x2, Pallas kernels: 69.8 us -> 75.5 us  [attention_forward(): pl.pallas_call(lambda *refs: forward_kernel(*refs, chunks=chunks, first=f...]
    unnamed x111 -> x112, local copies, waits for them, and re-layouts: 22.6 us -> 18.3 us
  transfers between devices with their start and end apart: 29 -> 38, of which waited for: 19 -> 18; matrix products, arithmetic and copies ran while one was open for 14% -> 13% of each run, Pallas kernels for 9% -> 20%
where the time goes in v2:
time: 757 us; the launch traced here: 753 us
  Pallas kernels  221 us (29%)
  waiting for transfers between devices  200 us (26%)
  matrix products  159 us (21%)
  starting transfers between devices  66.8 us (9%)
  local copies, waits for them, and re-layouts  52.7 us (7%)
  other arithmetic  38.4 us (5%)
  between operations  15.3 us (2%)
    dot_general x42, matrix products, dot(): lax.dot_general(left, right, (((left_dim,), (right_dim,)), ((), ())), pre...  159 us
    pallas_call x4, Pallas kernels, attention_backward(): pl.pallas_call(lambda *refs: backward_kernel(*refs, bk=bk, bq=bq), grid=(...  145 us
    pallas_call x2, Pallas kernels, attention_forward(): pl.pallas_call(lambda *refs: forward_kernel(*refs, chunks=chunks, first=f...  75.5 us
    ppermute x10, waiting for transfers between devices, sum_all(): lax.ppermute(vector, axis, [(i, i ^ bit) for i in range(size)])  55.2 us
    ppermute x3, waiting for transfers between devices, ring_gather(): first = lax.ppermute(first, 'ctx', up)  54 us
    ppermute x6, waiting for transfers between devices, ring_return(): return (lax.ppermute(first, 'ctx', down), lax.ppermute(second, 'ctx', up))  35.2 us
    ppermute x3, starting transfers between devices, ring_gather(): first = lax.ppermute(first, 'ctx', up)  32.2 us
    ppermute x3, waiting for transfers between devices, ring_gather(): second = lax.ppermute(second, 'ctx', down)  29.2 us
  transfers between devices with their start and end apart: 38, of which 18 were waited for; matrix products, arithmetic and copies ran while one was open for 13% of the time, Pallas kernels for 20%

profile of v2, /device:TPU:0, one launch (start us, length us, event | category | flops | bytes accessed | tf_op | source)
XLA Modules:
  0.0 752.5 jit_solution(14669324924144051604)
XLA Ops:
  19.9 21.2 %collective-permute-done.1 = bf16[512,768]{1,0:T(8,128)(2,1)} collective-permute-done((bf16[512,768]{1,0:T(8,128)(2,1)S(1)}, bf16[512,768]{1,0:T(8,128)(2,1)}, u32[]{:S(2)}, u32[]{:S(2)}) %collective-permute-start.1) | collective-permute-done | bytes 786464 | tf_op jit(solution)/shard_map/ppermute | solution.py:233
  41.1 10.3 %collective-permute-start.2 = (bf16[512,768]{1,0:T(8,128)(2,1)}, bf16[512,768]{1,0:T(8,128)(2,1)}, u32[]{:S(2)}, u32[]{:S(2)}) collective-permute-start(bf16[512,768]{1,0:T(8,128)(2,1)} %collective-permute-done.1), channel_id=1, source_target_pairs={{0,2},{2,4},{4,6},{6,0},{1,3},{3,5},{5,7},{7,1},{8,10},{10,12},{12... | collective-permute-start | bytes 2359304 | tf_op jit(solution)/shard_map/ppermute | solution.py:233
  54.6 10.2 %collective-permute-done.3 = bf16[512,768]{1,0:T(8,128)(2,1)} collective-permute-done((bf16[512,768]{1,0:T(8,128)(2,1)}, bf16[512,768]{1,0:T(8,128)(2,1)}, u32[]{:S(2)}, u32[]{:S(2)}) %collective-permute-start.3) | collective-permute-done | bytes 786464 | tf_op jit(solution)/shard_map/ppermute | solution.py:234
  68.5 17.5 %collective-permute-done.2 = bf16[512,768]{1,0:T(8,128)(2,1)} collective-permute-done((bf16[512,768]{1,0:T(8,128)(2,1)}, bf16[512,768]{1,0:T(8,128)(2,1)}, u32[]{:S(2)}, u32[]{:S(2)}) %collective-permute-start.2) | collective-permute-done | bytes 786464 | tf_op jit(solution)/shard_map/ppermute | solution.py:233
  86.0 18.8 %collective-permute-start.5 = (bf16[512,768]{1,0:T(8,128)(2,1)}, bf16[512,768]{1,0:T(8,128)(2,1)S(1)}, u32[]{:S(2)}, u32[]{:S(2)}) collective-permute-start(bf16[512,768]{1,0:T(8,128)(2,1)} %collective-permute-done.2), channel_id=1, source_target_pairs={{0,2},{2,4},{4,6},{6,0},{1,3},{3,5},{5,7},{7,1},{8,10},{10,12},{12... | collective-permute-start | bytes 2359304 | tf_op jit(solution)/shard_map/ppermute | solution.py:233
  114.7 15.3 %collective-permute-done.5 = bf16[512,768]{1,0:T(8,128)(2,1)S(1)} collective-permute-done((bf16[512,768]{1,0:T(8,128)(2,1)}, bf16[512,768]{1,0:T(8,128)(2,1)S(1)}, u32[]{:S(2)}, u32[]{:S(2)}) %collective-permute-start.5) | collective-permute-done | bytes 786464 | tf_op jit(solution)/shard_map/ppermute | solution.py:233
  130.9 16.4 %collective-permute-done.6 = bf16[512,768]{1,0:T(8,128)(2,1)S(1)} collective-permute-done((bf16[512,768]{1,0:T(8,128)(2,1)}, bf16[512,768]{1,0:T(8,128)(2,1)S(1)}, u32[]{:S(2)}, u32[]{:S(2)}) %collective-permute-start.6) | collective-permute-done | bytes 786464 | tf_op jit(solution)/shard_map/ppermute | solution.py:234
  161.3 5.7 add_convert_fusion.4
  171.3 34.5 %attn_forward.2 = (f32[2,384,1024]{2,1,0:T(8,128)}, f32[2,6,2,1024]{3,2,1,0:T(2,128)}) custom-call(bf16[2,384,1024]{2,1,0:T(8,128)(2,1)} %add_convert_fusion.9.refs_0_, bf16[2,2,384,1024]{3,2,1,0:T(8,128)(2,1)} %bitcast.358, bf16[2,2,384,1024]{3,2,1,0:T(8,128)(2,1)} %bitcast.360), custom_call_target="tpu_custom_call" | custom-call | flops 25769803776 | bytes 16777216 | tf_op jit(solution)/shard_map/attn_forward/pallas_call | solution.py:100
  205.7 41.1 %attn_forward.3 = (f32[2,384,1024]{2,1,0:T(8,128)}, f32[2,6,1,1024]{3,2,1,0:T(1,128)}) custom-call(bf16[2,384,1024]{2,1,0:T(8,128)(2,1)} %add_convert_fusion.9.refs_0_, bf16[2,2,384,1024]{3,2,1,0:T(8,128)(2,1)} %bitcast.362, bf16[2,2,384,1024]{3,2,1,0:T(8,128)(2,1)} %bitcast.364, f32[2,384,1024]{2,1,0:T(8,128)} %get-tuple-element.39.refs_3_, ...), custom_call_target="tpu_custom_call" | custom-call | flops 25769803776 | bytes 16777216 | tf_op jit(solution)/shard_map/attn_forward/pallas_call | solution.py:100
  258.0 16.9 %multiply_convert_fusion.1 = (bf16[1024,1536]{1,0:T(8,128)(2,1)S(1)}, f32[1024,1536]{1,0:T(8,128)}, f32[1024,1536]{1,0:T(8,128)}) fusion(f32[1536]{0:T(1024)S(1)} %get-tuple-element.112, bf16[1024,768]{1,0:T(8,128)(2,1)S(1)} %fusion.21, bf16[2,768,3456]{2,1,0:T(8,128)(2,1)S(1)} %bitcast.353), kind=kOutput, calls=%fused_computation.22 | convolution fusion | flops 2519728128 | bytes 19668992 | tf_op jit(solution)/shard_map/dot_general | solution.py:18
  277.6 17.2 %multiply_convert_fusion = (bf16[1024,1536]{1,0:T(8,128)(2,1)S(1)}, f32[1024,1536]{1,0:T(8,128)}, f32[1024,1536]{1,0:T(8,128)}) fusion(f32[1536]{0:T(1024)S(1)} %get-tuple-element.111, bf16[1024,768]{1,0:T(8,128)(2,1)S(1)} %fusion.21, bf16[2,768,3456]{2,1,0:T(8,128)(2,1)S(1)} %bitcast.355), kind=kOutput, calls=%fused_computation.9 | convolution fusion | flops 2519728128 | bytes 19668992 | tf_op jit(solution)/shard_map/dot_general | solution.py:18
  305.3 7.9 %convert_reduce_fusion.1 = (f32[1536]{0:T(1024)}, bf16[1024,1536]{1,0:T(8,128)(2,1)S(1)}) fusion(f32[1024,1536]{1,0:T(8,128)S(1)} %bitcast.367, bf16[1024,768]{1,0:T(8,128)(2,1)S(1)} %get-tuple-element.116, bf16[2,768,3456]{2,1,0:T(8,128)(2,1)} %bitcast.346, f32[1024,1536]{1,0:T(8,128)} %get-tuple-element.149, f32[1536]{0:T(1024)S(1)} %get-tuple-element.112), kind=kOutput, calls=%fused_computation.6 | convolution fusion | flops 2442656256 | bytes 19673088 | tf_op jit(solution)/shard_map/dot_general | solution.py:18
  324.6 9.0 %convert_reduce_fusion = (f32[1536]{0:T(1024)}, bf16[1024,1536]{1,0:T(8,128)(2,1)S(1)}) fusion(f32[1024,1536]{1,0:T(8,128)} %get-tuple-element.121, bf16[1024,768]{1,0:T(8,128)(2,1)S(1)} %get-tuple-element.116, bf16[2,768,3456]{2,1,0:T(8,128)(2,1)} %bitcast.348, f32[1024,1536]{1,0:T(8,128)} %get-tuple-element.150, f32[1536]{0:T(1024)S(1)} %get-tuple-element.111), kind=kOutput, calls=%fused_computation.5 | convolution fusion | flops 2442656256 | bytes 19673088 | tf_op jit(solution)/shard_map/dot_general | solution.py:18
  333.5 6.3 multiply_reduce_fusion
  369.6 36.1 %attn_backward.4 = (f32[2,384,1024]{2,1,0:T(8,128)}, bf16[2,2,384,1024]{3,2,1,0:T(8,128)(2,1)}) custom-call(bf16[2,384,1024]{2,1,0:T(8,128)(2,1)} %add_convert_fusion.9.refs_0_, bf16[2,2,384,1024]{3,2,1,0:T(8,128)(2,1)} %bitcast.365, bf16[2,384,1024]{2,1,0:T(8,128)(2,1)} %convolution_convert_fusion.4.refs_2_, ...), custom_call_target="tpu_custom_call", output_to_operand_aliasing={{0}: (5, {})} | custom-call | flops 25769803776 | bytes 16777216 | tf_op jit(solution)/shard_map/attn_backward/pallas_call | solution.py:198
  420.9 36.3 %attn_backward.5 = (f32[2,384,1024]{2,1,0:T(8,128)}, bf16[2,2,384,1024]{3,2,1,0:T(8,128)(2,1)}) custom-call(bf16[2,384,1024]{2,1,0:T(8,128)(2,1)} %add_convert_fusion.9.refs_0_, bf16[2,2,384,1024]{3,2,1,0:T(8,128)(2,1)} %bitcast.363, bf16[2,384,1024]{2,1,0:T(8,128)(2,1)} %convolution_convert_fusion.4.refs_2_, ...), custom_call_target="tpu_custom_call", output_to_operand_aliasing={{0}: (5, {})} | custom-call | flops 25769803776 | bytes 16777216 | tf_op jit(solution)/shard_map/attn_backward/pallas_call | solution.py:198
  482.7 17.3 %collective-permute-done.33 = f32[8448]{0:T(1024)S(1)} collective-permute-done((f32[8448]{0:T(1024)S(1)}, f32[8448]{0:T(1024)S(1)}, u32[]{:S(2)}, u32[]{:S(2)}) %collective-permute-start.33) | collective-permute-done | bytes 33824 | tf_op jit(solution)/shard_map/ppermute | solution.py:276
  510.9 36.4 %attn_backward.6 = (f32[2,384,1024]{2,1,0:T(8,128)}, bf16[2,2,384,1024]{3,2,1,0:T(8,128)(2,1)}) custom-call(bf16[2,384,1024]{2,1,0:T(8,128)(2,1)} %add_convert_fusion.9.refs_0_, bf16[2,2,384,1024]{3,2,1,0:T(8,128)(2,1)} %bitcast.361, bf16[2,384,1024]{2,1,0:T(8,128)(2,1)} %convolution_convert_fusion.4.refs_2_, ...), custom_call_target="tpu_custom_call", output_to_operand_aliasing={{0}: (5, {})} | custom-call | flops 25769803776 | bytes 16777216 | tf_op jit(solution)/shard_map/attn_backward/pallas_call | solution.py:198
  563.5 16.5 %collective-permute-done.10 = bf16[512,768]{1,0:T(8,128)(2,1)S(1)} collective-permute-done((bf16[512,768]{1,0:T(8,128)(2,1)S(1)}, bf16[512,768]{1,0:T(8,128)(2,1)S(1)}, u32[]{:S(2)}, u32[]{:S(2)}) %collective-permute-start.10) | collective-permute-done | bytes 786464 | tf_op jit(solution)/shard_map/ppermute | solution.py:243
  580.0 18.7 %collective-permute-done.11 = bf16[512,768]{1,0:T(8,128)(2,1)S(1)} collective-permute-done((bf16[512,768]{1,0:T(8,128)(2,1)S(1)}, bf16[512,768]{1,0:T(8,128)(2,1)S(1)}, u32[]{:S(2)}, u32[]{:S(2)}) %collective-permute-start.11) | collective-permute-done | bytes 786464 | tf_op jit(solution)/shard_map/ppermute | solution.py:243
  600.3 36.5 %attn_backward.7 = (f32[2,384,1024]{2,1,0:T(8,128)}, bf16[2,2,384,1024]{3,2,1,0:T(8,128)(2,1)}) custom-call(bf16[2,384,1024]{2,1,0:T(8,128)(2,1)} %add_convert_fusion.9.refs_0_, bf16[2,2,384,1024]{3,2,1,0:T(8,128)(2,1)} %bitcast.359, bf16[2,384,1024]{2,1,0:T(8,128)(2,1)} %convolution_convert_fusion.4.refs_2_, ...), custom_call_target="tpu_custom_call", output_to_operand_aliasing={{0}: (5, {})} | custom-call | flops 25769803776 | bytes 16777216 | tf_op jit(solution)/shard_map/attn_backward/pallas_call | solution.py:198
  661.1 32.9 %collective-permute-done.28 = f32[768]{0:T(1024)S(1)} collective-permute-done((f32[768]{0:T(1024)S(1)}, f32[768]{0:T(1024)S(1)}, u32[]{:S(2)}, u32[]{:S(2)}) %collective-permute-start.28) | collective-permute-done | bytes 3104 | tf_op jit(solution)/shard_map/ppermute | solution.py:276
  722.5 7.0 collective-permute-done.22
  (338 shorter events, 251.4 us)
Async XLA Ops:
  7.2 141.1 %all-gather.3.cloned.1.call-start = ((), (), s32[]{:S(2)}) async-start(), calls=%async_computation.1 | async-start | bytes 4055040 | tf_op jit(solution)/shard_map/all_gather | solution.py:361
  10.6 240.7 %all-gather.5.cloned.1.call-start = ((), (), s32[]{:S(2)}) async-start(), calls=%async_computation.2 | async-start | bytes 10948608 | tf_op jit(solution)/shard_map/all_gather | solution.py:365
  12.4 730.1 %reduce-scatter.2.cloned.1.call-start = ((), (), s32[]{:S(2)}) async-start(), calls=%async_computation.3 | async-start | bytes 10948608 | tf_op jit(solution)/shard_map/reduce_scatter | solution.py:454
  14.9 26.2 %collective-permute-start.1 = (bf16[512,768]{1,0:T(8,128)(2,1)S(1)}, bf16[512,768]{1,0:T(8,128)(2,1)}, u32[]{:S(2)}, u32[]{:S(2)}) collective-permute-start(bf16[512,768]{1,0:T(8,128)(2,1)S(1)} %get-tuple-element.138), channel_id=1, source_target_pairs={{0,2},{2,4},{4,6},{6,0},{1,3},{3,5},{5,7},{7,1},{8,10},{10,12},{12... | collective-permute-start | bytes 2359304 | tf_op jit(solution)/shard_map/ppermute | solution.py:233
  17.9 46.9 %collective-permute-start.3 = (bf16[512,768]{1,0:T(8,128)(2,1)}, bf16[512,768]{1,0:T(8,128)(2,1)}, u32[]{:S(2)}, u32[]{:S(2)}) collective-permute-start(bf16[512,768]{1,0:T(8,128)(2,1)} %get-tuple-element.137), channel_id=1, source_target_pairs={{2,0},{4,2},{6,4},{0,6},{3,1},{5,3},{7,5},{1,7},{10,8},{12,10},{14... | collective-permute-start | bytes 2359304 | tf_op jit(solution)/shard_map/ppermute | solution.py:234
  41.1 44.9 %collective-permute-start.2 = (bf16[512,768]{1,0:T(8,128)(2,1)}, bf16[512,768]{1,0:T(8,128)(2,1)}, u32[]{:S(2)}, u32[]{:S(2)}) collective-permute-start(bf16[512,768]{1,0:T(8,128)(2,1)} %collective-permute-done.1), channel_id=1, source_target_pairs={{0,2},{2,4},{4,6},{6,0},{1,3},{3,5},{5,7},{7,1},{8,10},{10,12},{12... | collective-permute-start | bytes 2359304 | tf_op jit(solution)/shard_map/ppermute | solution.py:233
  51.9 16.5 %collective-permute-start = (bf16[2304]{0:T(1024)(128)(2,1)S(1)}, bf16[2304]{0:T(1024)(128)(2,1)S(1)}, u32[]{:S(2)}, u32[]{:S(2)}) collective-permute-start(bf16[2304]{0:T(1024)(128)(2,1)S(1)} %dynamic-update-slice.16), channel_id=1, source_target_pairs={{0,1},{1,0},{2,3},{3,2},{4,5},{5,4},{6,7},{7,6},{8,9},{9,8},{10,11... | collective-permute-start | bytes 13832 | tf_op jit(solution)/shard_map/ppermute | solution.py:287
  64.8 42.7 %collective-permute-start.4 = (bf16[512,768]{1,0:T(8,128)(2,1)}, bf16[512,768]{1,0:T(8,128)(2,1)}, u32[]{:S(2)}, u32[]{:S(2)}) collective-permute-start(bf16[512,768]{1,0:T(8,128)(2,1)} %collective-permute-done.3), channel_id=1, source_target_pairs={{2,0},{4,2},{6,4},{0,6},{3,1},{5,3},{7,5},{1,7},{10,8},{12,10},{14... | collective-permute-start | bytes 2359304 | tf_op jit(solution)/shard_map/ppermute | solution.py:234
  86.0 44.0 %collective-permute-start.5 = (bf16[512,768]{1,0:T(8,128)(2,1)}, bf16[512,768]{1,0:T(8,128)(2,1)S(1)}, u32[]{:S(2)}, u32[]{:S(2)}) collective-permute-start(bf16[512,768]{1,0:T(8,128)(2,1)} %collective-permute-done.2), channel_id=1, source_target_pairs={{0,2},{2,4},{4,6},{6,0},{1,3},{3,5},{5,7},{7,1},{8,10},{10,12},{12... | collective-permute-start | bytes 2359304 | tf_op jit(solution)/shard_map/ppermute | solution.py:233
  107.4 39.9 %collective-permute-start.6 = (bf16[512,768]{1,0:T(8,128)(2,1)}, bf16[512,768]{1,0:T(8,128)(2,1)S(1)}, u32[]{:S(2)}, u32[]{:S(2)}) collective-permute-start(bf16[512,768]{1,0:T(8,128)(2,1)} %collective-permute-done.4), channel_id=1, source_target_pairs={{2,0},{4,2},{6,4},{0,6},{3,1},{5,3},{7,5},{1,7},{10,8},{12,10},{14... | collective-permute-start | bytes 2359304 | tf_op jit(solution)/shard_map/ppermute | solution.py:234
  462.5 45.5 %collective-permute-start.8 = (bf16[512,768]{1,0:T(8,128)(2,1)}, bf16[512,768]{1,0:T(8,128)(2,1)}, u32[]{:S(2)}, u32[]{:S(2)}) collective-permute-start(bf16[512,768]{1,0:T(8,128)(2,1)} %get-tuple-element.48), channel_id=1, source_target_pairs={{2,0},{4,2},{6,4},{0,6},{3,1},{5,3},{7,5},{1,7},{10,8},{12,10},{14... | collective-permute-start | bytes 2359304 | tf_op jit(solution)/shard_map/ppermute | solution.py:243
  465.2 42.8 %collective-permute-start.9 = (bf16[512,768]{1,0:T(8,128)(2,1)}, bf16[512,768]{1,0:T(8,128)(2,1)}, u32[]{:S(2)}, u32[]{:S(2)}) collective-permute-start(bf16[512,768]{1,0:T(8,128)(2,1)} %get-tuple-element.49), channel_id=1, source_target_pairs={{0,2},{2,4},{4,6},{6,0},{1,3},{3,5},{5,7},{7,1},{8,10},{10,12},{12... | collective-permute-start | bytes 2359304 | tf_op jit(solution)/shard_map/ppermute | solution.py:243
  480.0 20.0 %collective-permute-start.33 = (f32[8448]{0:T(1024)S(1)}, f32[8448]{0:T(1024)S(1)}, u32[]{:S(2)}, u32[]{:S(2)}) collective-permute-start(f32[8448]{0:T(1024)S(1)} %add.472), channel_id=1, source_target_pairs={{0,2},{2,0},{4,6},{6,4},{1,3},{3,1},{5,7},{7,5},{8,10},{10,8},{12,... | collective-permute-start | bytes 101384 | tf_op jit(solution)/shard_map/ppermute | solution.py:276
  482.2 76.8 %collective-permute-start.7 = (bf16[1,512,768]{2,1,0:T(8,128)(2,1)}, bf16[1,512,768]{2,1,0:T(8,128)(2,1)S(1)}, u32[]{:S(2)}, u32[]{:S(2)}) collective-permute-start(bf16[1,512,768]{2,1,0:T(8,128)(2,1)} %dynamic-slice_bitcast_fusion.5), channel_id=1, source_target_pairs={{0,1},{1,0},{2,3},{3,2},{4,5},{5,4},{6,7},{7,6},{8,9},{9,8},{10,11... | collective-permute-start | bytes 2359304 | tf_op jit(solution)/shard_map/ppermute | solution.py:302
  549.6 30.3 %collective-permute-start.10 = (bf16[512,768]{1,0:T(8,128)(2,1)S(1)}, bf16[512,768]{1,0:T(8,128)(2,1)S(1)}, u32[]{:S(2)}, u32[]{:S(2)}) collective-permute-start(bf16[512,768]{1,0:T(8,128)(2,1)S(1)} %get-tuple-element.55), channel_id=1, source_target_pairs={{2,0},{4,2},{6,4},{0,6},{3,1},{5,3},{7,5},{1,7},{10,8},{12,10},{14... | collective-permute-start | bytes 2359304 | tf_op jit(solution)/shard_map/ppermute | solution.py:243
  552.4 46.2 %collective-permute-start.11 = (bf16[512,768]{1,0:T(8,128)(2,1)S(1)}, bf16[512,768]{1,0:T(8,128)(2,1)S(1)}, u32[]{:S(2)}, u32[]{:S(2)}) collective-permute-start(bf16[512,768]{1,0:T(8,128)(2,1)S(1)} %get-tuple-element.56), channel_id=1, source_target_pairs={{0,2},{2,4},{4,6},{6,0},{1,3},{3,5},{5,7},{7,1},{8,10},{10,12},{12... | collective-permute-start | bytes 2359304 | tf_op jit(solution)/shard_map/ppermute | solution.py:243
  639.1 13.4 %collective-permute-start.25 = (f32[768]{0:T(1024)S(1)}, f32[768]{0:T(1024)S(1)}, u32[]{:S(2)}, u32[]{:S(2)}) collective-permute-start(f32[768]{0:T(1024)S(1)} %reshape.291), channel_id=1, source_target_pairs={{0,8},{8,0},{16,24},{24,16},{1,9},{9,1},{17,25},{25,17},{2,10},{10... | collective-permute-start | bytes 9224 | tf_op jit(solution)/shard_map/ppermute | solution.py:276
  651.9 47.3 %collective-permute-start.15 = (bf16[2,2,2,2,48,512]{5,4,3,2,1,0:T(8,128)(2,1)S(1)}, bf16[2,2,2,2,48,512]{5,4,3,2,1,0:T(8,128)(2,1)S(1)}, u32[]{:S(2)}, u32[]{:S(2)}) collective-permute-start(bf16[2,2,2,2,48,512]{5,4,3,2,1,0:T(8,128)(2,1)S(1)} %dynamic-slice_bitcast_fusion.3), channel_id=1, source_target_pairs={{0,8},{8,0},{16,24},{24,16},{1,9},{9,1},{17,25},{25,17},{2,10},{10... | collective-permute-start | bytes 2359304 | tf_op jit(solution)/shard_map/ppermute | solution.py:265
  658.6 41.6 %collective-permute-start.12 = (bf16[512,768]{1,0:T(8,128)(2,1)S(1)}, bf16[512,768]{1,0:T(8,128)(2,1)S(1)}, u32[]{:S(2)}, u32[]{:S(2)}) collective-permute-start(bf16[512,768]{1,0:T(8,128)(2,1)S(1)} %copy-done.23), channel_id=1, source_target_pairs={{2,0},{4,2},{6,4},{0,6},{3,1},{5,3},{7,5},{1,7},{10,8},{12,10},{14... | collective-permute-start | bytes 2359304 | tf_op jit(solution)/shard_map/ppermute | solution.py:243
  659.2 41.0 %collective-permute-start.13 = (bf16[512,768]{1,0:T(8,128)(2,1)S(1)}, bf16[512,768]{1,0:T(8,128)(2,1)S(1)}, u32[]{:S(2)}, u32[]{:S(2)}) collective-permute-start(bf16[512,768]{1,0:T(8,128)(2,1)S(1)} %copy-done.22), channel_id=1, source_target_pairs={{0,2},{2,4},{4,6},{6,0},{1,3},{3,5},{5,7},{7,1},{8,10},{10,12},{12... | collective-permute-start | bytes 2359304 | tf_op jit(solution)/shard_map/ppermute | solution.py:243
  660.9 33.2 %collective-permute-start.28 = (f32[768]{0:T(1024)S(1)}, f32[768]{0:T(1024)S(1)}, u32[]{:S(2)}, u32[]{:S(2)}) collective-permute-start(f32[768]{0:T(1024)S(1)} %add.466), channel_id=1, source_target_pairs={{0,2},{2,0},{4,6},{6,4},{1,3},{3,1},{5,7},{7,5},{8,10},{10,8},{12,... | collective-permute-start | bytes 9224 | tf_op jit(solution)/shard_map/ppermute | solution.py:276
  701.9 16.4 %collective-permute-start.21 = (bf16[2,2,2,48,640]{4,3,2,1,0:T(8,128)(2,1)S(1)}, bf16[2,2,2,48,640]{4,3,2,1,0:T(8,128)(2,1)S(1)}, u32[]{:S(2)}, u32[]{:S(2)}) collective-permute-start(bf16[2,2,2,48,640]{4,3,2,1,0:T(8,128)(2,1)S(1)} %dynamic-slice_bitcast_fusion.7), channel_id=1, source_target_pairs={{0,16},{8,24},{16,0},{24,8},{1,17},{9,25},{17,1},{25,9},{2,18},{10... | collective-permute-start | bytes 1474568 | tf_op jit(solution)/shard_map/ppermute | solution.py:265
  710.3 27.3 %collective-permute-start.14 = (bf16[1,512,768]{2,1,0:T(8,128)(2,1)S(1)}, bf16[1,512,768]{2,1,0:T(8,128)(2,1)S(1)}, u32[]{:S(2)}, u32[]{:S(2)}) collective-permute-start(bf16[1,512,768]{2,1,0:T(8,128)(2,1)S(1)} %dynamic-slice_bitcast_fusion.4), channel_id=1, source_target_pairs={{0,1},{1,0},{2,3},{3,2},{4,5},{5,4},{6,7},{7,6},{8,9},{9,8},{10,11... | collective-permute-start | bytes 2359304 | tf_op jit(solution)/shard_map/ppermute | solution.py:302
  721.9 12.1 %collective-permute-start.19 = (bf16[48,512]{1,0:T(8,128)(2,1)S(1)}, bf16[48,512]{1,0:T(8,128)(2,1)S(1)}, u32[]{:S(2)}, u32[]{:S(2)}) collective-permute-start(bf16[48,512]{1,0:T(8,128)(2,1)S(1)} %dynamic-slice_bitcast_fusion.14), channel_id=1, source_target_pairs={{0,2},{2,0},{4,6},{6,4},{1,3},{3,1},{5,7},{7,5},{8,10},{10,8},{12,... | collective-permute-start | bytes 147464 | tf_op jit(solution)/shard_map/ppermute | solution.py:265
  (63 other events, 559.8 us)
Sparse Core Ops, SparseCore 0:
  11.4 85.2 all-gather.2
  99.5 112.3 all-gather.4
  480.1 163.7 reduce-scatter.1

commit v3 on v2

--- a/solution.py
+++ b/solution.py
@@ -4,6 +4,7 @@
 from jax.experimental import pallas as pl
 from jax.experimental.pallas import tpu as pltpu
 from jax.sharding import PartitionSpec as P
+
 
 HD = 64
 B = jnp.bfloat16
@@ -229,7 +230,7 @@
     half = block.shape[0] // 2
     first, second = block[:half], block[half:]
     pieces = []
-    for _ in range(count - 1):
+    for _ in range(1, count):
         first = lax.ppermute(first, "ctx", up)
         second = lax.ppermute(second, "ctx", down)
         pieces.append((first, second))
@@ -324,7 +325,7 @@
     return jax.nn.gelu(values, approximate=False)
 
 
-def body(
+def layer(
     tokens,
     qkv_weight,
     qv_bias,
@@ -478,7 +479,9 @@
         dq = jnp.zeros(om_t[s].shape, F)
         got = None
         for c in reversed(range(chunk_count)):
-            dq, dkv = attention_backward(q_t[s], kv_t[s][c], do_s, lse[s], delta, dq, 1024, 512)
+            dq, dkv = attention_backward(
+                q_t[s], kv_t[s][c], do_s, lse[s], delta, dq, 1024, 512
+            )
             dkv = dkv.reshape(tp_count, 2 * head_width, dkv.shape[3])
             part = sum(dot(dkv[t], w_kv[t], 0, 1) for t in range(tp_count))
             kv_grad = [kv_grad[t] + dot(x_chunks[s][c], dkv[t], 0, 1) for t in range(tp_count)]
@@ -564,4 +567,4 @@
         P(("fsdp", "ctx"), None),
         P(("fsdp", "ctx"), None),
     )
-    return jax.shard_map(body, mesh=mesh, in_specs=in_specs, out_specs=out_specs, check_vma=False)
+    return jax.shard_map(layer, mesh=mesh, in_specs=in_specs, out_specs=out_specs, check_vma=False)

time: 757 us -> 757 us (level)
  no operation moved by 1% of the time
where the time goes in v3:
time: 757 us; the launch traced here: 753 us
  Pallas kernels  221 us (29%)
  waiting for transfers between devices  200 us (26%)
  matrix products  159 us (21%)
  starting transfers between devices  66.8 us (9%)
  local copies, waits for them, and re-layouts  52.7 us (7%)
  other arithmetic  38.4 us (5%)
  between operations  15.3 us (2%)
    dot_general x42, matrix products, dot(): lax.dot_general(left, right, (((left_dim,), (right_dim,)), ((), ())), pre...  159 us
    pallas_call x4, Pallas kernels, attention_backward(): pl.pallas_call(lambda *refs: backward_kernel(*refs, bk=bk, bq=bq), grid=(...  145 us
    pallas_call x2, Pallas kernels, attention_forward(): pl.pallas_call(lambda *refs: forward_kernel(*refs, chunks=chunks, first=f...  75.5 us
    ppermute x10, waiting for transfers between devices, sum_all(): lax.ppermute(vector, axis, [(i, i ^ bit) for i in range(size)])  55.2 us
    ppermute x3, waiting for transfers between devices, ring_gather(): first = lax.ppermute(first, 'ctx', up)  54 us
    ppermute x6, waiting for transfers between devices, ring_return(): return (lax.ppermute(first, 'ctx', down), lax.ppermute(second, 'ctx', up))  35.2 us
    ppermute x3, starting transfers between devices, ring_gather(): first = lax.ppermute(first, 'ctx', up)  32.2 us
    ppermute x3, waiting for transfers between devices, ring_gather(): second = lax.ppermute(second, 'ctx', down)  29.2 us
  transfers between devices with their start and end apart: 38, of which 18 were waited for; matrix products, arithmetic and copies ran while one was open for 13% of the time, Pallas kernels for 20%

profile of v3, /device:TPU:0, one launch (start us, length us, event | category | flops | bytes accessed | tf_op | source)
XLA Modules:
  0.0 752.5 jit_solution(14669324924144051604)
XLA Ops:
  19.9 21.2 %collective-permute-done.1 = bf16[512,768]{1,0:T(8,128)(2,1)} collective-permute-done((bf16[512,768]{1,0:T(8,128)(2,1)S(1)}, bf16[512,768]{1,0:T(8,128)(2,1)}, u32[]{:S(2)}, u32[]{:S(2)}) %collective-permute-start.1) | collective-permute-done | bytes 786464 | tf_op jit(solution)/shard_map/ppermute | solution.py:234
  41.1 10.3 %collective-permute-start.2 = (bf16[512,768]{1,0:T(8,128)(2,1)}, bf16[512,768]{1,0:T(8,128)(2,1)}, u32[]{:S(2)}, u32[]{:S(2)}) collective-permute-start(bf16[512,768]{1,0:T(8,128)(2,1)} %collective-permute-done.1), channel_id=1, source_target_pairs={{0,2},{2,4},{4,6},{6,0},{1,3},{3,5},{5,7},{7,1},{8,10},{10,12},{12... | collective-permute-start | bytes 2359304 | tf_op jit(solution)/shard_map/ppermute | solution.py:234
  54.6 10.2 %collective-permute-done.3 = bf16[512,768]{1,0:T(8,128)(2,1)} collective-permute-done((bf16[512,768]{1,0:T(8,128)(2,1)}, bf16[512,768]{1,0:T(8,128)(2,1)}, u32[]{:S(2)}, u32[]{:S(2)}) %collective-permute-start.3) | collective-permute-done | bytes 786464 | tf_op jit(solution)/shard_map/ppermute | solution.py:235
  68.5 17.5 %collective-permute-done.2 = bf16[512,768]{1,0:T(8,128)(2,1)} collective-permute-done((bf16[512,768]{1,0:T(8,128)(2,1)}, bf16[512,768]{1,0:T(8,128)(2,1)}, u32[]{:S(2)}, u32[]{:S(2)}) %collective-permute-start.2) | collective-permute-done | bytes 786464 | tf_op jit(solution)/shard_map/ppermute | solution.py:234
  86.0 18.8 %collective-permute-start.5 = (bf16[512,768]{1,0:T(8,128)(2,1)}, bf16[512,768]{1,0:T(8,128)(2,1)S(1)}, u32[]{:S(2)}, u32[]{:S(2)}) collective-permute-start(bf16[512,768]{1,0:T(8,128)(2,1)} %collective-permute-done.2), channel_id=1, source_target_pairs={{0,2},{2,4},{4,6},{6,0},{1,3},{3,5},{5,7},{7,1},{8,10},{10,12},{12... | collective-permute-start | bytes 2359304 | tf_op jit(solution)/shard_map/ppermute | solution.py:234
  114.7 15.3 %collective-permute-done.5 = bf16[512,768]{1,0:T(8,128)(2,1)S(1)} collective-permute-done((bf16[512,768]{1,0:T(8,128)(2,1)}, bf16[512,768]{1,0:T(8,128)(2,1)S(1)}, u32[]{:S(2)}, u32[]{:S(2)}) %collective-permute-start.5) | collective-permute-done | bytes 786464 | tf_op jit(solution)/shard_map/ppermute | solution.py:234
  130.9 16.4 %collective-permute-done.6 = bf16[512,768]{1,0:T(8,128)(2,1)S(1)} collective-permute-done((bf16[512,768]{1,0:T(8,128)(2,1)}, bf16[512,768]{1,0:T(8,128)(2,1)S(1)}, u32[]{:S(2)}, u32[]{:S(2)}) %collective-permute-start.6) | collective-permute-done | bytes 786464 | tf_op jit(solution)/shard_map/ppermute | solution.py:235
  161.3 5.7 add_convert_fusion.4
  171.3 34.5 %attn_forward.2 = (f32[2,384,1024]{2,1,0:T(8,128)}, f32[2,6,2,1024]{3,2,1,0:T(2,128)}) custom-call(bf16[2,384,1024]{2,1,0:T(8,128)(2,1)} %add_convert_fusion.9.refs_0_, bf16[2,2,384,1024]{3,2,1,0:T(8,128)(2,1)} %bitcast.358, bf16[2,2,384,1024]{3,2,1,0:T(8,128)(2,1)} %bitcast.360), custom_call_target="tpu_custom_call" | custom-call | flops 25769803776 | bytes 16777216 | tf_op jit(solution)/shard_map/attn_forward/pallas_call | solution.py:101
  205.7 41.1 %attn_forward.3 = (f32[2,384,1024]{2,1,0:T(8,128)}, f32[2,6,1,1024]{3,2,1,0:T(1,128)}) custom-call(bf16[2,384,1024]{2,1,0:T(8,128)(2,1)} %add_convert_fusion.9.refs_0_, bf16[2,2,384,1024]{3,2,1,0:T(8,128)(2,1)} %bitcast.362, bf16[2,2,384,1024]{3,2,1,0:T(8,128)(2,1)} %bitcast.364, f32[2,384,1024]{2,1,0:T(8,128)} %get-tuple-element.39.refs_3_, ...), custom_call_target="tpu_custom_call" | custom-call | flops 25769803776 | bytes 16777216 | tf_op jit(solution)/shard_map/attn_forward/pallas_call | solution.py:101
  258.0 16.9 %multiply_convert_fusion.1 = (bf16[1024,1536]{1,0:T(8,128)(2,1)S(1)}, f32[1024,1536]{1,0:T(8,128)}, f32[1024,1536]{1,0:T(8,128)}) fusion(f32[1536]{0:T(1024)S(1)} %get-tuple-element.112, bf16[1024,768]{1,0:T(8,128)(2,1)S(1)} %fusion.21, bf16[2,768,3456]{2,1,0:T(8,128)(2,1)S(1)} %bitcast.353), kind=kOutput, calls=%fused_computation.22 | convolution fusion | flops 2519728128 | bytes 19668992 | tf_op jit(solution)/shard_map/dot_general | solution.py:19
  277.6 17.2 %multiply_convert_fusion = (bf16[1024,1536]{1,0:T(8,128)(2,1)S(1)}, f32[1024,1536]{1,0:T(8,128)}, f32[1024,1536]{1,0:T(8,128)}) fusion(f32[1536]{0:T(1024)S(1)} %get-tuple-element.111, bf16[1024,768]{1,0:T(8,128)(2,1)S(1)} %fusion.21, bf16[2,768,3456]{2,1,0:T(8,128)(2,1)S(1)} %bitcast.355), kind=kOutput, calls=%fused_computation.9 | convolution fusion | flops 2519728128 | bytes 19668992 | tf_op jit(solution)/shard_map/dot_general | solution.py:19
  305.3 7.9 %convert_reduce_fusion.1 = (f32[1536]{0:T(1024)}, bf16[1024,1536]{1,0:T(8,128)(2,1)S(1)}) fusion(f32[1024,1536]{1,0:T(8,128)S(1)} %bitcast.367, bf16[1024,768]{1,0:T(8,128)(2,1)S(1)} %get-tuple-element.116, bf16[2,768,3456]{2,1,0:T(8,128)(2,1)} %bitcast.346, f32[1024,1536]{1,0:T(8,128)} %get-tuple-element.149, f32[1536]{0:T(1024)S(1)} %get-tuple-element.112), kind=kOutput, calls=%fused_computation.6 | convolution fusion | flops 2442656256 | bytes 19673088 | tf_op jit(solution)/shard_map/dot_general | solution.py:19
  324.6 9.0 %convert_reduce_fusion = (f32[1536]{0:T(1024)}, bf16[1024,1536]{1,0:T(8,128)(2,1)S(1)}) fusion(f32[1024,1536]{1,0:T(8,128)} %get-tuple-element.121, bf16[1024,768]{1,0:T(8,128)(2,1)S(1)} %get-tuple-element.116, bf16[2,768,3456]{2,1,0:T(8,128)(2,1)} %bitcast.348, f32[1024,1536]{1,0:T(8,128)} %get-tuple-element.150, f32[1536]{0:T(1024)S(1)} %get-tuple-element.111), kind=kOutput, calls=%fused_computation.5 | convolution fusion | flops 2442656256 | bytes 19673088 | tf_op jit(solution)/shard_map/dot_general | solution.py:19
  333.5 6.3 multiply_reduce_fusion
  369.6 36.1 %attn_backward.4 = (f32[2,384,1024]{2,1,0:T(8,128)}, bf16[2,2,384,1024]{3,2,1,0:T(8,128)(2,1)}) custom-call(bf16[2,384,1024]{2,1,0:T(8,128)(2,1)} %add_convert_fusion.9.refs_0_, bf16[2,2,384,1024]{3,2,1,0:T(8,128)(2,1)} %bitcast.365, bf16[2,384,1024]{2,1,0:T(8,128)(2,1)} %convolution_convert_fusion.4.refs_2_, ...), custom_call_target="tpu_custom_call", output_to_operand_aliasing={{0}: (5, {})} | custom-call | flops 25769803776 | bytes 16777216 | tf_op jit(solution)/shard_map/attn_backward/pallas_call | solution.py:199
  420.9 36.3 %attn_backward.5 = (f32[2,384,1024]{2,1,0:T(8,128)}, bf16[2,2,384,1024]{3,2,1,0:T(8,128)(2,1)}) custom-call(bf16[2,384,1024]{2,1,0:T(8,128)(2,1)} %add_convert_fusion.9.refs_0_, bf16[2,2,384,1024]{3,2,1,0:T(8,128)(2,1)} %bitcast.363, bf16[2,384,1024]{2,1,0:T(8,128)(2,1)} %convolution_convert_fusion.4.refs_2_, ...), custom_call_target="tpu_custom_call", output_to_operand_aliasing={{0}: (5, {})} | custom-call | flops 25769803776 | bytes 16777216 | tf_op jit(solution)/shard_map/attn_backward/pallas_call | solution.py:199
  482.7 17.3 %collective-permute-done.33 = f32[8448]{0:T(1024)S(1)} collective-permute-done((f32[8448]{0:T(1024)S(1)}, f32[8448]{0:T(1024)S(1)}, u32[]{:S(2)}, u32[]{:S(2)}) %collective-permute-start.33) | collective-permute-done | bytes 33824 | tf_op jit(solution)/shard_map/ppermute | solution.py:277
  510.9 36.4 %attn_backward.6 = (f32[2,384,1024]{2,1,0:T(8,128)}, bf16[2,2,384,1024]{3,2,1,0:T(8,128)(2,1)}) custom-call(bf16[2,384,1024]{2,1,0:T(8,128)(2,1)} %add_convert_fusion.9.refs_0_, bf16[2,2,384,1024]{3,2,1,0:T(8,128)(2,1)} %bitcast.361, bf16[2,384,1024]{2,1,0:T(8,128)(2,1)} %convolution_convert_fusion.4.refs_2_, ...), custom_call_target="tpu_custom_call", output_to_operand_aliasing={{0}: (5, {})} | custom-call | flops 25769803776 | bytes 16777216 | tf_op jit(solution)/shard_map/attn_backward/pallas_call | solution.py:199
  563.5 16.5 %collective-permute-done.10 = bf16[512,768]{1,0:T(8,128)(2,1)S(1)} collective-permute-done((bf16[512,768]{1,0:T(8,128)(2,1)S(1)}, bf16[512,768]{1,0:T(8,128)(2,1)S(1)}, u32[]{:S(2)}, u32[]{:S(2)}) %collective-permute-start.10) | collective-permute-done | bytes 786464 | tf_op jit(solution)/shard_map/ppermute | solution.py:244
  580.0 18.7 %collective-permute-done.11 = bf16[512,768]{1,0:T(8,128)(2,1)S(1)} collective-permute-done((bf16[512,768]{1,0:T(8,128)(2,1)S(1)}, bf16[512,768]{1,0:T(8,128)(2,1)S(1)}, u32[]{:S(2)}, u32[]{:S(2)}) %collective-permute-start.11) | collective-permute-done | bytes 786464 | tf_op jit(solution)/shard_map/ppermute | solution.py:244
  600.3 36.5 %attn_backward.7 = (f32[2,384,1024]{2,1,0:T(8,128)}, bf16[2,2,384,1024]{3,2,1,0:T(8,128)(2,1)}) custom-call(bf16[2,384,1024]{2,1,0:T(8,128)(2,1)} %add_convert_fusion.9.refs_0_, bf16[2,2,384,1024]{3,2,1,0:T(8,128)(2,1)} %bitcast.359, bf16[2,384,1024]{2,1,0:T(8,128)(2,1)} %convolution_convert_fusion.4.refs_2_, ...), custom_call_target="tpu_custom_call", output_to_operand_aliasing={{0}: (5, {})} | custom-call | flops 25769803776 | bytes 16777216 | tf_op jit(solution)/shard_map/attn_backward/pallas_call | solution.py:199
  661.1 32.9 %collective-permute-done.28 = f32[768]{0:T(1024)S(1)} collective-permute-done((f32[768]{0:T(1024)S(1)}, f32[768]{0:T(1024)S(1)}, u32[]{:S(2)}, u32[]{:S(2)}) %collective-permute-start.28) | collective-permute-done | bytes 3104 | tf_op jit(solution)/shard_map/ppermute | solution.py:277
  722.5 7.0 collective-permute-done.22
  (338 shorter events, 251.4 us)
Async XLA Ops:
  7.2 141.1 %all-gather.3.cloned.1.call-start = ((), (), s32[]{:S(2)}) async-start(), calls=%async_computation.1 | async-start | bytes 4055040 | tf_op jit(solution)/shard_map/all_gather | solution.py:362
  10.6 240.7 %all-gather.5.cloned.1.call-start = ((), (), s32[]{:S(2)}) async-start(), calls=%async_computation.2 | async-start | bytes 10948608 | tf_op jit(solution)/shard_map/all_gather | solution.py:366
  12.4 730.1 %reduce-scatter.2.cloned.1.call-start = ((), (), s32[]{:S(2)}) async-start(), calls=%async_computation.3 | async-start | bytes 10948608 | tf_op jit(solution)/shard_map/reduce_scatter | solution.py:455
  14.9 26.2 %collective-permute-start.1 = (bf16[512,768]{1,0:T(8,128)(2,1)S(1)}, bf16[512,768]{1,0:T(8,128)(2,1)}, u32[]{:S(2)}, u32[]{:S(2)}) collective-permute-start(bf16[512,768]{1,0:T(8,128)(2,1)S(1)} %get-tuple-element.138), channel_id=1, source_target_pairs={{0,2},{2,4},{4,6},{6,0},{1,3},{3,5},{5,7},{7,1},{8,10},{10,12},{12... | collective-permute-start | bytes 2359304 | tf_op jit(solution)/shard_map/ppermute | solution.py:234
  17.9 46.9 %collective-permute-start.3 = (bf16[512,768]{1,0:T(8,128)(2,1)}, bf16[512,768]{1,0:T(8,128)(2,1)}, u32[]{:S(2)}, u32[]{:S(2)}) collective-permute-start(bf16[512,768]{1,0:T(8,128)(2,1)} %get-tuple-element.137), channel_id=1, source_target_pairs={{2,0},{4,2},{6,4},{0,6},{3,1},{5,3},{7,5},{1,7},{10,8},{12,10},{14... | collective-permute-start | bytes 2359304 | tf_op jit(solution)/shard_map/ppermute | solution.py:235
  41.1 44.9 %collective-permute-start.2 = (bf16[512,768]{1,0:T(8,128)(2,1)}, bf16[512,768]{1,0:T(8,128)(2,1)}, u32[]{:S(2)}, u32[]{:S(2)}) collective-permute-start(bf16[512,768]{1,0:T(8,128)(2,1)} %collective-permute-done.1), channel_id=1, source_target_pairs={{0,2},{2,4},{4,6},{6,0},{1,3},{3,5},{5,7},{7,1},{8,10},{10,12},{12... | collective-permute-start | bytes 2359304 | tf_op jit(solution)/shard_map/ppermute | solution.py:234
  51.9 16.5 %collective-permute-start = (bf16[2304]{0:T(1024)(128)(2,1)S(1)}, bf16[2304]{0:T(1024)(128)(2,1)S(1)}, u32[]{:S(2)}, u32[]{:S(2)}) collective-permute-start(bf16[2304]{0:T(1024)(128)(2,1)S(1)} %dynamic-update-slice.16), channel_id=1, source_target_pairs={{0,1},{1,0},{2,3},{3,2},{4,5},{5,4},{6,7},{7,6},{8,9},{9,8},{10,11... | collective-permute-start | bytes 13832 | tf_op jit(solution)/shard_map/ppermute | solution.py:288
  64.8 42.7 %collective-permute-start.4 = (bf16[512,768]{1,0:T(8,128)(2,1)}, bf16[512,768]{1,0:T(8,128)(2,1)}, u32[]{:S(2)}, u32[]{:S(2)}) collective-permute-start(bf16[512,768]{1,0:T(8,128)(2,1)} %collective-permute-done.3), channel_id=1, source_target_pairs={{2,0},{4,2},{6,4},{0,6},{3,1},{5,3},{7,5},{1,7},{10,8},{12,10},{14... | collective-permute-start | bytes 2359304 | tf_op jit(solution)/shard_map/ppermute | solution.py:235
  86.0 44.0 %collective-permute-start.5 = (bf16[512,768]{1,0:T(8,128)(2,1)}, bf16[512,768]{1,0:T(8,128)(2,1)S(1)}, u32[]{:S(2)}, u32[]{:S(2)}) collective-permute-start(bf16[512,768]{1,0:T(8,128)(2,1)} %collective-permute-done.2), channel_id=1, source_target_pairs={{0,2},{2,4},{4,6},{6,0},{1,3},{3,5},{5,7},{7,1},{8,10},{10,12},{12... | collective-permute-start | bytes 2359304 | tf_op jit(solution)/shard_map/ppermute | solution.py:234
  107.4 39.9 %collective-permute-start.6 = (bf16[512,768]{1,0:T(8,128)(2,1)}, bf16[512,768]{1,0:T(8,128)(2,1)S(1)}, u32[]{:S(2)}, u32[]{:S(2)}) collective-permute-start(bf16[512,768]{1,0:T(8,128)(2,1)} %collective-permute-done.4), channel_id=1, source_target_pairs={{2,0},{4,2},{6,4},{0,6},{3,1},{5,3},{7,5},{1,7},{10,8},{12,10},{14... | collective-permute-start | bytes 2359304 | tf_op jit(solution)/shard_map/ppermute | solution.py:235
  462.5 45.5 %collective-permute-start.8 = (bf16[512,768]{1,0:T(8,128)(2,1)}, bf16[512,768]{1,0:T(8,128)(2,1)}, u32[]{:S(2)}, u32[]{:S(2)}) collective-permute-start(bf16[512,768]{1,0:T(8,128)(2,1)} %get-tuple-element.48), channel_id=1, source_target_pairs={{2,0},{4,2},{6,4},{0,6},{3,1},{5,3},{7,5},{1,7},{10,8},{12,10},{14... | collective-permute-start | bytes 2359304 | tf_op jit(solution)/shard_map/ppermute | solution.py:244
  465.2 42.8 %collective-permute-start.9 = (bf16[512,768]{1,0:T(8,128)(2,1)}, bf16[512,768]{1,0:T(8,128)(2,1)}, u32[]{:S(2)}, u32[]{:S(2)}) collective-permute-start(bf16[512,768]{1,0:T(8,128)(2,1)} %get-tuple-element.49), channel_id=1, source_target_pairs={{0,2},{2,4},{4,6},{6,0},{1,3},{3,5},{5,7},{7,1},{8,10},{10,12},{12... | collective-permute-start | bytes 2359304 | tf_op jit(solution)/shard_map/ppermute | solution.py:244
  480.0 20.0 %collective-permute-start.33 = (f32[8448]{0:T(1024)S(1)}, f32[8448]{0:T(1024)S(1)}, u32[]{:S(2)}, u32[]{:S(2)}) collective-permute-start(f32[8448]{0:T(1024)S(1)} %add.472), channel_id=1, source_target_pairs={{0,2},{2,0},{4,6},{6,4},{1,3},{3,1},{5,7},{7,5},{8,10},{10,8},{12,... | collective-permute-start | bytes 101384 | tf_op jit(solution)/shard_map/ppermute | solution.py:277
  482.2 76.8 %collective-permute-start.7 = (bf16[1,512,768]{2,1,0:T(8,128)(2,1)}, bf16[1,512,768]{2,1,0:T(8,128)(2,1)S(1)}, u32[]{:S(2)}, u32[]{:S(2)}) collective-permute-start(bf16[1,512,768]{2,1,0:T(8,128)(2,1)} %dynamic-slice_bitcast_fusion.5), channel_id=1, source_target_pairs={{0,1},{1,0},{2,3},{3,2},{4,5},{5,4},{6,7},{7,6},{8,9},{9,8},{10,11... | collective-permute-start | bytes 2359304 | tf_op jit(solution)/shard_map/ppermute | solution.py:303
  549.6 30.3 %collective-permute-start.10 = (bf16[512,768]{1,0:T(8,128)(2,1)S(1)}, bf16[512,768]{1,0:T(8,128)(2,1)S(1)}, u32[]{:S(2)}, u32[]{:S(2)}) collective-permute-start(bf16[512,768]{1,0:T(8,128)(2,1)S(1)} %get-tuple-element.55), channel_id=1, source_target_pairs={{2,0},{4,2},{6,4},{0,6},{3,1},{5,3},{7,5},{1,7},{10,8},{12,10},{14... | collective-permute-start | bytes 2359304 | tf_op jit(solution)/shard_map/ppermute | solution.py:244
  552.4 46.2 %collective-permute-start.11 = (bf16[512,768]{1,0:T(8,128)(2,1)S(1)}, bf16[512,768]{1,0:T(8,128)(2,1)S(1)}, u32[]{:S(2)}, u32[]{:S(2)}) collective-permute-start(bf16[512,768]{1,0:T(8,128)(2,1)S(1)} %get-tuple-element.56), channel_id=1, source_target_pairs={{0,2},{2,4},{4,6},{6,0},{1,3},{3,5},{5,7},{7,1},{8,10},{10,12},{12... | collective-permute-start | bytes 2359304 | tf_op jit(solution)/shard_map/ppermute | solution.py:244
  639.1 13.4 %collective-permute-start.25 = (f32[768]{0:T(1024)S(1)}, f32[768]{0:T(1024)S(1)}, u32[]{:S(2)}, u32[]{:S(2)}) collective-permute-start(f32[768]{0:T(1024)S(1)} %reshape.291), channel_id=1, source_target_pairs={{0,8},{8,0},{16,24},{24,16},{1,9},{9,1},{17,25},{25,17},{2,10},{10... | collective-permute-start | bytes 9224 | tf_op jit(solution)/shard_map/ppermute | solution.py:277
  651.9 47.3 %collective-permute-start.15 = (bf16[2,2,2,2,48,512]{5,4,3,2,1,0:T(8,128)(2,1)S(1)}, bf16[2,2,2,2,48,512]{5,4,3,2,1,0:T(8,128)(2,1)S(1)}, u32[]{:S(2)}, u32[]{:S(2)}) collective-permute-start(bf16[2,2,2,2,48,512]{5,4,3,2,1,0:T(8,128)(2,1)S(1)} %dynamic-slice_bitcast_fusion.3), channel_id=1, source_target_pairs={{0,8},{8,0},{16,24},{24,16},{1,9},{9,1},{17,25},{25,17},{2,10},{10... | collective-permute-start | bytes 2359304 | tf_op jit(solution)/shard_map/ppermute | solution.py:266
  658.6 41.6 %collective-permute-start.12 = (bf16[512,768]{1,0:T(8,128)(2,1)S(1)}, bf16[512,768]{1,0:T(8,128)(2,1)S(1)}, u32[]{:S(2)}, u32[]{:S(2)}) collective-permute-start(bf16[512,768]{1,0:T(8,128)(2,1)S(1)} %copy-done.23), channel_id=1, source_target_pairs={{2,0},{4,2},{6,4},{0,6},{3,1},{5,3},{7,5},{1,7},{10,8},{12,10},{14... | collective-permute-start | bytes 2359304 | tf_op jit(solution)/shard_map/ppermute | solution.py:244
  659.2 41.0 %collective-permute-start.13 = (bf16[512,768]{1,0:T(8,128)(2,1)S(1)}, bf16[512,768]{1,0:T(8,128)(2,1)S(1)}, u32[]{:S(2)}, u32[]{:S(2)}) collective-permute-start(bf16[512,768]{1,0:T(8,128)(2,1)S(1)} %copy-done.22), channel_id=1, source_target_pairs={{0,2},{2,4},{4,6},{6,0},{1,3},{3,5},{5,7},{7,1},{8,10},{10,12},{12... | collective-permute-start | bytes 2359304 | tf_op jit(solution)/shard_map/ppermute | solution.py:244
  660.9 33.2 %collective-permute-start.28 = (f32[768]{0:T(1024)S(1)}, f32[768]{0:T(1024)S(1)}, u32[]{:S(2)}, u32[]{:S(2)}) collective-permute-start(f32[768]{0:T(1024)S(1)} %add.466), channel_id=1, source_target_pairs={{0,2},{2,0},{4,6},{6,4},{1,3},{3,1},{5,7},{7,5},{8,10},{10,8},{12,... | collective-permute-start | bytes 9224 | tf_op jit(solution)/shard_map/ppermute | solution.py:277
  701.9 16.4 %collective-permute-start.21 = (bf16[2,2,2,48,640]{4,3,2,1,0:T(8,128)(2,1)S(1)}, bf16[2,2,2,48,640]{4,3,2,1,0:T(8,128)(2,1)S(1)}, u32[]{:S(2)}, u32[]{:S(2)}) collective-permute-start(bf16[2,2,2,48,640]{4,3,2,1,0:T(8,128)(2,1)S(1)} %dynamic-slice_bitcast_fusion.7), channel_id=1, source_target_pairs={{0,16},{8,24},{16,0},{24,8},{1,17},{9,25},{17,1},{25,9},{2,18},{10... | collective-permute-start | bytes 1474568 | tf_op jit(solution)/shard_map/ppermute | solution.py:266
  710.3 27.3 %collective-permute-start.14 = (bf16[1,512,768]{2,1,0:T(8,128)(2,1)S(1)}, bf16[1,512,768]{2,1,0:T(8,128)(2,1)S(1)}, u32[]{:S(2)}, u32[]{:S(2)}) collective-permute-start(bf16[1,512,768]{2,1,0:T(8,128)(2,1)S(1)} %dynamic-slice_bitcast_fusion.4), channel_id=1, source_target_pairs={{0,1},{1,0},{2,3},{3,2},{4,5},{5,4},{6,7},{7,6},{8,9},{9,8},{10,11... | collective-permute-start | bytes 2359304 | tf_op jit(solution)/shard_map/ppermute | solution.py:303
  721.9 12.1 %collective-permute-start.19 = (bf16[48,512]{1,0:T(8,128)(2,1)S(1)}, bf16[48,512]{1,0:T(8,128)(2,1)S(1)}, u32[]{:S(2)}, u32[]{:S(2)}) collective-permute-start(bf16[48,512]{1,0:T(8,128)(2,1)S(1)} %dynamic-slice_bitcast_fusion.14), channel_id=1, source_target_pairs={{0,2},{2,0},{4,6},{6,4},{1,3},{3,1},{5,7},{7,5},{8,10},{10,8},{12,... | collective-permute-start | bytes 147464 | tf_op jit(solution)/shard_map/ppermute | solution.py:266
  (63 other events, 559.8 us)
Sparse Core Ops, SparseCore 0:
  11.4 85.2 all-gather.2
  99.5 112.3 all-gather.4
  480.1 163.7 reduce-scatter.1

commit v4 on v3

--- a/solution.py
+++ b/solution.py
@@ -43,7 +43,8 @@
     if not first:
         o_in, stat_in = refs[at : at + 2]
         at += 2
-    o_ref, stat_ref, qx, kx, vx = refs[at:]
+    o_ref, stat_ref = refs[at : at + 2]
+    qx, kx, vx = refs[-3:]
     rows = q_ref.shape[-1]
     keys = kx.shape[-1]
     scaled = q_ref[0].astype(F) * (score_scale * LOG2E)
@@ -78,7 +79,9 @@
         start = (stat_in[0, 0, 0:1, :], o_in[0], stat_in[0, 0, 1:2, :])
     row_max, mixed, total = lax.fori_loop(0, keys // bk, step, start)
     if last:
-        o_ref[0] = mixed / total
+        mixed = mixed / total
+        o_ref[0] = mixed
+        refs[-4][0] = mixed.astype(B)
         stat_ref[0, 0] = row_max + jnp.log2(total)
     else:
         o_ref[0] = mixed
@@ -102,11 +105,12 @@
         lambda *refs: forward_kernel(*refs, chunks=chunks, first=first, last=last, bk=bk),
         grid=(parts, heads),
         in_specs=[row_spec] + [key_spec] * chunks + ([] if first else [row_spec, two_spec]),
-        out_specs=[row_spec, one_spec if last else two_spec],
+        out_specs=[row_spec, one_spec, row_spec] if last else [row_spec, two_spec],
         out_shape=[
             jax.ShapeDtypeStruct((parts, width, rows), F),
             jax.ShapeDtypeStruct((parts, heads, 1 if last else 2, rows), F),
-        ],
+        ]
+        + ([jax.ShapeDtypeStruct((parts, width, rows), B)] if last else []),
         scratch_shapes=[
             pltpu.VMEM((2 * HD, rows), B),
             pltpu.VMEM((2 * HD, keys * chunks), B),
@@ -122,24 +126,9 @@
     )(q_t, *kv_list, *(() if first else state))
 
 
-def backward_kernel(
-    q_ref,
-    kv_ref,
-    do_ref,
-    lse_ref,
-    delta_ref,
-    dq_in,
-    dq_ref,
-    dkv_ref,
-    qx,
-    kx,
-    dx,
-    vx,
-    dq_acc,
-    *,
-    bk,
-    bq,
-):
+def backward_kernel(*refs, first, bk, bq):
+    q_ref, kv_ref, do_ref, lse_ref, om_ref = refs[:5]
+    dq_ref, dkv_ref, qx, kx, dx, vx, dq_acc = refs[-7:]
     rows = q_ref.shape[-1]
     keys = kv_ref.shape[-1]
     scaled = q_ref[0].astype(F) * (score_scale * LOG2E)
@@ -156,7 +145,8 @@
     qx[HD : 2 * HD, :] = rest
     qx[2 * HD : 2 * HD + 16, :] = stacked(lse_ref[0, 0])
     dx[0:HD, :] = do_ref[0]
-    dx[HD : HD + 16, :] = stacked(delta_ref[0, 0])
+    delta = jnp.sum(om_ref[0] * do_ref[0].astype(F), axis=0, keepdims=True)
+    dx[HD : HD + 16, :] = stacked(delta)
     kx[0:HD, :] = kv_ref[0, 0]
     kx[HD : 2 * HD, :] = kv_ref[0, 0]
     kx[2 * HD : 2 * HD + 16, :] = jnp.full((16, keys), -1.0, B)
@@ -183,26 +173,31 @@
         return carry
 
     lax.fori_loop(0, keys // bk, step, 0)
-    dq_ref[0] = dq_in[0] + jnp.transpose(dq_acc[...] * score_scale)
-
-
-def attention_backward(q_t, kv_t, do_t, lse, delta, dq_t, bk, bq):
+    total = jnp.transpose(dq_acc[...] * score_scale)
+    if not first:
+        total = total + refs[5][0]
+    dq_ref[0] = total.astype(dq_ref.dtype)
+
+
+def attention_backward(q_t, kv_t, do_t, lse, om_t, dq_t, last, bk, bq):
     parts, width, rows = q_t.shape
     keys = kv_t.shape[3]
     heads = width // HD
     bk = pick_block(keys, bk)
     bq = pick_block(rows, bq)
+    first = dq_t is None
     total = parts * heads * rows * keys
     row_spec = pl.BlockSpec((1, HD, rows), lambda t, h: (t, h, 0))
     stat_spec = pl.BlockSpec((1, 1, 1, rows), lambda t, h: (t, h, 0, 0))
     key_spec = pl.BlockSpec((1, 2, HD, keys), lambda t, h: (t, 0, h, 0))
     return pl.pallas_call(
-        lambda *refs: backward_kernel(*refs, bk=bk, bq=bq),
+        lambda *refs: backward_kernel(*refs, first=first, bk=bk, bq=bq),
         grid=(parts, heads),
-        in_specs=[row_spec, key_spec, row_spec, stat_spec, stat_spec, row_spec],
+        in_specs=[row_spec, key_spec, row_spec, stat_spec, row_spec]
+        + ([] if first else [row_spec]),
         out_specs=[row_spec, key_spec],
         out_shape=[
-            jax.ShapeDtypeStruct((parts, width, rows), F),
+            jax.ShapeDtypeStruct((parts, width, rows), B if last else F),
             jax.ShapeDtypeStruct((parts, 2, width, keys), B),
         ],
         scratch_shapes=[
@@ -218,9 +213,161 @@
         cost_estimate=pl.CostEstimate(
             flops=2048 * total, transcendentals=total, bytes_accessed=16 << 20
         ),
-        input_output_aliases={5: 0},
         name="attn_backward",
-    )(q_t, kv_t, do_t, lse, delta, dq_t)
+    )(q_t, kv_t, do_t, lse, om_t, *([] if first else [dq_t]))
+
+
+def gelu_both(u):
+    z = jnp.abs(u) * 0.7071067811865476
+    t = 1.0 / (1.0 + 0.5 * z)
+    series = 0.17087277
+    for c in (
+        -0.82215223,
+        1.48851587,
+        -1.13520398,
+        0.27886807,
+        -0.18628806,
+        0.09678418,
+        0.37409196,
+        1.00002368,
+        -1.26551223,
+    ):
+        series = series * t + c
+    bell = jnp.exp(u * u * -0.5)
+    tail = (0.5 * t) * bell * jnp.exp(series)
+    below = jnp.where(u >= 0, 1.0 - tail, tail)
+    return u * below, below + u * (bell * 0.3989422804014327)
+
+
+def ffn_forward_kernel(y_ref, up_ref, down_ref, bias_ref, act_ref, slope_ref, out_ref, *, br):
+    start = (pl.program_id(0) == 0) & (pl.program_id(1) == 0)
+
+    @pl.when(start)
+    def _():
+        out_ref[...] = jnp.zeros_like(out_ref)
+
+    for r in range(0, y_ref.shape[0], br):
+        u = dot(y_ref[r : r + br, :], up_ref[0], 1, 0) + bias_ref[...]
+        act, slope = gelu_both(u)
+        low = act.astype(B)
+        act_ref[r : r + br, :] = low
+        slope_ref[r : r + br, :] = slope
+        out_ref[r : r + br, :] += dot(low, down_ref[0], 1, 1)
+
+
+def ffn_backward_kernel(df_ref, up_ref, down_ref, slope_ref, du_ref, sum_ref, out_ref, *, br):
+    start = (pl.program_id(0) == 0) & (pl.program_id(1) == 0)
+
+    @pl.when(start)
+    def _():
+        out_ref[...] = jnp.zeros_like(out_ref)
+
+    total = jnp.zeros(sum_ref.shape, F)
+    for r in range(0, df_ref.shape[0], br):
+        du = (dot(df_ref[r : r + br, :], down_ref[0], 1, 0) * slope_ref[r : r + br, :]).astype(B)
+        du_ref[r : r + br, :] = du
+        total = total + jnp.sum(du.astype(F), axis=0, keepdims=True)
+        out_ref[r : r + br, :] += dot(du, up_ref[0], 1, 1)
+    sum_ref[...] = total
+
+
+def ffn_specs(rows, width, weights, head_width, ff_width):
+    block = head_width
+    per = ff_width // block
+    up_spec = pl.BlockSpec((1, width, block), lambda t, j: (t, 0, 1 + j))
+    down_spec = pl.BlockSpec((1, width, block), lambda t, j: (t, 0, 1 + per + j))
+    row_spec = pl.BlockSpec((rows, width), lambda t, j: (0, 0))
+    hidden_spec = pl.BlockSpec((rows, block), lambda t, j: (0, t * per + j))
+    vector_spec = pl.BlockSpec((1, block), lambda t, j: (0, t * per + j))
+    return (weights.shape[0], per), up_spec, down_spec, row_spec, hidden_spec, vector_spec
+
+
+FFN_PARAMS = pltpu.CompilerParams(
+    vmem_limit_bytes=56 << 20, dimension_semantics=("arbitrary", "arbitrary")
+)
+
+
+def ffn_forward(y_low, weights, bias, head_width, ff_width):
+    rows, width = y_low.shape
+    grid, up_spec, down_spec, row_spec, hidden_spec, vector_spec = ffn_specs(
+        rows, width, weights, head_width, ff_width
+    )
+    hidden = grid[0] * ff_width
+    return pl.pallas_call(
+        lambda *refs: ffn_forward_kernel(*refs, br=pick_block(rows, 256)),
+        grid=grid,
+        in_specs=[row_spec, up_spec, down_spec, vector_spec],
+        out_specs=[hidden_spec, hidden_spec, row_spec],
+        out_shape=[
+            jax.ShapeDtypeStruct((rows, hidden), B),
+            jax.ShapeDtypeStruct((rows, hidden), F),
+            jax.ShapeDtypeStruct((rows, width), F),
+        ],
+        compiler_params=FFN_PARAMS,
+        name="ffn_forward",
+    )(y_low, weights, weights, bias)
+
+
+def ffn_backward(df, weights, slope, head_width, ff_width):
+    rows, width = df.shape
+    grid, up_spec, down_spec, row_spec, hidden_spec, vector_spec = ffn_specs(
+        rows, width, weights, head_width, ff_width
+    )
+    hidden = grid[0] * ff_width
+    return pl.pallas_call(
+        lambda *refs: ffn_backward_kernel(*refs, br=pick_block(rows, 256)),
+        grid=grid,
+        in_specs=[row_spec, up_spec, down_spec, hidden_spec],
+        out_specs=[hidden_spec, vector_spec, row_spec],
+        out_shape=[
+            jax.ShapeDtypeStruct((rows, hidden), B),
+            jax.ShapeDtypeStruct((1, hidden), F),
+            jax.ShapeDtypeStruct((rows, width), F),
+        ],
+        compiler_params=FFN_PARAMS,
+        name="ffn_backward",
+    )(df, weights, weights, slope)
+
+
+def weight_grad_kernel(da_ref, y_ref, df_ref, mixed_ref, du_ref, act_ref, out_ref, *, per):
+    j = pl.program_id(1)
+
+    @pl.when(j == 0)
+    def _():
+        out_ref[0] = dot(da_ref[...], mixed_ref[0], 0, 1).astype(B)
+
+    @pl.when((j > 0) & (j <= per))
+    def _():
+        out_ref[0] = dot(y_ref[...], du_ref[...], 0, 0).astype(B)
+
+    @pl.when(j > per)
+    def _():
+        out_ref[0] = dot(df_ref[...], act_ref[...], 0, 0).astype(B)
+
+
+def weight_grads(da, y_low, df, mixed_t, du, act):
+    rows, width = da.shape
+    parts, block, _ = mixed_t.shape
+    per = du.shape[1] // parts // block
+    row_spec = pl.BlockSpec((rows, width), lambda t, j: (0, 0))
+    return pl.pallas_call(
+        lambda *refs: weight_grad_kernel(*refs, per=per),
+        grid=(parts, 1 + 2 * per),
+        in_specs=[
+            row_spec,
+            row_spec,
+            row_spec,
+            pl.BlockSpec((1, block, rows), lambda t, j: (t, 0, 0)),
+            pl.BlockSpec((rows, block), lambda t, j: (0, t * per + jnp.clip(j - 1, 0, per - 1))),
+            pl.BlockSpec(
+                (rows, block), lambda t, j: (0, t * per + jnp.clip(j - 1 - per, 0, per - 1))
+            ),
+        ],
+        out_specs=pl.BlockSpec((1, width, block), lambda t, j: (t, 0, j)),
+        out_shape=jax.ShapeDtypeStruct((parts, width, block * (1 + 2 * per)), B),
+        compiler_params=FFN_PARAMS,
+        name="weight_grads",
+    )(da, y_low, df, mixed_t, du, act)
 
 
 def ring_gather(block):
@@ -270,13 +417,8 @@
 
 
 def sum_all(vector):
-    for axis in ("fsdp", "tp", "ctx"):
-        size = lax.axis_size(axis)
-        bit = 1
-        while bit < size:
-            vector = vector + lax.ppermute(vector, axis, [(i, i ^ bit) for i in range(size)])
-            bit *= 2
-    return vector
+    every = lax.all_gather(vector.reshape(-1, 128), ("fsdp", "ctx", "tp"), axis=0)
+    return jnp.sum(every, axis=0).reshape(-1)
 
 
 def tp_gather(vector):
@@ -319,10 +461,6 @@
         - jnp.mean(grad_norm, axis=-1, keepdims=True)
         - normed * jnp.mean(grad_norm * normed, axis=-1, keepdims=True)
     )
-
-
-def gelu_exact(values):
-    return jax.nn.gelu(values, approximate=False)
 
 
 def layer(
@@ -371,8 +509,6 @@
     gain1, gain2 = rows_all[0], rows_all[1]
     out_bias, shift1, down_bias, shift2 = (rows_all[2 + i] for i in range(4))
     w_out = second_all[:, :, :head_width]
-    w_up = second_all[:, :, head_width : head_width + ff_width]
-    w_down = second_all[:, :, head_width + ff_width :]
     bias_all = tp_gather(jnp.concatenate([qv_bias.reshape(-1), up_bias]))
     q_bias = bias_all[:, :head_width].astype(F)
     v_bias = bias_all[:, head_width : 2 * head_width].astype(F)
@@ -389,7 +525,7 @@
     ]
     chunk_count = len(x_chunks[0])
     near = (chunk_count + 1) // 2
-    q_t, kv_t, om_t, lse = [], [], [], []
+    q_t, kv_t, om_t, lse, mixed_s = [], [], [], [], []
     for s in range(own_seqs):
         q_s = (dot(w_q, own_tokens[s], 1, 1) + q_bias[:, :, None]).astype(B)
         kv_s = [project(block) for block in x_chunks[s][:near]]
@@ -404,7 +540,8 @@
         kv_t.append(kv_s)
         om_t.append(done[0])
         lse.append(done[1])
-    mixed_t = jnp.concatenate([one.astype(B) for one in om_t], axis=2)
+        mixed_s.append(done[2])
+    mixed_t = jnp.concatenate(mixed_s, axis=2) if own_seqs > 1 else mixed_s[0]
     attn_part = sum(dot(mixed_t[t], w_out[t], 0, 1) for t in range(tp_count))
     x_float = x_own.astype(F)
     first_out, first_norm, first_scale = norm_forward(
@@ -412,13 +549,10 @@
     )
     first_low = first_out.astype(B)
 
-    act_low, gelu_back = [], []
-    for t in range(tp_count):
-        inner = dot(first_low, w_up[t], 1, 0) + u_bias[t]
-        activated, back = jax.vjp(gelu_exact, inner)
-        act_low.append(activated.astype(B))
-        gelu_back.append(back)
-    ffn_out = sum(dot(act_low[t], w_down[t], 1, 1) for t in range(tp_count)) + down_bias
+    act_low, slope, ffn_out = ffn_forward(
+        first_low, second_all, u_bias.reshape(1, -1), head_width, ff_width
+    )
+    ffn_out = ffn_out + down_bias
     grad_final = own_cotangent.reshape(rows, width).astype(F)
     final_out, final_norm, final_scale = norm_forward(first_out + ffn_out, gain2, shift2)
     output = tp_exchange(final_out.astype(B).reshape(own_seqs, local_len, width))
@@ -427,29 +561,14 @@
     grad_second = norm_backward(grad_final, final_norm, final_scale, gain2)
     df = grad_second.astype(B)
     down_bias_grad = jnp.sum(df.astype(F), axis=0)
-    inner_low = [
-        gelu_back[t](dot(df, w_down[t], 1, 0))[0].astype(B) for t in range(tp_count)
-    ]
-    up_bias_grad = [jnp.sum(inner_low[t].astype(F), axis=0) for t in range(tp_count)]
-    first_grad = grad_second + sum(dot(inner_low[t], w_up[t], 1, 1) for t in range(tp_count))
+    inner_low, up_bias_grad, back = ffn_backward(df, second_all, slope, head_width, ff_width)
+    first_grad = grad_second + back
     gain1_grad = jnp.sum(first_grad * first_norm, axis=0)
     shift1_grad = jnp.sum(first_grad, axis=0)
     resid_grad = norm_backward(first_grad, first_norm, first_scale, gain1)
     da = resid_grad.astype(B)
     out_bias_grad = jnp.sum(da.astype(F), axis=0)
-    second_grad = jnp.stack(
-        [
-            jnp.concatenate(
-                [
-                    dot(da, mixed_t[t], 0, 1).astype(B),
-                    dot(first_low, inner_low[t], 0, 0).astype(B),
-                    dot(df, act_low[t], 0, 0).astype(B),
-                ],
-                axis=1,
-            )
-            for t in range(tp_count)
-        ]
-    )
+    second_grad = weight_grads(da, first_low, df, mixed_t, inner_low, act_low)
     do_t = dot(w_out, da, 1, 1).astype(B)
     do_t, second_grad = lax.optimization_barrier((do_t, second_grad))
     second_grad = lax.psum_scatter(
@@ -463,8 +582,7 @@
     early = sum_all(
         jnp.concatenate(
             [gain1_grad, gain2_grad, out_bias_grad, shift1_grad, down_bias_grad, shift2_grad]
-            + up_bias_grad
-            + [v_bias_grad.reshape(-1)]
+            + [up_bias_grad.reshape(-1), v_bias_grad.reshape(-1)]
         )
     )
     kv_grad = [0.0] * tp_count
@@ -474,27 +592,26 @@
     half = local_len // 2
     for s in range(own_seqs):
         do_s = do_t[:, :, s * local_len : (s + 1) * local_len]
-        delta = (om_t[s] * do_s.astype(F)).reshape(tp_count, head_width // HD, HD, local_len)
-        delta = jnp.sum(delta, axis=2, keepdims=True)
-        dq = jnp.zeros(om_t[s].shape, F)
+        dq = None
+        grads = []
         got = None
         for c in reversed(range(chunk_count)):
             dq, dkv = attention_backward(
-                q_t[s], kv_t[s][c], do_s, lse[s], delta, dq, 1024, 512
+                q_t[s], kv_t[s][c], do_s, lse[s], om_t[s], dq, c == 0, 1024, 512
             )
             dkv = dkv.reshape(tp_count, 2 * head_width, dkv.shape[3])
             part = sum(dot(dkv[t], w_kv[t], 0, 1) for t in range(tp_count))
-            kv_grad = [kv_grad[t] + dot(x_chunks[s][c], dkv[t], 0, 1) for t in range(tp_count)]
+            grads.append((c, dkv))
             if c:
                 one, two = part[:half], part[half:]
                 if got is not None:
                     one = one + got[0].astype(F)
                     two = two + got[1].astype(F)
-                one, two, dq, *kv_grad = lax.optimization_barrier(
-                    (one.astype(B), two.astype(B), dq, *kv_grad)
-                )
+                one, two, dq = lax.optimization_barrier((one.astype(B), two.astype(B), dq))
                 got = ring_return(one, two)
-        dq_low = dq.astype(B)
+        dq_low = dq
+        for c, dkv in grads:
+            kv_grad = [kv_grad[t] + dot(x_chunks[s][c], dkv[t], 0, 1) for t in range(tp_count)]
         q_bias_grad = q_bias_grad + jnp.sum(dq_low.astype(F), axis=2)
         q_grad = [q_grad[t] + dot(own_tokens[s], dq_low[t], 0, 1) for t in range(tp_count)]
         part = part + sum(dot(dq_low[t], w_q[t], 0, 1) for t in range(tp_count))

time: 757 us -> 790 us (1.044)
  matrix products: 159 us -> 74.7 us
  Pallas kernels: 221 us -> 302 us
  blocking collectives: 0 us -> 66.1 us
  starting transfers between devices: 66.8 us -> 55.8 us
  local copies, waits for them, and re-layouts: 52.7 us -> 44.6 us
    dot_general x42 -> x28, matrix products: 159 us -> 74.7 us  [dot(): lax.dot_general(left, right, (((left_dim,), (right_dim,)), ((), ())), pre...]
    pallas_call x4 -> x7, Pallas kernels: 145 us -> 226 us  [the longest x4 145 us: attention_backward(): pl.pallas_call(lambda *refs: backward_kernel(*refs, first=first, bk=bk, b...]
    all_gather x0 -> x1, blocking collectives: none -> 66.1 us  [sum_all(): lax.all_gather(vector.reshape(-1, 128), ('fsdp', 'ctx', 'tp'), axis=0)]
    ppermute x10 -> x0, waiting for transfers between devices: 55.2 us -> none  [sum_all(): lax.ppermute(vector, axis, [(i, i ^ bit) for i in range(size)])]
    ppermute x6, waiting for transfers between devices: 35.2 us -> 81.4 us  [ring_return(): return (lax.ppermute(first, 'ctx', down), lax.ppermute(second, 'ctx', up))]
    another operation x5 -> x0, other arithmetic: 9.7 us -> none  [the longest x3 8.97 us: layer(): jnp.stack([jnp.concatenate([dot(da, mixed_t[t], 0, 1).astype(B), dot(firs...]
    reduce_sum x1 -> x4, other arithmetic: 0.38 us -> 9.1 us  [the longest x1 4.82 us: layer(): gain1_grad = jnp.sum(first_grad * first_norm, axis=0)]
    unnamed x112 -> x100, local copies, waits for them, and re-layouts: 18.3 us -> 16.4 us
  transfers between devices with their start and end apart: 38 -> 29, of which waited for: 18 -> 15; matrix products, arithmetic and copies ran while one was open for 13% -> 14% of each run, Pallas kernels for 20% -> 28%
where the time goes in v4:
time: 790 us; the launch traced here: 783 us
  Pallas kernels  302 us (38%)
  waiting for transfers between devices  194 us (25%)
  matrix products  74.7 us (9%)
  blocking collectives  66.1 us (8%)
  starting transfers between devices  55.8 us (7%)
  local copies, waits for them, and re-layouts  44.6 us (6%)
  other arithmetic  31.1 us (4%)
  between operations  15.2 us (2%)
    pallas_call x4, Pallas kernels, attention_backward(): pl.pallas_call(lambda *refs: backward_kernel(*refs, first=first, bk=bk, b...  145 us
    ppermute x6, waiting for transfers between devices, ring_return(): return (lax.ppermute(first, 'ctx', down), lax.ppermute(second, 'ctx', up))  81.4 us
    pallas_call x2, Pallas kernels, attention_forward(): pl.pallas_call(lambda *refs: forward_kernel(*refs, chunks=chunks, first=f...  75.7 us
    dot_general x28, matrix products, dot(): lax.dot_general(left, right, (((left_dim,), (right_dim,)), ((), ())), pre...  74.7 us
    all_gather x1, blocking collectives, sum_all(): lax.all_gather(vector.reshape(-1, 128), ('fsdp', 'ctx', 'tp'), axis=0)  66.1 us
    ppermute x3, waiting for transfers between devices, ring_gather(): first = lax.ppermute(first, 'ctx', up)  51 us
    pallas_call x1, Pallas kernels, ffn_forward(): pl.pallas_call(lambda *refs: ffn_forward_kernel(*refs, br=pick_block(rows...  34.4 us
    ppermute x3, waiting for transfers between devices, ring_gather(): second = lax.ppermute(second, 'ctx', down)  32.6 us
  transfers between devices with their start and end apart: 29, of which 15 were waited for; matrix products, arithmetic and copies ran while one was open for 14% of the time, Pallas kernels for 28%

profile of v4, /device:TPU:0, one launch (start us, length us, event | category | flops | bytes accessed | tf_op | source)
XLA Modules:
  0.0 783.3 jit_solution(7557745005444288041)
XLA Ops:
  19.2 21.1 %collective-permute-done.1 = bf16[512,768]{1,0:T(8,128)(2,1)} collective-permute-done((bf16[512,768]{1,0:T(8,128)(2,1)S(1)}, bf16[512,768]{1,0:T(8,128)(2,1)}, u32[]{:S(2)}, u32[]{:S(2)}) %collective-permute-start.1) | collective-permute-done | bytes 786464 | tf_op jit(solution)/shard_map/ppermute | solution.py:381
  40.3 10.3 %collective-permute-start.2 = (bf16[512,768]{1,0:T(8,128)(2,1)}, bf16[512,768]{1,0:T(8,128)(2,1)}, u32[]{:S(2)}, u32[]{:S(2)}) collective-permute-start(bf16[512,768]{1,0:T(8,128)(2,1)} %collective-permute-done.1), channel_id=1, source_target_pairs={{0,2},{2,4},{4,6},{6,0},{1,3},{3,5},{5,7},{7,1},{8,10},{10,12},{12... | collective-permute-start | bytes 2359304 | tf_op jit(solution)/shard_map/ppermute | solution.py:381
  50.6 12.7 %collective-permute-done.3 = bf16[512,768]{1,0:T(8,128)(2,1)} collective-permute-done((bf16[512,768]{1,0:T(8,128)(2,1)S(1)}, bf16[512,768]{1,0:T(8,128)(2,1)}, u32[]{:S(2)}, u32[]{:S(2)}) %collective-permute-start.3) | collective-permute-done | bytes 786464 | tf_op jit(solution)/shard_map/ppermute | solution.py:382
  70.1 15.1 %collective-permute-done.2 = bf16[512,768]{1,0:T(8,128)(2,1)} collective-permute-done((bf16[512,768]{1,0:T(8,128)(2,1)}, bf16[512,768]{1,0:T(8,128)(2,1)}, u32[]{:S(2)}, u32[]{:S(2)}) %collective-permute-start.2) | collective-permute-done | bytes 786464 | tf_op jit(solution)/shard_map/ppermute | solution.py:381
  85.2 18.8 %collective-permute-start.5 = (bf16[512,768]{1,0:T(8,128)(2,1)}, bf16[512,768]{1,0:T(8,128)(2,1)S(1)}, u32[]{:S(2)}, u32[]{:S(2)}) collective-permute-start(bf16[512,768]{1,0:T(8,128)(2,1)} %collective-permute-done.2), channel_id=1, source_target_pairs={{0,2},{2,4},{4,6},{6,0},{1,3},{3,5},{5,7},{7,1},{8,10},{10,12},{12... | collective-permute-start | bytes 2359304 | tf_op jit(solution)/shard_map/ppermute | solution.py:381
  114.4 14.8 %collective-permute-done.5 = bf16[512,768]{1,0:T(8,128)(2,1)S(1)} collective-permute-done((bf16[512,768]{1,0:T(8,128)(2,1)}, bf16[512,768]{1,0:T(8,128)(2,1)S(1)}, u32[]{:S(2)}, u32[]{:S(2)}) %collective-permute-start.5) | collective-permute-done | bytes 786464 | tf_op jit(solution)/shard_map/ppermute | solution.py:381
  129.2 17.3 %collective-permute-done.6 = bf16[512,768]{1,0:T(8,128)(2,1)S(1)} collective-permute-done((bf16[512,768]{1,0:T(8,128)(2,1)}, bf16[512,768]{1,0:T(8,128)(2,1)S(1)}, u32[]{:S(2)}, u32[]{:S(2)}) %collective-permute-start.6) | collective-permute-done | bytes 786464 | tf_op jit(solution)/shard_map/ppermute | solution.py:382
  171.2 34.5 %attn_forward.2 = (f32[2,384,1024]{2,1,0:T(8,128)}, f32[2,6,2,1024]{3,2,1,0:T(2,128)}) custom-call(bf16[2,384,1024]{2,1,0:T(8,128)(2,1)} %add_convert_fusion.7.refs_0_, bf16[2,2,384,1024]{3,2,1,0:T(8,128)(2,1)} %bitcast.301, bf16[2,2,384,1024]{3,2,1,0:T(8,128)(2,1)} %bitcast.303), custom_call_target="tpu_custom_call" | custom-call | flops 25769803776 | bytes 16777216 | tf_op jit(solution)/shard_map/attn_forward/pallas_call | solution.py:104
  205.7 41.3 %attn_forward.3 = (f32[2,384,1024]{2,1,0:T(8,128)}, f32[2,6,1,1024]{3,2,1,0:T(1,128)}, bf16[2,384,1024]{2,1,0:T(8,128)(2,1)}) custom-call(bf16[2,384,1024]{2,1,0:T(8,128)(2,1)} %add_convert_fusion.7.refs_0_, bf16[2,2,384,1024]{3,2,1,0:T(8,128)(2,1)} %bitcast.305, bf16[2,2,384,1024]{3,2,1,0:T(8,128)(2,1)} %bitcast.307, ...), custom_call_target="tpu_custom_call" | custom-call | flops 25769803776 | bytes 16777216 | tf_op jit(solution)/shard_map/attn_forward/pallas_call | solution.py:104
  254.3 34.4 %ffn_forward.1 = (bf16[1024,3072]{1,0:T(8,128)(2,1)}, f32[1024,3072]{1,0:T(8,128)}, f32[1024,768]{1,0:T(8,128)}) custom-call(bf16[1024,768]{1,0:T(8,128)(2,1)} %fusion.9.refs_0_.refs_1_, bf16[2,768,3456]{2,1,0:T(8,128)(2,1)} %bitcast.239, bf16[2,768,3456]{2,1,0:T(8,128)(2,1)} %bitcast.240, f32[1,3072]{1,0:T(1,128)} %bitcast.297), custom_call_target="tpu_custom_call" | custom-call | tf_op jit(solution)/shard_map/ffn_forward/pallas_call | solution.py:296
  297.1 20.1 %ffn_backward.1 = (bf16[1024,3072]{1,0:T(8,128)(2,1)}, f32[1,3072]{1,0:T(1,128)}, f32[1024,768]{1,0:T(8,128)}) custom-call(bf16[1024,768]{1,0:T(8,128)(2,1)} %get-tuple-element.114.refs_0_.refs_2_, bf16[2,768,3456]{2,1,0:T(8,128)(2,1)} %bitcast.241, bf16[2,768,3456]{2,1,0:T(8,128)(2,1)} %bitcast.242, f32[1024,3072]{1,0:T(8,128)} %get-tuple-element.44.refs_3_), custom_call_target="tpu_custom_call" | custom-call | tf_op jit(solution)/shard_map/ffn_backward/pallas_call | solution.py:317
  327.7 26.3 %weight_grads.1 = bf16[2,768,3456]{2,1,0:T(8,128)(2,1)} custom-call(bf16[1024,768]{1,0:T(8,128)(2,1)} %copy-done.10, bf16[1024,768]{1,0:T(8,128)(2,1)} %fusion.9.refs_0_.refs_1_, bf16[1024,768]{1,0:T(8,128)(2,1)} %get-tuple-element.114.refs_0_.refs_2_, bf16[2,384,1024]{2,1,0:T(8,128)(2,1)} %get-tuple-element.42.refs_3_, ...), custom_call_target="tpu_custom_call" | custom-call | tf_op jit(solution)/shard_map/weight_grads/pallas_call | solution.py:353
  355.1 36.2 %attn_backward.4 = (f32[2,384,1024]{2,1,0:T(8,128)}, bf16[2,2,384,1024]{3,2,1,0:T(8,128)(2,1)}) custom-call(bf16[2,384,1024]{2,1,0:T(8,128)(2,1)} %add_convert_fusion.7.refs_0_, bf16[2,2,384,1024]{3,2,1,0:T(8,128)(2,1)} %bitcast.308, bf16[2,384,1024]{2,1,0:T(8,128)(2,1)} %copy-done.29, f32[2,6,1,1024]{3,2,1,0:T(1,128)} %get-tuple-element.49.refs_3_, ...), custom_call_target="tpu_custom_call" | custom-call | flops 25769803776 | bytes 16777216 | tf_op jit(solution)/shard_map/attn_backward/pallas_call | solution.py:193
  398.7 36.3 %attn_backward.5 = (f32[2,384,1024]{2,1,0:T(8,128)}, bf16[2,2,384,1024]{3,2,1,0:T(8,128)(2,1)}) custom-call(bf16[2,384,1024]{2,1,0:T(8,128)(2,1)} %add_convert_fusion.7.refs_0_, bf16[2,2,384,1024]{3,2,1,0:T(8,128)(2,1)} %bitcast.306, bf16[2,384,1024]{2,1,0:T(8,128)(2,1)} %copy-done.29, f32[2,6,1,1024]{3,2,1,0:T(1,128)} %get-tuple-element.49.refs_3_, ...), custom_call_target="tpu_custom_call" | custom-call | flops 25769803776 | bytes 16777216 | tf_op jit(solution)/shard_map/attn_backward/pallas_call | solution.py:193
  453.8 17.8 %collective-permute-done.8 = bf16[512,768]{1,0:T(8,128)(2,1)} collective-permute-done((bf16[512,768]{1,0:T(8,128)(2,1)}, bf16[512,768]{1,0:T(8,128)(2,1)}, u32[]{:S(2)}, u32[]{:S(2)}) %collective-permute-start.8) | collective-permute-done | bytes 786464 | tf_op jit(solution)/shard_map/ppermute | solution.py:391
  473.5 36.3 %attn_backward.6 = (f32[2,384,1024]{2,1,0:T(8,128)}, bf16[2,2,384,1024]{3,2,1,0:T(8,128)(2,1)}) custom-call(bf16[2,384,1024]{2,1,0:T(8,128)(2,1)} %add_convert_fusion.7.refs_0_, bf16[2,2,384,1024]{3,2,1,0:T(8,128)(2,1)} %bitcast.304, bf16[2,384,1024]{2,1,0:T(8,128)(2,1)} %copy-done.29, f32[2,6,1,1024]{3,2,1,0:T(1,128)} %get-tuple-element.49.refs_3_, ...), custom_call_target="tpu_custom_call" | custom-call | flops 25769803776 | bytes 16777216 | tf_op jit(solution)/shard_map/attn_backward/pallas_call | solution.py:193
  524.7 23.0 %collective-permute-done.10 = bf16[512,768]{1,0:T(8,128)(2,1)S(1)} collective-permute-done((bf16[512,768]{1,0:T(8,128)(2,1)S(1)}, bf16[512,768]{1,0:T(8,128)(2,1)S(1)}, u32[]{:S(2)}, u32[]{:S(2)}) %collective-permute-start.10) | collective-permute-done | bytes 786464 | tf_op jit(solution)/shard_map/ppermute | solution.py:391
  547.7 19.6 %collective-permute-done.11 = bf16[512,768]{1,0:T(8,128)(2,1)S(1)} collective-permute-done((bf16[512,768]{1,0:T(8,128)(2,1)S(1)}, bf16[512,768]{1,0:T(8,128)(2,1)S(1)}, u32[]{:S(2)}, u32[]{:S(2)}) %collective-permute-start.11) | collective-permute-done | bytes 786464 | tf_op jit(solution)/shard_map/ppermute | solution.py:391
  568.9 36.4 %attn_backward.7 = (bf16[2,384,1024]{2,1,0:T(8,128)(2,1)}, bf16[2,2,384,1024]{3,2,1,0:T(8,128)(2,1)}) custom-call(bf16[2,384,1024]{2,1,0:T(8,128)(2,1)} %add_convert_fusion.7.refs_0_, bf16[2,2,384,1024]{3,2,1,0:T(8,128)(2,1)} %bitcast.302, bf16[2,384,1024]{2,1,0:T(8,128)(2,1)} %copy-done.29, f32[2,6,1,1024]{3,2,1,0:T(1,128)} %get-tuple-element.49.refs_3_, ...), custom_call_target="tpu_custom_call" | custom-call | flops 25769803776 | bytes 16777216 | tf_op jit(solution)/shard_map/attn_backward/pallas_call | solution.py:193
  607.0 66.1 %all_gather.14 = f32[32,6,128]{2,1,0:T(8,128)S(1)} all-gather(f32[1,6,128]{2,1,0:T(8,128)S(1)} %all_gather_reshape_reshape.3), channel_id=1, replica_groups=mesh['fsdp'=4,'ctx'=4,'tp'=2] {'fsdp','ctx','tp'}, dimensions={0}, use_global_device_ids=true | all-gather | bytes 101376 | tf_op jit(solution)/shard_map/all_gather | solution.py:420
  707.4 20.9 %collective-permute-done.12 = bf16[512,768]{1,0:T(8,128)(2,1)} collective-permute-done((bf16[512,768]{1,0:T(8,128)(2,1)}, bf16[512,768]{1,0:T(8,128)(2,1)}, u32[]{:S(2)}, u32[]{:S(2)}) %collective-permute-start.12) | collective-permute-done | bytes 786464 | tf_op jit(solution)/shard_map/ppermute | solution.py:391
  728.4 5.2 add_convert_fusion.4
  738.2 13.5 %collective-permute-done.17 = bf16[2,2,48,512]{3,2,1,0:T(8,128)(2,1)S(1)} collective-permute-done((bf16[2,2,48,512]{3,2,1,0:T(8,128)(2,1)S(1)}, bf16[2,2,48,512]{3,2,1,0:T(8,128)(2,1)S(1)}, u32[]{:S(2)}, u32[]{:S(2)}) %collective-permute-start.17) | collective-permute-done | bytes 196640 | tf_op jit(solution)/shard_map/ppermute | solution.py:413
  763.1 5.1 collective-permute-done.23
  (275 shorter events, 185.0 us)
Async XLA Ops:
  7.2 139.4 %all-gather.4.cloned.1.call-start = ((), (), s32[]{:S(2)}) async-start(), calls=%async_computation.1 | async-start | bytes 4055040 | tf_op jit(solution)/shard_map/all_gather | solution.py:500
  10.5 236.5 %all-gather.6.cloned.1.call-start = ((), (), s32[]{:S(2)}) async-start(), calls=%async_computation.2 | async-start | bytes 10948608 | tf_op jit(solution)/shard_map/all_gather | solution.py:504
  12.5 688.8 %all-gather.8.cloned.1.call-start = ((), (), s32[]{:S(2)}) async-start(), calls=%async_computation.3 | async-start | bytes 1216512 | tf_op jit(solution)/shard_map/all_gather | solution.py:420
  14.0 26.3 %collective-permute-start.1 = (bf16[512,768]{1,0:T(8,128)(2,1)S(1)}, bf16[512,768]{1,0:T(8,128)(2,1)}, u32[]{:S(2)}, u32[]{:S(2)}) collective-permute-start(bf16[512,768]{1,0:T(8,128)(2,1)S(1)} %get-tuple-element.135), channel_id=1, source_target_pairs={{0,2},{2,4},{4,6},{6,0},{1,3},{3,5},{5,7},{7,1},{8,10},{10,12},{12... | collective-permute-start | bytes 2359304 | tf_op jit(solution)/shard_map/ppermute | solution.py:381
  17.1 46.2 %collective-permute-start.3 = (bf16[512,768]{1,0:T(8,128)(2,1)S(1)}, bf16[512,768]{1,0:T(8,128)(2,1)}, u32[]{:S(2)}, u32[]{:S(2)}) collective-permute-start(bf16[512,768]{1,0:T(8,128)(2,1)S(1)} %get-tuple-element.134), channel_id=1, source_target_pairs={{2,0},{4,2},{6,4},{0,6},{3,1},{5,3},{7,5},{1,7},{10,8},{12,10},{14... | collective-permute-start | bytes 2359304 | tf_op jit(solution)/shard_map/ppermute | solution.py:382
  40.3 44.9 %collective-permute-start.2 = (bf16[512,768]{1,0:T(8,128)(2,1)}, bf16[512,768]{1,0:T(8,128)(2,1)}, u32[]{:S(2)}, u32[]{:S(2)}) collective-permute-start(bf16[512,768]{1,0:T(8,128)(2,1)} %collective-permute-done.1), channel_id=1, source_target_pairs={{0,2},{2,4},{4,6},{6,0},{1,3},{3,5},{5,7},{7,1},{8,10},{10,12},{12... | collective-permute-start | bytes 2359304 | tf_op jit(solution)/shard_map/ppermute | solution.py:381
  63.3 43.3 %collective-permute-start.4 = (bf16[512,768]{1,0:T(8,128)(2,1)}, bf16[512,768]{1,0:T(8,128)(2,1)}, u32[]{:S(2)}, u32[]{:S(2)}) collective-permute-start(bf16[512,768]{1,0:T(8,128)(2,1)} %collective-permute-done.3), channel_id=1, source_target_pairs={{2,0},{4,2},{6,4},{0,6},{3,1},{5,3},{7,5},{1,7},{10,8},{12,10},{14... | collective-permute-start | bytes 2359304 | tf_op jit(solution)/shard_map/ppermute | solution.py:382
  85.2 44.0 %collective-permute-start.5 = (bf16[512,768]{1,0:T(8,128)(2,1)}, bf16[512,768]{1,0:T(8,128)(2,1)S(1)}, u32[]{:S(2)}, u32[]{:S(2)}) collective-permute-start(bf16[512,768]{1,0:T(8,128)(2,1)} %collective-permute-done.2), channel_id=1, source_target_pairs={{0,2},{2,4},{4,6},{6,0},{1,3},{3,5},{5,7},{7,1},{8,10},{10,12},{12... | collective-permute-start | bytes 2359304 | tf_op jit(solution)/shard_map/ppermute | solution.py:381
  106.6 39.9 %collective-permute-start.6 = (bf16[512,768]{1,0:T(8,128)(2,1)}, bf16[512,768]{1,0:T(8,128)(2,1)S(1)}, u32[]{:S(2)}, u32[]{:S(2)}) collective-permute-start(bf16[512,768]{1,0:T(8,128)(2,1)} %collective-permute-done.4), channel_id=1, source_target_pairs={{2,0},{4,2},{6,4},{0,6},{3,1},{5,3},{7,5},{1,7},{10,8},{12,10},{14... | collective-permute-start | bytes 2359304 | tf_op jit(solution)/shard_map/ppermute | solution.py:382
  355.1 418.2 %reduce-scatter.2.cloned.1.call-start = ((), (), s32[]{:S(2)}) async-start(), calls=%async_computation.4 | async-start | bytes 10948608 | tf_op jit(solution)/shard_map/reduce_scatter | solution.py:574
  435.0 36.7 %collective-permute-start.8 = (bf16[512,768]{1,0:T(8,128)(2,1)}, bf16[512,768]{1,0:T(8,128)(2,1)}, u32[]{:S(2)}, u32[]{:S(2)}) collective-permute-start(bf16[512,768]{1,0:T(8,128)(2,1)} %get-tuple-element.55), channel_id=1, source_target_pairs={{2,0},{4,2},{6,4},{0,6},{3,1},{5,3},{7,5},{1,7},{10,8},{12,10},{14... | collective-permute-start | bytes 2359304 | tf_op jit(solution)/shard_map/ppermute | solution.py:391
  436.8 34.8 %collective-permute-start.9 = (bf16[512,768]{1,0:T(8,128)(2,1)}, bf16[512,768]{1,0:T(8,128)(2,1)}, u32[]{:S(2)}, u32[]{:S(2)}) collective-permute-start(bf16[512,768]{1,0:T(8,128)(2,1)} %get-tuple-element.56), channel_id=1, source_target_pairs={{0,2},{2,4},{4,6},{6,0},{1,3},{3,5},{5,7},{7,1},{8,10},{10,12},{12... | collective-permute-start | bytes 2359304 | tf_op jit(solution)/shard_map/ppermute | solution.py:391
  438.2 76.6 %collective-permute-start.7 = (bf16[1,512,768]{2,1,0:T(8,128)(2,1)}, bf16[1,512,768]{2,1,0:T(8,128)(2,1)}, u32[]{:S(2)}, u32[]{:S(2)}) collective-permute-start(bf16[1,512,768]{2,1,0:T(8,128)(2,1)} %dynamic-slice_bitcast_fusion.5), channel_id=1, source_target_pairs={{0,1},{1,0},{2,3},{3,2},{4,5},{5,4},{6,7},{7,6},{8,9},{9,8},{10,11... | collective-permute-start | bytes 2359304 | tf_op jit(solution)/shard_map/ppermute | solution.py:445
  509.9 37.8 %collective-permute-start.10 = (bf16[512,768]{1,0:T(8,128)(2,1)S(1)}, bf16[512,768]{1,0:T(8,128)(2,1)S(1)}, u32[]{:S(2)}, u32[]{:S(2)}) collective-permute-start(bf16[512,768]{1,0:T(8,128)(2,1)S(1)} %get-tuple-element.60), channel_id=1, source_target_pairs={{2,0},{4,2},{6,4},{0,6},{3,1},{5,3},{7,5},{1,7},{10,8},{12,10},{14... | collective-permute-start | bytes 2359304 | tf_op jit(solution)/shard_map/ppermute | solution.py:391
  511.7 55.6 %collective-permute-start.11 = (bf16[512,768]{1,0:T(8,128)(2,1)S(1)}, bf16[512,768]{1,0:T(8,128)(2,1)S(1)}, u32[]{:S(2)}, u32[]{:S(2)}) collective-permute-start(bf16[512,768]{1,0:T(8,128)(2,1)S(1)} %get-tuple-element.61), channel_id=1, source_target_pairs={{0,2},{2,4},{4,6},{6,0},{1,3},{3,5},{5,7},{7,1},{8,10},{10,12},{12... | collective-permute-start | bytes 2359304 | tf_op jit(solution)/shard_map/ppermute | solution.py:391
  689.9 15.4 %collective-permute-start.15 = (bf16[2,2,2,2,48,512]{5,4,3,2,1,0:T(8,128)(2,1)}, bf16[2,2,2,2,48,512]{5,4,3,2,1,0:T(8,128)(2,1)}, u32[]{:S(2)}, u32[]{:S(2)}) collective-permute-start(bf16[2,2,2,2,48,512]{5,4,3,2,1,0:T(8,128)(2,1)} %dynamic-slice_bitcast_fusion.3), channel_id=1, source_target_pairs={{0,8},{8,0},{16,24},{24,16},{1,9},{9,1},{17,25},{25,17},{2,10},{10... | collective-permute-start | bytes 2359304 | tf_op jit(solution)/shard_map/ppermute | solution.py:413
  691.2 42.5 %collective-permute-start.20 = (bf16[2,2,2,2,48,640]{5,4,3,2,1,0:T(8,128)(2,1)}, bf16[2,2,2,2,48,640]{5,4,3,2,1,0:T(8,128)(2,1)}, u32[]{:S(2)}, u32[]{:S(2)}) collective-permute-start(bf16[2,2,2,2,48,640]{5,4,3,2,1,0:T(8,128)(2,1)} %dynamic-slice_bitcast_fusion), channel_id=1, source_target_pairs={{0,8},{8,0},{16,24},{24,16},{1,9},{9,1},{17,25},{25,17},{2,10},{10... | collective-permute-start | bytes 2949128 | tf_op jit(solution)/shard_map/ppermute | solution.py:413
  691.8 36.6 %collective-permute-start.12 = (bf16[512,768]{1,0:T(8,128)(2,1)}, bf16[512,768]{1,0:T(8,128)(2,1)}, u32[]{:S(2)}, u32[]{:S(2)}) collective-permute-start(bf16[512,768]{1,0:T(8,128)(2,1)} %get-tuple-element.66), channel_id=1, source_target_pairs={{2,0},{4,2},{6,4},{0,6},{3,1},{5,3},{7,5},{1,7},{10,8},{12,10},{14... | collective-permute-start | bytes 2359304 | tf_op jit(solution)/shard_map/ppermute | solution.py:391
  691.8 36.6 %collective-permute-start.13 = (bf16[512,768]{1,0:T(8,128)(2,1)}, bf16[512,768]{1,0:T(8,128)(2,1)}, u32[]{:S(2)}, u32[]{:S(2)}) collective-permute-start(bf16[512,768]{1,0:T(8,128)(2,1)} %get-tuple-element.67), channel_id=1, source_target_pairs={{0,2},{2,4},{4,6},{6,0},{1,3},{3,5},{5,7},{7,1},{8,10},{10,12},{12... | collective-permute-start | bytes 2359304 | tf_op jit(solution)/shard_map/ppermute | solution.py:391
  706.9 29.4 %collective-permute-start.16 = (bf16[2,2,2,48,512]{4,3,2,1,0:T(8,128)(2,1)S(1)}, bf16[2,2,2,48,512]{4,3,2,1,0:T(8,128)(2,1)S(1)}, u32[]{:S(2)}, u32[]{:S(2)}) collective-permute-start(bf16[2,2,2,48,512]{4,3,2,1,0:T(8,128)(2,1)S(1)} %dynamic-slice_bitcast_fusion.8), channel_id=1, source_target_pairs={{0,1},{1,0},{2,3},{3,2},{4,5},{5,4},{6,7},{7,6},{8,9},{9,8},{10,11... | collective-permute-start | bytes 1179656 | tf_op jit(solution)/shard_map/ppermute | solution.py:413
  735.1 18.8 %collective-permute-start.21 = (bf16[2,2,2,48,640]{4,3,2,1,0:T(8,128)(2,1)S(1)}, bf16[2,2,2,48,640]{4,3,2,1,0:T(8,128)(2,1)S(1)}, u32[]{:S(2)}, u32[]{:S(2)}) collective-permute-start(bf16[2,2,2,48,640]{4,3,2,1,0:T(8,128)(2,1)S(1)} %dynamic-slice_bitcast_fusion.7), channel_id=1, source_target_pairs={{0,16},{8,24},{16,0},{24,8},{1,17},{9,25},{17,1},{25,9},{2,18},{10... | collective-permute-start | bytes 1474568 | tf_op jit(solution)/shard_map/ppermute | solution.py:413
  736.4 15.3 %collective-permute-start.17 = (bf16[2,2,48,512]{3,2,1,0:T(8,128)(2,1)S(1)}, bf16[2,2,48,512]{3,2,1,0:T(8,128)(2,1)S(1)}, u32[]{:S(2)}, u32[]{:S(2)}) collective-permute-start(bf16[2,2,48,512]{3,2,1,0:T(8,128)(2,1)S(1)} %dynamic-slice_bitcast_fusion.10), channel_id=1, source_target_pairs={{0,16},{8,24},{16,0},{24,8},{1,17},{9,25},{17,1},{25,9},{2,18},{10... | collective-permute-start | bytes 589832 | tf_op jit(solution)/shard_map/ppermute | solution.py:413
  737.5 30.8 %collective-permute-start.14 = (bf16[1,512,768]{2,1,0:T(8,128)(2,1)S(1)}, bf16[1,512,768]{2,1,0:T(8,128)(2,1)S(1)}, u32[]{:S(2)}, u32[]{:S(2)}) collective-permute-start(bf16[1,512,768]{2,1,0:T(8,128)(2,1)S(1)} %dynamic-slice_bitcast_fusion.4), channel_id=1, source_target_pairs={{0,1},{1,0},{2,3},{3,2},{4,5},{5,4},{6,7},{7,6},{8,9},{9,8},{10,11... | collective-permute-start | bytes 2359304 | tf_op jit(solution)/shard_map/ppermute | solution.py:445
  761.0 7.2 collective-permute-start.23
  (48 other events, 643.0 us)
Sparse Core Ops, SparseCore 0:
  11.4 84.4 all-gather.3
  98.7 112.3 all-gather.5
  355.2 53.4 all-gather.7
  448.4 168.6 reduce-scatter.1

commit v5 on v4

--- a/solution.py
+++ b/solution.py
@@ -271,11 +271,10 @@
     sum_ref[...] = total
 
 
-def ffn_specs(rows, width, weights, head_width, ff_width):
-    block = head_width
+def ffn_specs(rows, width, weights, block, ff_width):
     per = ff_width // block
-    up_spec = pl.BlockSpec((1, width, block), lambda t, j: (t, 0, 1 + j))
-    down_spec = pl.BlockSpec((1, width, block), lambda t, j: (t, 0, 1 + per + j))
+    up_spec = pl.BlockSpec((1, width, block), lambda t, j: (t, 0, j))
+    down_spec = pl.BlockSpec((1, width, block), lambda t, j: (t, 0, per + j))
     row_spec = pl.BlockSpec((rows, width), lambda t, j: (0, 0))
     hidden_spec = pl.BlockSpec((rows, block), lambda t, j: (0, t * per + j))
     vector_spec = pl.BlockSpec((1, block), lambda t, j: (0, t * per + j))
@@ -287,10 +286,10 @@
 )
 
 
-def ffn_forward(y_low, weights, bias, head_width, ff_width):
+def ffn_forward(y_low, weights, bias, block, ff_width):
     rows, width = y_low.shape
     grid, up_spec, down_spec, row_spec, hidden_spec, vector_spec = ffn_specs(
-        rows, width, weights, head_width, ff_width
+        rows, width, weights, block, ff_width
     )
     hidden = grid[0] * ff_width
     return pl.pallas_call(
@@ -308,10 +307,10 @@
     )(y_low, weights, weights, bias)
 
 
-def ffn_backward(df, weights, slope, head_width, ff_width):
+def ffn_backward(df, weights, slope, block, ff_width):
     rows, width = df.shape
     grid, up_spec, down_spec, row_spec, hidden_spec, vector_spec = ffn_specs(
-        rows, width, weights, head_width, ff_width
+        rows, width, weights, block, ff_width
     )
     hidden = grid[0] * ff_width
     return pl.pallas_call(
@@ -332,22 +331,22 @@
 def weight_grad_kernel(da_ref, y_ref, df_ref, mixed_ref, du_ref, act_ref, out_ref, *, per):
     j = pl.program_id(1)
 
-    @pl.when(j == 0)
+    @pl.when(j == 2 * per)
     def _():
-        out_ref[0] = dot(da_ref[...], mixed_ref[0], 0, 1).astype(B)
-
-    @pl.when((j > 0) & (j <= per))
+        out_ref[0, :, : mixed_ref.shape[1]] = dot(da_ref[...], mixed_ref[0], 0, 1).astype(B)
+
+    @pl.when(j < per)
     def _():
         out_ref[0] = dot(y_ref[...], du_ref[...], 0, 0).astype(B)
 
-    @pl.when(j > per)
+    @pl.when((j >= per) & (j < 2 * per))
     def _():
         out_ref[0] = dot(df_ref[...], act_ref[...], 0, 0).astype(B)
 
 
-def weight_grads(da, y_low, df, mixed_t, du, act):
+def weight_grads(da, y_low, df, mixed_t, du, act, block):
     rows, width = da.shape
-    parts, block, _ = mixed_t.shape
+    parts, head_width, _ = mixed_t.shape
     per = du.shape[1] // parts // block
     row_spec = pl.BlockSpec((rows, width), lambda t, j: (0, 0))
     return pl.pallas_call(
@@ -357,14 +356,12 @@
             row_spec,
             row_spec,
             row_spec,
-            pl.BlockSpec((1, block, rows), lambda t, j: (t, 0, 0)),
-            pl.BlockSpec((rows, block), lambda t, j: (0, t * per + jnp.clip(j - 1, 0, per - 1))),
-            pl.BlockSpec(
-                (rows, block), lambda t, j: (0, t * per + jnp.clip(j - 1 - per, 0, per - 1))
-            ),
+            pl.BlockSpec((1, head_width, rows), lambda t, j: (t, 0, 0)),
+            pl.BlockSpec((rows, block), lambda t, j: (0, t * per + jnp.clip(j, 0, per - 1))),
+            pl.BlockSpec((rows, block), lambda t, j: (0, t * per + jnp.clip(j - per, 0, per - 1))),
         ],
         out_specs=pl.BlockSpec((1, width, block), lambda t, j: (t, 0, j)),
-        out_shape=jax.ShapeDtypeStruct((parts, width, block * (1 + 2 * per)), B),
+        out_shape=jax.ShapeDtypeStruct((parts, width, head_width + 2 * per * block), B),
         compiler_params=FFN_PARAMS,
         name="weight_grads",
     )(da, y_low, df, mixed_t, du, act)
@@ -419,6 +416,16 @@
 def sum_all(vector):
     every = lax.all_gather(vector.reshape(-1, 128), ("fsdp", "ctx", "tp"), axis=0)
     return jnp.sum(every, axis=0).reshape(-1)
+
+
+def sum_steps(vector):
+    for axis in ("fsdp", "tp", "ctx"):
+        size = lax.axis_size(axis)
+        bit = 1
+        while bit < size:
+            vector = vector + lax.ppermute(vector, axis, [(i, i ^ bit) for i in range(size)])
+            bit *= 2
+    return vector
 
 
 def tp_gather(vector):
@@ -500,7 +507,7 @@
     first_all = lax.all_gather(first_shard, WEIGHT_AXES, axis=0, tiled=True)
     first_all = first_all.reshape(tp_count, width, first_shard.shape[1])
     x_pieces = [ring_gather(own_tokens[s]) for s in range(own_seqs)]
-    second_shard = jnp.concatenate([out_weight, up_weight, down_weight], axis=1)
+    second_shard = jnp.concatenate([up_weight, down_weight, out_weight], axis=1)
     second_all = lax.all_gather(second_shard, WEIGHT_AXES, axis=0, tiled=True)
     second_all = second_all.reshape(tp_count, width, second_shard.shape[1])
     w_q = first_all[:, :, :head_width]
@@ -508,7 +515,7 @@
     rows_all = jnp.transpose(first_all[0, :, 3 * head_width :]).astype(F)
     gain1, gain2 = rows_all[0], rows_all[1]
     out_bias, shift1, down_bias, shift2 = (rows_all[2 + i] for i in range(4))
-    w_out = second_all[:, :, :head_width]
+    w_out = second_all[:, :, 2 * ff_width :]
     bias_all = tp_gather(jnp.concatenate([qv_bias.reshape(-1), up_bias]))
     q_bias = bias_all[:, :head_width].astype(F)
     v_bias = bias_all[:, head_width : 2 * head_width].astype(F)
@@ -528,7 +535,8 @@
     q_t, kv_t, om_t, lse, mixed_s = [], [], [], [], []
     for s in range(own_seqs):
         q_s = (dot(w_q, own_tokens[s], 1, 1) + q_bias[:, :, None]).astype(B)
-        kv_s = [project(block) for block in x_chunks[s][:near]]
+        kv_s = [project(x_chunks[s][0])]
+        kv_s = kv_s + [project(block) for block in x_chunks[s][1:near]]
         if near < chunk_count:
             state = attention_forward(q_s, kv_s, None, False, 2048)
             kv_far = [project(block) for block in x_chunks[s][near:]]
@@ -549,8 +557,9 @@
     )
     first_low = first_out.astype(B)
 
+    block = ff_width // 2
     act_low, slope, ffn_out = ffn_forward(
-        first_low, second_all, u_bias.reshape(1, -1), head_width, ff_width
+        first_low, second_all, u_bias.reshape(1, -1), block, ff_width
     )
     ffn_out = ffn_out + down_bias
     grad_final = own_cotangent.reshape(rows, width).astype(F)
@@ -561,14 +570,14 @@
     grad_second = norm_backward(grad_final, final_norm, final_scale, gain2)
     df = grad_second.astype(B)
     down_bias_grad = jnp.sum(df.astype(F), axis=0)
-    inner_low, up_bias_grad, back = ffn_backward(df, second_all, slope, head_width, ff_width)
+    inner_low, up_bias_grad, back = ffn_backward(df, second_all, slope, block, ff_width)
     first_grad = grad_second + back
     gain1_grad = jnp.sum(first_grad * first_norm, axis=0)
     shift1_grad = jnp.sum(first_grad, axis=0)
     resid_grad = norm_backward(first_grad, first_norm, first_scale, gain1)
     da = resid_grad.astype(B)
     out_bias_grad = jnp.sum(da.astype(F), axis=0)
-    second_grad = weight_grads(da, first_low, df, mixed_t, inner_low, act_low)
+    second_grad = weight_grads(da, first_low, df, mixed_t, inner_low, act_low, block)
     do_t = dot(w_out, da, 1, 1).astype(B)
     do_t, second_grad = lax.optimization_barrier((do_t, second_grad))
     second_grad = lax.psum_scatter(
@@ -618,7 +627,7 @@
         if got is not None:
             part = part + jnp.concatenate(got, axis=0).astype(F)
         own_grads.append(part)
-    q_bias_grad = sum_all(q_bias_grad.reshape(-1))
+    q_bias_grad = sum_steps(q_bias_grad.reshape(-1))
     qkv_grad = jnp.stack(
         [jnp.concatenate([q_grad[t], kv_grad[t]], axis=1).astype(B) for t in range(tp_count)]
     )
@@ -650,10 +659,10 @@
         tokens_out,
         qkv_grad.reshape(shard_rows, 3, head_width),
         jnp.stack([q_total, v_total]),
-        second_grad[:, :head_width],
-        second_grad[:, head_width : head_width + ff_width],
+        second_grad[:, 2 * ff_width :],
+        second_grad[:, :ff_width],
         up_total,
-        second_grad[:, head_width + ff_width :],
+        second_grad[:, ff_width : 2 * ff_width],
         six[:, :2],
         six[:, 2:],
     )

time: 790 us -> 740 us (0.937)
  blocking collectives: 66.1 us -> 0 us
  waiting for transfers between devices: 194 us -> 212 us
  Pallas kernels: 302 us -> 289 us
  starting transfers between devices: 55.8 us -> 66.3 us
    all_gather x1 -> x0, blocking collectives: 66.1 us -> none  [sum_all(): lax.all_gather(vector.reshape(-1, 128), ('fsdp', 'ctx', 'tp'), axis=0)]
    ppermute x0 -> x5, waiting for transfers between devices: none -> 35.8 us  [sum_steps(): lax.ppermute(vector, axis, [(i, i ^ bit) for i in range(size)])]
    ppermute x6, waiting for transfers between devices: 81.4 us -> 71.3 us  [ring_return(): return (lax.ppermute(first, 'ctx', down), lax.ppermute(second, 'ctx', up))]
    unnamed x100 -> x104, local copies, waits for them, and re-layouts: 16.4 us -> 16.5 us
  transfers between devices with their start and end apart: 29 -> 34, of which waited for: 15 -> 18; matrix products, arithmetic and copies ran while one was open for 14% -> 14% of each run, Pallas kernels for 28% -> 25%
where the time goes in v5:
time: 740 us; the launch traced here: 734 us
  Pallas kernels  289 us (39%)
  waiting for transfers between devices  212 us (29%)
  matrix products  75 us (10%)
  starting transfers between devices  66.3 us (9%)
  local copies, waits for them, and re-layouts  44.6 us (6%)
  other arithmetic  32.2 us (4%)
  between operations  15.2 us (2%)
    pallas_call x4, Pallas kernels, attention_backward(): pl.pallas_call(lambda *refs: backward_kernel(*refs, first=first, bk=bk, b...  145 us
    pallas_call x2, Pallas kernels, attention_forward(): pl.pallas_call(lambda *refs: forward_kernel(*refs, chunks=chunks, first=f...  75.5 us
    dot_general x28, matrix products, dot(): lax.dot_general(left, right, (((left_dim,), (right_dim,)), ((), ())), pre...  75 us
    ppermute x6, waiting for transfers between devices, ring_return(): return (lax.ppermute(first, 'ctx', down), lax.ppermute(second, 'ctx', up))  71.3 us
    ppermute x3, waiting for transfers between devices, ring_gather(): first = lax.ppermute(first, 'ctx', up)  50.4 us
    ppermute x5, waiting for transfers between devices, sum_steps(): lax.ppermute(vector, axis, [(i, i ^ bit) for i in range(size)])  35.8 us
    ppermute x3, waiting for transfers between devices, ring_gather(): second = lax.ppermute(second, 'ctx', down)  32.6 us
    ppermute x3, starting transfers between devices, ring_gather(): first = lax.ppermute(first, 'ctx', up)  32.2 us
  transfers between devices with their start and end apart: 34, of which 18 were waited for; matrix products, arithmetic and copies ran while one was open for 14% of the time, Pallas kernels for 25%

profile of v5, /device:TPU:0, one launch (start us, length us, event | category | flops | bytes accessed | tf_op | source)
XLA Modules:
  0.0 734.1 jit_solution(12100787752960723896)
XLA Ops:
  19.2 21.1 %collective-permute-done.1 = bf16[512,768]{1,0:T(8,128)(2,1)} collective-permute-done((bf16[512,768]{1,0:T(8,128)(2,1)S(1)}, bf16[512,768]{1,0:T(8,128)(2,1)}, u32[]{:S(2)}, u32[]{:S(2)}) %collective-permute-start.1) | collective-permute-done | bytes 786464 | tf_op jit(solution)/shard_map/ppermute | solution.py:378
  40.3 10.3 %collective-permute-start.2 = (bf16[512,768]{1,0:T(8,128)(2,1)}, bf16[512,768]{1,0:T(8,128)(2,1)}, u32[]{:S(2)}, u32[]{:S(2)}) collective-permute-start(bf16[512,768]{1,0:T(8,128)(2,1)} %collective-permute-done.1), channel_id=1, source_target_pairs={{0,2},{2,4},{4,6},{6,0},{1,3},{3,5},{5,7},{7,1},{8,10},{10,12},{12... | collective-permute-start | bytes 2359304 | tf_op jit(solution)/shard_map/ppermute | solution.py:378
  50.6 12.7 %collective-permute-done.3 = bf16[512,768]{1,0:T(8,128)(2,1)} collective-permute-done((bf16[512,768]{1,0:T(8,128)(2,1)S(1)}, bf16[512,768]{1,0:T(8,128)(2,1)}, u32[]{:S(2)}, u32[]{:S(2)}) %collective-permute-start.3) | collective-permute-done | bytes 786464 | tf_op jit(solution)/shard_map/ppermute | solution.py:379
  70.7 14.5 %collective-permute-done.2 = bf16[512,768]{1,0:T(8,128)(2,1)} collective-permute-done((bf16[512,768]{1,0:T(8,128)(2,1)}, bf16[512,768]{1,0:T(8,128)(2,1)}, u32[]{:S(2)}, u32[]{:S(2)}) %collective-permute-start.2) | collective-permute-done | bytes 786464 | tf_op jit(solution)/shard_map/ppermute | solution.py:378
  85.2 18.8 %collective-permute-start.5 = (bf16[512,768]{1,0:T(8,128)(2,1)}, bf16[512,768]{1,0:T(8,128)(2,1)S(1)}, u32[]{:S(2)}, u32[]{:S(2)}) collective-permute-start(bf16[512,768]{1,0:T(8,128)(2,1)} %collective-permute-done.2), channel_id=1, source_target_pairs={{0,2},{2,4},{4,6},{6,0},{1,3},{3,5},{5,7},{7,1},{8,10},{10,12},{12... | collective-permute-start | bytes 2359304 | tf_op jit(solution)/shard_map/ppermute | solution.py:378
  114.4 14.8 %collective-permute-done.5 = bf16[512,768]{1,0:T(8,128)(2,1)S(1)} collective-permute-done((bf16[512,768]{1,0:T(8,128)(2,1)}, bf16[512,768]{1,0:T(8,128)(2,1)S(1)}, u32[]{:S(2)}, u32[]{:S(2)}) %collective-permute-start.5) | collective-permute-done | bytes 786464 | tf_op jit(solution)/shard_map/ppermute | solution.py:378
  129.3 17.3 %collective-permute-done.6 = bf16[512,768]{1,0:T(8,128)(2,1)S(1)} collective-permute-done((bf16[512,768]{1,0:T(8,128)(2,1)}, bf16[512,768]{1,0:T(8,128)(2,1)S(1)}, u32[]{:S(2)}, u32[]{:S(2)}) %collective-permute-start.6) | collective-permute-done | bytes 786464 | tf_op jit(solution)/shard_map/ppermute | solution.py:379
  149.1 4.6 add_convert_fusion.7.refs_0_
  171.2 34.5 %attn_forward.2 = (f32[2,384,1024]{2,1,0:T(8,128)}, f32[2,6,2,1024]{3,2,1,0:T(2,128)}) custom-call(bf16[2,384,1024]{2,1,0:T(8,128)(2,1)} %add_convert_fusion.7.refs_0_, bf16[2,2,384,1024]{3,2,1,0:T(8,128)(2,1)} %bitcast.299, bf16[2,2,384,1024]{3,2,1,0:T(8,128)(2,1)} %bitcast.301), custom_call_target="tpu_custom_call" | custom-call | flops 25769803776 | bytes 16777216 | tf_op jit(solution)/shard_map/attn_forward/pallas_call | solution.py:104
  205.7 41.0 %attn_forward.3 = (f32[2,384,1024]{2,1,0:T(8,128)}, f32[2,6,1,1024]{3,2,1,0:T(1,128)}, bf16[2,384,1024]{2,1,0:T(8,128)(2,1)}) custom-call(bf16[2,384,1024]{2,1,0:T(8,128)(2,1)} %add_convert_fusion.7.refs_0_, bf16[2,2,384,1024]{3,2,1,0:T(8,128)(2,1)} %bitcast.303, bf16[2,2,384,1024]{3,2,1,0:T(8,128)(2,1)} %bitcast.305, ...), custom_call_target="tpu_custom_call" | custom-call | flops 25769803776 | bytes 16777216 | tf_op jit(solution)/shard_map/attn_forward/pallas_call | solution.py:104
  254.0 29.4 %ffn_forward.1 = (bf16[1024,3072]{1,0:T(8,128)(2,1)}, f32[1024,3072]{1,0:T(8,128)}, f32[1024,768]{1,0:T(8,128)}) custom-call(bf16[1024,768]{1,0:T(8,128)(2,1)} %fusion.9.refs_0_.refs_1_, bf16[2,768,3456]{2,1,0:T(8,128)(2,1)} %bitcast.238, bf16[2,768,3456]{2,1,0:T(8,128)(2,1)} %bitcast.239, f32[1,3072]{1,0:T(1,128)} %bitcast.296), custom_call_target="tpu_custom_call" | custom-call | tf_op jit(solution)/shard_map/ffn_forward/pallas_call | solution.py:295
  292.3 16.6 %ffn_backward.1 = (bf16[1024,3072]{1,0:T(8,128)(2,1)}, f32[1,3072]{1,0:T(1,128)}, f32[1024,768]{1,0:T(8,128)}) custom-call(bf16[1024,768]{1,0:T(8,128)(2,1)} %get-tuple-element.114.refs_0_.refs_2_, bf16[2,768,3456]{2,1,0:T(8,128)(2,1)} %bitcast.240, bf16[2,768,3456]{2,1,0:T(8,128)(2,1)} %bitcast.241, f32[1024,3072]{1,0:T(8,128)} %get-tuple-element.44.refs_3_), custom_call_target="tpu_custom_call" | custom-call | tf_op jit(solution)/shard_map/ffn_backward/pallas_call | solution.py:316
  308.9 4.8 multiply_reduce_fusion
  319.4 21.9 %weight_grads.1 = bf16[2,768,3456]{2,1,0:T(8,128)(2,1)} custom-call(bf16[1024,768]{1,0:T(8,128)(2,1)} %copy-done.10, bf16[1024,768]{1,0:T(8,128)(2,1)} %fusion.9.refs_0_.refs_1_, bf16[1024,768]{1,0:T(8,128)(2,1)} %get-tuple-element.114.refs_0_.refs_2_, bf16[2,384,1024]{2,1,0:T(8,128)(2,1)} %get-tuple-element.42.refs_3_, ...), custom_call_target="tpu_custom_call" | custom-call | tf_op jit(solution)/shard_map/weight_grads/pallas_call | solution.py:352
  341.6 36.2 %attn_backward.4 = (f32[2,384,1024]{2,1,0:T(8,128)}, bf16[2,2,384,1024]{3,2,1,0:T(8,128)(2,1)}) custom-call(bf16[2,384,1024]{2,1,0:T(8,128)(2,1)} %add_convert_fusion.7.refs_0_, bf16[2,2,384,1024]{3,2,1,0:T(8,128)(2,1)} %bitcast.306, bf16[2,384,1024]{2,1,0:T(8,128)(2,1)} %copy-done.29, f32[2,6,1,1024]{3,2,1,0:T(1,128)} %get-tuple-element.49.refs_3_, ...), custom_call_target="tpu_custom_call" | custom-call | flops 25769803776 | bytes 16777216 | tf_op jit(solution)/shard_map/attn_backward/pallas_call | solution.py:193
  385.9 36.3 %attn_backward.5 = (f32[2,384,1024]{2,1,0:T(8,128)}, bf16[2,2,384,1024]{3,2,1,0:T(8,128)(2,1)}) custom-call(bf16[2,384,1024]{2,1,0:T(8,128)(2,1)} %add_convert_fusion.7.refs_0_, bf16[2,2,384,1024]{3,2,1,0:T(8,128)(2,1)} %bitcast.304, bf16[2,384,1024]{2,1,0:T(8,128)(2,1)} %copy-done.29, f32[2,6,1,1024]{3,2,1,0:T(1,128)} %get-tuple-element.49.refs_3_, ...), custom_call_target="tpu_custom_call" | custom-call | flops 25769803776 | bytes 16777216 | tf_op jit(solution)/shard_map/attn_backward/pallas_call | solution.py:193
  440.7 21.3 %collective-permute-done.8 = bf16[512,768]{1,0:T(8,128)(2,1)} collective-permute-done((bf16[512,768]{1,0:T(8,128)(2,1)}, bf16[512,768]{1,0:T(8,128)(2,1)}, u32[]{:S(2)}, u32[]{:S(2)}) %collective-permute-start.8) | collective-permute-done | bytes 786464 | tf_op jit(solution)/shard_map/ppermute | solution.py:388
  463.9 36.3 %attn_backward.6 = (f32[2,384,1024]{2,1,0:T(8,128)}, bf16[2,2,384,1024]{3,2,1,0:T(8,128)(2,1)}) custom-call(bf16[2,384,1024]{2,1,0:T(8,128)(2,1)} %add_convert_fusion.7.refs_0_, bf16[2,2,384,1024]{3,2,1,0:T(8,128)(2,1)} %bitcast.302, bf16[2,384,1024]{2,1,0:T(8,128)(2,1)} %copy-done.29, f32[2,6,1,1024]{3,2,1,0:T(1,128)} %get-tuple-element.49.refs_3_, ...), custom_call_target="tpu_custom_call" | custom-call | flops 25769803776 | bytes 16777216 | tf_op jit(solution)/shard_map/attn_backward/pallas_call | solution.py:193
  515.0 34.8 %collective-permute-done.10 = bf16[512,768]{1,0:T(8,128)(2,1)S(1)} collective-permute-done((bf16[512,768]{1,0:T(8,128)(2,1)S(1)}, bf16[512,768]{1,0:T(8,128)(2,1)S(1)}, u32[]{:S(2)}, u32[]{:S(2)}) %collective-permute-start.10) | collective-permute-done | bytes 786464 | tf_op jit(solution)/shard_map/ppermute | solution.py:388
  549.8 15.1 %collective-permute-done.11 = bf16[512,768]{1,0:T(8,128)(2,1)S(1)} collective-permute-done((bf16[512,768]{1,0:T(8,128)(2,1)S(1)}, bf16[512,768]{1,0:T(8,128)(2,1)S(1)}, u32[]{:S(2)}, u32[]{:S(2)}) %collective-permute-start.11) | collective-permute-done | bytes 786464 | tf_op jit(solution)/shard_map/ppermute | solution.py:388
  566.5 36.5 %attn_backward.7 = (bf16[2,384,1024]{2,1,0:T(8,128)(2,1)}, bf16[2,2,384,1024]{3,2,1,0:T(8,128)(2,1)}) custom-call(bf16[2,384,1024]{2,1,0:T(8,128)(2,1)} %add_convert_fusion.7.refs_0_, bf16[2,2,384,1024]{3,2,1,0:T(8,128)(2,1)} %bitcast.300, bf16[2,384,1024]{2,1,0:T(8,128)(2,1)} %copy-done.29, f32[2,6,1,1024]{3,2,1,0:T(1,128)} %get-tuple-element.49.refs_3_, ...), custom_call_target="tpu_custom_call" | custom-call | flops 25769803776 | bytes 16777216 | tf_op jit(solution)/shard_map/attn_backward/pallas_call | solution.py:193
  636.8 32.7 %collective-permute-done.28 = f32[768]{0:T(1024)S(1)} collective-permute-done((f32[768]{0:T(1024)S(1)}, f32[768]{0:T(1024)S(1)}, u32[]{:S(2)}, u32[]{:S(2)}) %collective-permute-start.28) | collective-permute-done | bytes 3104 | tf_op jit(solution)/shard_map/ppermute | solution.py:426
  680.3 5.2 add_convert_fusion.4
  691.6 10.8 %collective-permute-done.17 = bf16[2,2,48,512]{3,2,1,0:T(8,128)(2,1)S(1)} collective-permute-done((bf16[2,2,48,512]{3,2,1,0:T(8,128)(2,1)S(1)}, bf16[2,2,48,512]{3,2,1,0:T(8,128)(2,1)S(1)}, u32[]{:S(2)}, u32[]{:S(2)}) %collective-permute-start.17) | collective-permute-done | bytes 196640 | tf_op jit(solution)/shard_map/ppermute | solution.py:410
  (292 shorter events, 191.4 us)
Async XLA Ops:
  7.2 139.4 %all-gather.4.cloned.1.call-start = ((), (), s32[]{:S(2)}) async-start(), calls=%async_computation.1 | async-start | bytes 4055040 | tf_op jit(solution)/shard_map/all_gather | solution.py:507
  10.5 236.2 %all-gather.6.cloned.1.call-start = ((), (), s32[]{:S(2)}) async-start(), calls=%async_computation.2 | async-start | bytes 10948608 | tf_op jit(solution)/shard_map/all_gather | solution.py:511
  12.5 661.7 %all-gather.8.cloned.1.call-start = ((), (), s32[]{:S(2)}) async-start(), calls=%async_computation.3 | async-start | bytes 1216512 | tf_op jit(solution)/shard_map/all_gather | solution.py:417
  14.0 26.3 %collective-permute-start.1 = (bf16[512,768]{1,0:T(8,128)(2,1)S(1)}, bf16[512,768]{1,0:T(8,128)(2,1)}, u32[]{:S(2)}, u32[]{:S(2)}) collective-permute-start(bf16[512,768]{1,0:T(8,128)(2,1)S(1)} %get-tuple-element.135), channel_id=1, source_target_pairs={{0,2},{2,4},{4,6},{6,0},{1,3},{3,5},{5,7},{7,1},{8,10},{10,12},{12... | collective-permute-start | bytes 2359304 | tf_op jit(solution)/shard_map/ppermute | solution.py:378
  17.1 46.2 %collective-permute-start.3 = (bf16[512,768]{1,0:T(8,128)(2,1)S(1)}, bf16[512,768]{1,0:T(8,128)(2,1)}, u32[]{:S(2)}, u32[]{:S(2)}) collective-permute-start(bf16[512,768]{1,0:T(8,128)(2,1)S(1)} %get-tuple-element.134), channel_id=1, source_target_pairs={{2,0},{4,2},{6,4},{0,6},{3,1},{5,3},{7,5},{1,7},{10,8},{12,10},{14... | collective-permute-start | bytes 2359304 | tf_op jit(solution)/shard_map/ppermute | solution.py:379
  40.3 44.9 %collective-permute-start.2 = (bf16[512,768]{1,0:T(8,128)(2,1)}, bf16[512,768]{1,0:T(8,128)(2,1)}, u32[]{:S(2)}, u32[]{:S(2)}) collective-permute-start(bf16[512,768]{1,0:T(8,128)(2,1)} %collective-permute-done.1), channel_id=1, source_target_pairs={{0,2},{2,4},{4,6},{6,0},{1,3},{3,5},{5,7},{7,1},{8,10},{10,12},{12... | collective-permute-start | bytes 2359304 | tf_op jit(solution)/shard_map/ppermute | solution.py:378
  63.3 43.3 %collective-permute-start.4 = (bf16[512,768]{1,0:T(8,128)(2,1)}, bf16[512,768]{1,0:T(8,128)(2,1)}, u32[]{:S(2)}, u32[]{:S(2)}) collective-permute-start(bf16[512,768]{1,0:T(8,128)(2,1)} %collective-permute-done.3), channel_id=1, source_target_pairs={{2,0},{4,2},{6,4},{0,6},{3,1},{5,3},{7,5},{1,7},{10,8},{12,10},{14... | collective-permute-start | bytes 2359304 | tf_op jit(solution)/shard_map/ppermute | solution.py:379
  85.2 44.0 %collective-permute-start.5 = (bf16[512,768]{1,0:T(8,128)(2,1)}, bf16[512,768]{1,0:T(8,128)(2,1)S(1)}, u32[]{:S(2)}, u32[]{:S(2)}) collective-permute-start(bf16[512,768]{1,0:T(8,128)(2,1)} %collective-permute-done.2), channel_id=1, source_target_pairs={{0,2},{2,4},{4,6},{6,0},{1,3},{3,5},{5,7},{7,1},{8,10},{10,12},{12... | collective-permute-start | bytes 2359304 | tf_op jit(solution)/shard_map/ppermute | solution.py:378
  106.7 39.9 %collective-permute-start.6 = (bf16[512,768]{1,0:T(8,128)(2,1)}, bf16[512,768]{1,0:T(8,128)(2,1)S(1)}, u32[]{:S(2)}, u32[]{:S(2)}) collective-permute-start(bf16[512,768]{1,0:T(8,128)(2,1)} %collective-permute-done.4), channel_id=1, source_target_pairs={{2,0},{4,2},{6,4},{0,6},{3,1},{5,3},{7,5},{1,7},{10,8},{12,10},{14... | collective-permute-start | bytes 2359304 | tf_op jit(solution)/shard_map/ppermute | solution.py:379
  385.9 338.2 %reduce-scatter.2.cloned.1.call-start = ((), (), s32[]{:S(2)}) async-start(), calls=%async_computation.4 | async-start | bytes 10948608 | tf_op jit(solution)/shard_map/reduce_scatter | solution.py:583
  422.2 39.8 %collective-permute-start.8 = (bf16[512,768]{1,0:T(8,128)(2,1)}, bf16[512,768]{1,0:T(8,128)(2,1)}, u32[]{:S(2)}, u32[]{:S(2)}) collective-permute-start(bf16[512,768]{1,0:T(8,128)(2,1)} %get-tuple-element.55), channel_id=1, source_target_pairs={{2,0},{4,2},{6,4},{0,6},{3,1},{5,3},{7,5},{1,7},{10,8},{12,10},{14... | collective-permute-start | bytes 2359304 | tf_op jit(solution)/shard_map/ppermute | solution.py:388
  424.1 37.9 %collective-permute-start.9 = (bf16[512,768]{1,0:T(8,128)(2,1)}, bf16[512,768]{1,0:T(8,128)(2,1)}, u32[]{:S(2)}, u32[]{:S(2)}) collective-permute-start(bf16[512,768]{1,0:T(8,128)(2,1)} %get-tuple-element.56), channel_id=1, source_target_pairs={{0,2},{2,4},{4,6},{6,0},{1,3},{3,5},{5,7},{7,1},{8,10},{10,12},{12... | collective-permute-start | bytes 2359304 | tf_op jit(solution)/shard_map/ppermute | solution.py:388
  425.2 79.8 %collective-permute-start.7 = (bf16[1,512,768]{2,1,0:T(8,128)(2,1)}, bf16[1,512,768]{2,1,0:T(8,128)(2,1)}, u32[]{:S(2)}, u32[]{:S(2)}) collective-permute-start(bf16[1,512,768]{2,1,0:T(8,128)(2,1)} %dynamic-slice_bitcast_fusion.5), channel_id=1, source_target_pairs={{0,1},{1,0},{2,3},{3,2},{4,5},{5,4},{6,7},{7,6},{8,9},{9,8},{10,11... | collective-permute-start | bytes 2359304 | tf_op jit(solution)/shard_map/ppermute | solution.py:452
  500.2 49.6 %collective-permute-start.10 = (bf16[512,768]{1,0:T(8,128)(2,1)S(1)}, bf16[512,768]{1,0:T(8,128)(2,1)S(1)}, u32[]{:S(2)}, u32[]{:S(2)}) collective-permute-start(bf16[512,768]{1,0:T(8,128)(2,1)S(1)} %get-tuple-element.60), channel_id=1, source_target_pairs={{2,0},{4,2},{6,4},{0,6},{3,1},{5,3},{7,5},{1,7},{10,8},{12,10},{14... | collective-permute-start | bytes 2359304 | tf_op jit(solution)/shard_map/ppermute | solution.py:388
  501.9 63.0 %collective-permute-start.11 = (bf16[512,768]{1,0:T(8,128)(2,1)S(1)}, bf16[512,768]{1,0:T(8,128)(2,1)S(1)}, u32[]{:S(2)}, u32[]{:S(2)}) collective-permute-start(bf16[512,768]{1,0:T(8,128)(2,1)S(1)} %get-tuple-element.61), channel_id=1, source_target_pairs={{0,2},{2,4},{4,6},{6,0},{1,3},{3,5},{5,7},{7,1},{8,10},{10,12},{12... | collective-permute-start | bytes 2359304 | tf_op jit(solution)/shard_map/ppermute | solution.py:388
  604.8 22.0 %collective-permute-start.25 = (f32[768]{0:T(1024)S(1)}, f32[768]{0:T(1024)S(1)}, u32[]{:S(2)}, u32[]{:S(2)}) collective-permute-start(f32[768]{0:T(1024)S(1)} %reshape.296), channel_id=1, source_target_pairs={{0,8},{8,0},{16,24},{24,16},{1,9},{9,1},{17,25},{25,17},{2,10},{10... | collective-permute-start | bytes 9224 | tf_op jit(solution)/shard_map/ppermute | solution.py:426
  629.5 48.6 %collective-permute-start.15 = (bf16[2,2,2,2,48,512]{5,4,3,2,1,0:T(8,128)(2,1)}, bf16[2,2,2,2,48,512]{5,4,3,2,1,0:T(8,128)(2,1)}, u32[]{:S(2)}, u32[]{:S(2)}) collective-permute-start(bf16[2,2,2,2,48,512]{5,4,3,2,1,0:T(8,128)(2,1)} %dynamic-slice_bitcast_fusion.3), channel_id=1, source_target_pairs={{0,8},{8,0},{16,24},{24,16},{1,9},{9,1},{17,25},{25,17},{2,10},{10... | collective-permute-start | bytes 2359304 | tf_op jit(solution)/shard_map/ppermute | solution.py:410
  633.5 46.8 %collective-permute-start.12 = (bf16[512,768]{1,0:T(8,128)(2,1)}, bf16[512,768]{1,0:T(8,128)(2,1)}, u32[]{:S(2)}, u32[]{:S(2)}) collective-permute-start(bf16[512,768]{1,0:T(8,128)(2,1)} %get-tuple-element.66), channel_id=1, source_target_pairs={{2,0},{4,2},{6,4},{0,6},{3,1},{5,3},{7,5},{1,7},{10,8},{12,10},{14... | collective-permute-start | bytes 2359304 | tf_op jit(solution)/shard_map/ppermute | solution.py:388
  636.1 44.2 %collective-permute-start.13 = (bf16[512,768]{1,0:T(8,128)(2,1)}, bf16[512,768]{1,0:T(8,128)(2,1)}, u32[]{:S(2)}, u32[]{:S(2)}) collective-permute-start(bf16[512,768]{1,0:T(8,128)(2,1)} %get-tuple-element.67), channel_id=1, source_target_pairs={{0,2},{2,4},{4,6},{6,0},{1,3},{3,5},{5,7},{7,1},{8,10},{10,12},{12... | collective-permute-start | bytes 2359304 | tf_op jit(solution)/shard_map/ppermute | solution.py:388
  636.1 33.4 %collective-permute-start.28 = (f32[768]{0:T(1024)S(1)}, f32[768]{0:T(1024)S(1)}, u32[]{:S(2)}, u32[]{:S(2)}) collective-permute-start(f32[768]{0:T(1024)S(1)} %add.417), channel_id=1, source_target_pairs={{0,2},{2,0},{4,6},{6,4},{1,3},{3,1},{5,7},{7,5},{8,10},{10,8},{12,... | collective-permute-start | bytes 9224 | tf_op jit(solution)/shard_map/ppermute | solution.py:426
  671.8 13.7 %collective-permute-start.20 = (bf16[2,2,2,2,48,640]{5,4,3,2,1,0:T(8,128)(2,1)}, bf16[2,2,2,2,48,640]{5,4,3,2,1,0:T(8,128)(2,1)}, u32[]{:S(2)}, u32[]{:S(2)}) collective-permute-start(bf16[2,2,2,2,48,640]{5,4,3,2,1,0:T(8,128)(2,1)} %dynamic-slice_bitcast_fusion), channel_id=1, source_target_pairs={{0,8},{8,0},{16,24},{24,16},{1,9},{9,1},{17,25},{25,17},{2,10},{10... | collective-permute-start | bytes 2949128 | tf_op jit(solution)/shard_map/ppermute | solution.py:410
  687.1 17.3 %collective-permute-start.21 = (bf16[2,2,2,48,640]{4,3,2,1,0:T(8,128)(2,1)S(1)}, bf16[2,2,2,48,640]{4,3,2,1,0:T(8,128)(2,1)S(1)}, u32[]{:S(2)}, u32[]{:S(2)}) collective-permute-start(bf16[2,2,2,48,640]{4,3,2,1,0:T(8,128)(2,1)S(1)} %dynamic-slice_bitcast_fusion.7), channel_id=1, source_target_pairs={{0,16},{8,24},{16,0},{24,8},{1,17},{9,25},{17,1},{25,9},{2,18},{10... | collective-permute-start | bytes 1474568 | tf_op jit(solution)/shard_map/ppermute | solution.py:410
  689.3 13.2 %collective-permute-start.17 = (bf16[2,2,48,512]{3,2,1,0:T(8,128)(2,1)S(1)}, bf16[2,2,48,512]{3,2,1,0:T(8,128)(2,1)S(1)}, u32[]{:S(2)}, u32[]{:S(2)}) collective-permute-start(bf16[2,2,48,512]{3,2,1,0:T(8,128)(2,1)S(1)} %dynamic-slice_bitcast_fusion.10), channel_id=1, source_target_pairs={{0,16},{8,24},{16,0},{24,8},{1,17},{9,25},{17,1},{25,9},{2,18},{10... | collective-permute-start | bytes 589832 | tf_op jit(solution)/shard_map/ppermute | solution.py:410
  690.9 30.3 %collective-permute-start.14 = (bf16[1,512,768]{2,1,0:T(8,128)(2,1)S(1)}, bf16[1,512,768]{2,1,0:T(8,128)(2,1)S(1)}, u32[]{:S(2)}, u32[]{:S(2)}) collective-permute-start(bf16[1,512,768]{2,1,0:T(8,128)(2,1)S(1)} %dynamic-slice_bitcast_fusion.4), channel_id=1, source_target_pairs={{0,1},{1,0},{2,3},{3,2},{4,5},{5,4},{6,7},{7,6},{8,9},{9,8},{10,11... | collective-permute-start | bytes 2359304 | tf_op jit(solution)/shard_map/ppermute | solution.py:452
  (55 other events, 532.3 us)
Sparse Core Ops, SparseCore 0:
  11.4 84.5 all-gather.3
  98.7 112.3 all-gather.5
  386.0 58.0 all-gather.7
  450.0 172.6 reduce-scatter.1

commit v6 on v5

--- a/solution.py
+++ b/solution.py
@@ -79,7 +79,7 @@
         start = (stat_in[0, 0, 0:1, :], o_in[0], stat_in[0, 0, 1:2, :])
     row_max, mixed, total = lax.fori_loop(0, keys // bk, step, start)
     if last:
-        mixed = mixed / total
+        mixed = mixed * (1.0 / total)
         o_ref[0] = mixed
         refs[-4][0] = mixed.astype(B)
         stat_ref[0, 0] = row_max + jnp.log2(total)
@@ -388,7 +388,7 @@
     return lax.ppermute(first, "ctx", down), lax.ppermute(second, "ctx", up)
 
 
-def scatter_sum(blocks, order):
+def scatter_sum(blocks, order, extra=None):
     sizes = {axis: lax.axis_size(axis) for axis in WEIGHT_AXES}
     bits = []
     for axis in WEIGHT_AXES:
@@ -407,25 +407,26 @@
         mine = (lax.axis_index(axis) // bit) % 2
         sent = lax.dynamic_index_in_dim(left, 1 - mine, dim, keepdims=False)
         kept = lax.dynamic_index_in_dim(left, mine, dim, keepdims=False)
-        got = lax.ppermute(sent, axis, [(i, i ^ bit) for i in range(sizes[axis])])
+        pairs = [(i, i ^ bit) for i in range(sizes[axis])]
+        if extra is None:
+            got = lax.ppermute(sent, axis, pairs)
+        else:
+            columns = sent.shape[-1]
+            high, low = split_low(extra, 2)
+            tail = jnp.concatenate([high, low]).reshape(-1, columns)
+            flat = sent.reshape(-1, columns)
+            joined = lax.ppermute(jnp.concatenate([flat, tail], axis=0), axis, pairs)
+            got = joined[: flat.shape[0]].reshape(sent.shape)
+            other = joined[flat.shape[0] :].reshape(2, -1).astype(F)
+            extra = (high.astype(F) + low.astype(F)) + (other[0] + other[1])
         total = kept.astype(F) + got.astype(F)
         left = total.astype(B) if bits else total
-    return left
+    return left if extra is None else (left, extra)
 
 
 def sum_all(vector):
     every = lax.all_gather(vector.reshape(-1, 128), ("fsdp", "ctx", "tp"), axis=0)
     return jnp.sum(every, axis=0).reshape(-1)
-
-
-def sum_steps(vector):
-    for axis in ("fsdp", "tp", "ctx"):
-        size = lax.axis_size(axis)
-        bit = 1
-        while bit < size:
-            vector = vector + lax.ppermute(vector, axis, [(i, i ^ bit) for i in range(size)])
-            bit *= 2
-    return vector
 
 
 def tp_gather(vector):
@@ -627,19 +628,16 @@
         if got is not None:
             part = part + jnp.concatenate(got, axis=0).astype(F)
         own_grads.append(part)
-    q_bias_grad = sum_steps(q_bias_grad.reshape(-1))
     qkv_grad = jnp.stack(
         [jnp.concatenate([q_grad[t], kv_grad[t]], axis=1).astype(B) for t in range(tp_count)]
     )
     qkv_grad = qkv_grad.reshape(tp_count, width // shard_rows, shard_rows, 3 * head_width)
-    cut = (3 * head_width // 256) * 128
-    qkv_grad = jnp.concatenate(
-        [
-            scatter_sum(qkv_grad[..., :cut], ("tp", "fsdp", "ctx")),
-            scatter_sum(qkv_grad[..., cut:], ("fsdp", "tp", "ctx")),
-        ],
-        axis=1,
-    )
+    cut = 2 * head_width - 128
+    second_part, q_bias_grad = scatter_sum(
+        qkv_grad[..., cut:], ("fsdp", "tp", "ctx"), q_bias_grad.reshape(-1)
+    )
+    first_part = scatter_sum(qkv_grad[..., :cut], ("tp", "fsdp", "ctx"))
+    qkv_grad = jnp.concatenate([first_part, second_part], axis=1)
     tokens_grad = resid_grad.reshape(own_seqs, local_len, width) + jnp.stack(own_grads)
     tokens_out = tp_exchange(tokens_grad.astype(B))
 

time: 740 us -> 725 us (0.980)
  waiting for transfers between devices: 212 us -> 196 us
    ppermute x15 -> x10, waiting for transfers between devices: 57.9 us -> 35.1 us  [the longest x5 20.2 us: scatter_sum(): joined = lax.ppermute(jnp.concatenate([flat, tail], axis=0), axis, pairs)]
    ppermute x15 -> x10, starting transfers between devices: 18.4 us -> 11.3 us  [the longest x5 6.93 us: scatter_sum(): got = lax.ppermute(sent, axis, pairs)]
    unnamed x104 -> x114, local copies, waits for them, and re-layouts: 16.5 us -> 18.4 us
  transfers between devices with their start and end apart: 34 -> 29, of which waited for: 18 -> 16; matrix products, arithmetic and copies ran while one was open for 14% -> 16% of each run, Pallas kernels for 25% -> 31%
where the time goes in v6:
time: 725 us; the launch traced here: 720 us
  Pallas kernels  289 us (40%)
  waiting for transfers between devices  196 us (27%)
  matrix products  74.4 us (10%)
  starting transfers between devices  59.8 us (8%)
  local copies, waits for them, and re-layouts  51.7 us (7%)
  other arithmetic  33.4 us (5%)
  between operations  15.4 us (2%)
    pallas_call x4, Pallas kernels, attention_backward(): pl.pallas_call(lambda *refs: backward_kernel(*refs, first=first, bk=bk, b...  145 us
    ppermute x6, waiting for transfers between devices, ring_return(): return (lax.ppermute(first, 'ctx', down), lax.ppermute(second, 'ctx', up))  77.3 us
    pallas_call x2, Pallas kernels, attention_forward(): pl.pallas_call(lambda *refs: forward_kernel(*refs, chunks=chunks, first=f...  75.4 us
    dot_general x28, matrix products, dot(): lax.dot_general(left, right, (((left_dim,), (right_dim,)), ((), ())), pre...  74.4 us
    ppermute x3, waiting for transfers between devices, ring_gather(): first = lax.ppermute(first, 'ctx', up)  51 us
    ppermute x3, waiting for transfers between devices, ring_gather(): second = lax.ppermute(second, 'ctx', down)  32.6 us
    ppermute x3, starting transfers between devices, ring_gather(): first = lax.ppermute(first, 'ctx', up)  32.2 us
    pallas_call x1, Pallas kernels, ffn_forward(): pl.pallas_call(lambda *refs: ffn_forward_kernel(*refs, br=pick_block(rows...  29.4 us
  transfers between devices with their start and end apart: 29, of which 16 were waited for; matrix products, arithmetic and copies ran while one was open for 16% of the time, Pallas kernels for 31%

profile of v6, /device:TPU:0, one launch (start us, length us, event | category | flops | bytes accessed | tf_op | source)
XLA Modules:
  0.0 719.5 jit_solution(8221052959993999006)
XLA Ops:
  19.2 21.1 %collective-permute-done.1 = bf16[512,768]{1,0:T(8,128)(2,1)} collective-permute-done((bf16[512,768]{1,0:T(8,128)(2,1)S(1)}, bf16[512,768]{1,0:T(8,128)(2,1)}, u32[]{:S(2)}, u32[]{:S(2)}) %collective-permute-start.1) | collective-permute-done | bytes 786464 | tf_op jit(solution)/shard_map/ppermute | solution.py:378
  40.3 10.3 %collective-permute-start.2 = (bf16[512,768]{1,0:T(8,128)(2,1)}, bf16[512,768]{1,0:T(8,128)(2,1)}, u32[]{:S(2)}, u32[]{:S(2)}) collective-permute-start(bf16[512,768]{1,0:T(8,128)(2,1)} %collective-permute-done.1), channel_id=1, source_target_pairs={{0,2},{2,4},{4,6},{6,0},{1,3},{3,5},{5,7},{7,1},{8,10},{10,12},{12... | collective-permute-start | bytes 2359304 | tf_op jit(solution)/shard_map/ppermute | solution.py:378
  50.6 12.7 %collective-permute-done.3 = bf16[512,768]{1,0:T(8,128)(2,1)} collective-permute-done((bf16[512,768]{1,0:T(8,128)(2,1)S(1)}, bf16[512,768]{1,0:T(8,128)(2,1)}, u32[]{:S(2)}, u32[]{:S(2)}) %collective-permute-start.3) | collective-permute-done | bytes 786464 | tf_op jit(solution)/shard_map/ppermute | solution.py:379
  70.1 15.1 %collective-permute-done.2 = bf16[512,768]{1,0:T(8,128)(2,1)} collective-permute-done((bf16[512,768]{1,0:T(8,128)(2,1)}, bf16[512,768]{1,0:T(8,128)(2,1)}, u32[]{:S(2)}, u32[]{:S(2)}) %collective-permute-start.2) | collective-permute-done | bytes 786464 | tf_op jit(solution)/shard_map/ppermute | solution.py:378
  85.2 18.8 %collective-permute-start.5 = (bf16[512,768]{1,0:T(8,128)(2,1)}, bf16[512,768]{1,0:T(8,128)(2,1)S(1)}, u32[]{:S(2)}, u32[]{:S(2)}) collective-permute-start(bf16[512,768]{1,0:T(8,128)(2,1)} %collective-permute-done.2), channel_id=1, source_target_pairs={{0,2},{2,4},{4,6},{6,0},{1,3},{3,5},{5,7},{7,1},{8,10},{10,12},{12... | collective-permute-start | bytes 2359304 | tf_op jit(solution)/shard_map/ppermute | solution.py:378
  114.4 14.8 %collective-permute-done.5 = bf16[512,768]{1,0:T(8,128)(2,1)S(1)} collective-permute-done((bf16[512,768]{1,0:T(8,128)(2,1)}, bf16[512,768]{1,0:T(8,128)(2,1)S(1)}, u32[]{:S(2)}, u32[]{:S(2)}) %collective-permute-start.5) | collective-permute-done | bytes 786464 | tf_op jit(solution)/shard_map/ppermute | solution.py:378
  129.3 17.3 %collective-permute-done.6 = bf16[512,768]{1,0:T(8,128)(2,1)S(1)} collective-permute-done((bf16[512,768]{1,0:T(8,128)(2,1)}, bf16[512,768]{1,0:T(8,128)(2,1)S(1)}, u32[]{:S(2)}, u32[]{:S(2)}) %collective-permute-start.6) | collective-permute-done | bytes 786464 | tf_op jit(solution)/shard_map/ppermute | solution.py:379
  171.1 34.5 %attn_forward.2 = (f32[2,384,1024]{2,1,0:T(8,128)}, f32[2,6,2,1024]{3,2,1,0:T(2,128)}) custom-call(bf16[2,384,1024]{2,1,0:T(8,128)(2,1)} %add_convert_fusion.7.refs_0_, bf16[2,2,384,1024]{3,2,1,0:T(8,128)(2,1)} %bitcast.312, bf16[2,2,384,1024]{3,2,1,0:T(8,128)(2,1)} %bitcast.314), custom_call_target="tpu_custom_call" | custom-call | flops 25769803776 | bytes 16777216 | tf_op jit(solution)/shard_map/attn_forward/pallas_call | solution.py:104
  205.6 40.9 %attn_forward.3 = (f32[2,384,1024]{2,1,0:T(8,128)}, f32[2,6,1,1024]{3,2,1,0:T(1,128)}, bf16[2,384,1024]{2,1,0:T(8,128)(2,1)}) custom-call(bf16[2,384,1024]{2,1,0:T(8,128)(2,1)} %add_convert_fusion.7.refs_0_, bf16[2,2,384,1024]{3,2,1,0:T(8,128)(2,1)} %bitcast.316, bf16[2,2,384,1024]{3,2,1,0:T(8,128)(2,1)} %bitcast.318, ...), custom_call_target="tpu_custom_call" | custom-call | flops 25769803776 | bytes 16777216 | tf_op jit(solution)/shard_map/attn_forward/pallas_call | solution.py:104
  253.9 29.4 %ffn_forward.1 = (bf16[1024,3072]{1,0:T(8,128)(2,1)}, f32[1024,3072]{1,0:T(8,128)}, f32[1024,768]{1,0:T(8,128)}) custom-call(bf16[1024,768]{1,0:T(8,128)(2,1)} %fusion.9.refs_0_.refs_1_, bf16[2,768,3456]{2,1,0:T(8,128)(2,1)} %bitcast.244, bf16[2,768,3456]{2,1,0:T(8,128)(2,1)} %bitcast.245, f32[1,3072]{1,0:T(1,128)} %bitcast.309), custom_call_target="tpu_custom_call" | custom-call | tf_op jit(solution)/shard_map/ffn_forward/pallas_call | solution.py:295
  292.1 16.6 %ffn_backward.1 = (bf16[1024,3072]{1,0:T(8,128)(2,1)}, f32[1,3072]{1,0:T(1,128)}, f32[1024,768]{1,0:T(8,128)}) custom-call(bf16[1024,768]{1,0:T(8,128)(2,1)} %get-tuple-element.114.refs_0_.refs_2_, bf16[2,768,3456]{2,1,0:T(8,128)(2,1)} %bitcast.246, bf16[2,768,3456]{2,1,0:T(8,128)(2,1)} %bitcast.247, f32[1024,3072]{1,0:T(8,128)} %get-tuple-element.44.refs_3_), custom_call_target="tpu_custom_call" | custom-call | tf_op jit(solution)/shard_map/ffn_backward/pallas_call | solution.py:316
  308.7 4.8 multiply_reduce_fusion
  319.2 21.9 %weight_grads.1 = bf16[2,768,3456]{2,1,0:T(8,128)(2,1)} custom-call(bf16[1024,768]{1,0:T(8,128)(2,1)} %copy-done.10, bf16[1024,768]{1,0:T(8,128)(2,1)} %fusion.9.refs_0_.refs_1_, bf16[1024,768]{1,0:T(8,128)(2,1)} %get-tuple-element.114.refs_0_.refs_2_, bf16[2,384,1024]{2,1,0:T(8,128)(2,1)} %get-tuple-element.42.refs_3_, ...), custom_call_target="tpu_custom_call" | custom-call | tf_op jit(solution)/shard_map/weight_grads/pallas_call | solution.py:352
  342.1 36.2 %attn_backward.4 = (f32[2,384,1024]{2,1,0:T(8,128)}, bf16[2,2,384,1024]{3,2,1,0:T(8,128)(2,1)}) custom-call(bf16[2,384,1024]{2,1,0:T(8,128)(2,1)} %add_convert_fusion.7.refs_0_, bf16[2,2,384,1024]{3,2,1,0:T(8,128)(2,1)} %bitcast.319, bf16[2,384,1024]{2,1,0:T(8,128)(2,1)} %copy-done.31, f32[2,6,1,1024]{3,2,1,0:T(1,128)} %get-tuple-element.49.refs_3_, ...), custom_call_target="tpu_custom_call" | custom-call | flops 25769803776 | bytes 16777216 | tf_op jit(solution)/shard_map/attn_backward/pallas_call | solution.py:193
  385.7 36.3 %attn_backward.5 = (f32[2,384,1024]{2,1,0:T(8,128)}, bf16[2,2,384,1024]{3,2,1,0:T(8,128)(2,1)}) custom-call(bf16[2,384,1024]{2,1,0:T(8,128)(2,1)} %add_convert_fusion.7.refs_0_, bf16[2,2,384,1024]{3,2,1,0:T(8,128)(2,1)} %bitcast.317, bf16[2,384,1024]{2,1,0:T(8,128)(2,1)} %copy-done.31, f32[2,6,1,1024]{3,2,1,0:T(1,128)} %get-tuple-element.49.refs_3_, ...), custom_call_target="tpu_custom_call" | custom-call | flops 25769803776 | bytes 16777216 | tf_op jit(solution)/shard_map/attn_backward/pallas_call | solution.py:193
  440.7 17.9 %collective-permute-done.8 = bf16[512,768]{1,0:T(8,128)(2,1)} collective-permute-done((bf16[512,768]{1,0:T(8,128)(2,1)}, bf16[512,768]{1,0:T(8,128)(2,1)}, u32[]{:S(2)}, u32[]{:S(2)}) %collective-permute-start.8) | collective-permute-done | bytes 786464 | tf_op jit(solution)/shard_map/ppermute | solution.py:388
  460.5 36.4 %attn_backward.6 = (f32[2,384,1024]{2,1,0:T(8,128)}, bf16[2,2,384,1024]{3,2,1,0:T(8,128)(2,1)}) custom-call(bf16[2,384,1024]{2,1,0:T(8,128)(2,1)} %add_convert_fusion.7.refs_0_, bf16[2,2,384,1024]{3,2,1,0:T(8,128)(2,1)} %bitcast.315, bf16[2,384,1024]{2,1,0:T(8,128)(2,1)} %copy-done.31, f32[2,6,1,1024]{3,2,1,0:T(1,128)} %get-tuple-element.49.refs_3_, ...), custom_call_target="tpu_custom_call" | custom-call | flops 25769803776 | bytes 16777216 | tf_op jit(solution)/shard_map/attn_backward/pallas_call | solution.py:193
  512.7 22.9 %collective-permute-done.10 = bf16[512,768]{1,0:T(8,128)(2,1)S(1)} collective-permute-done((bf16[512,768]{1,0:T(8,128)(2,1)S(1)}, bf16[512,768]{1,0:T(8,128)(2,1)S(1)}, u32[]{:S(2)}, u32[]{:S(2)}) %collective-permute-start.10) | collective-permute-done | bytes 786464 | tf_op jit(solution)/shard_map/ppermute | solution.py:388
  535.6 18.7 %collective-permute-done.11 = bf16[512,768]{1,0:T(8,128)(2,1)S(1)} collective-permute-done((bf16[512,768]{1,0:T(8,128)(2,1)S(1)}, bf16[512,768]{1,0:T(8,128)(2,1)S(1)}, u32[]{:S(2)}, u32[]{:S(2)}) %collective-permute-start.11) | collective-permute-done | bytes 786464 | tf_op jit(solution)/shard_map/ppermute | solution.py:388
  555.8 36.5 %attn_backward.7 = (bf16[2,384,1024]{2,1,0:T(8,128)(2,1)}, bf16[2,2,384,1024]{3,2,1,0:T(8,128)(2,1)}) custom-call(bf16[2,384,1024]{2,1,0:T(8,128)(2,1)} %add_convert_fusion.7.refs_0_, bf16[2,2,384,1024]{3,2,1,0:T(8,128)(2,1)} %bitcast.313, bf16[2,384,1024]{2,1,0:T(8,128)(2,1)} %copy-done.31, f32[2,6,1,1024]{3,2,1,0:T(1,128)} %get-tuple-element.49.refs_3_, ...), custom_call_target="tpu_custom_call" | custom-call | flops 25769803776 | bytes 16777216 | tf_op jit(solution)/shard_map/attn_backward/pallas_call | solution.py:193
  632.4 17.9 %collective-permute-done.12 = bf16[512,768]{1,0:T(8,128)(2,1)} collective-permute-done((bf16[512,768]{1,0:T(8,128)(2,1)}, bf16[512,768]{1,0:T(8,128)(2,1)}, u32[]{:S(2)}, u32[]{:S(2)}) %collective-permute-start.12) | collective-permute-done | bytes 786464 | tf_op jit(solution)/shard_map/ppermute | solution.py:388
  650.3 4.9 add_convert_fusion.4
  663.0 18.1 %collective-permute-done.22 = bf16[195,512]{1,0:T(8,128)(2,1)S(1)} collective-permute-done((bf16[195,512]{1,0:T(8,128)(2,1)S(1)}, bf16[195,512]{1,0:T(8,128)(2,1)S(1)}, u32[]{:S(2)}, u32[]{:S(2)}) %collective-permute-start.22) | collective-permute-done | bytes 199712 | tf_op jit(solution)/shard_map/ppermute | solution.py:418
  682.9 6.9 collective-permute-done.16
  (328 shorter events, 193.4 us)
Async XLA Ops:
  7.2 139.4 %all-gather.4.cloned.1.call-start = ((), (), s32[]{:S(2)}) async-start(), calls=%async_computation.1 | async-start | bytes 4055040 | tf_op jit(solution)/shard_map/all_gather | solution.py:508
  10.5 236.1 %all-gather.6.cloned.1.call-start = ((), (), s32[]{:S(2)}) async-start(), calls=%async_computation.2 | async-start | bytes 10948608 | tf_op jit(solution)/shard_map/all_gather | solution.py:512
  12.5 610.7 %all-gather.8.cloned.1.call-start = ((), (), s32[]{:S(2)}) async-start(), calls=%async_computation.3 | async-start | bytes 1216512 | tf_op jit(solution)/shard_map/all_gather | solution.py:428
  14.0 26.3 %collective-permute-start.1 = (bf16[512,768]{1,0:T(8,128)(2,1)S(1)}, bf16[512,768]{1,0:T(8,128)(2,1)}, u32[]{:S(2)}, u32[]{:S(2)}) collective-permute-start(bf16[512,768]{1,0:T(8,128)(2,1)S(1)} %get-tuple-element.145), channel_id=1, source_target_pairs={{0,2},{2,4},{4,6},{6,0},{1,3},{3,5},{5,7},{7,1},{8,10},{10,12},{12... | collective-permute-start | bytes 2359304 | tf_op jit(solution)/shard_map/ppermute | solution.py:378
  17.1 46.2 %collective-permute-start.3 = (bf16[512,768]{1,0:T(8,128)(2,1)S(1)}, bf16[512,768]{1,0:T(8,128)(2,1)}, u32[]{:S(2)}, u32[]{:S(2)}) collective-permute-start(bf16[512,768]{1,0:T(8,128)(2,1)S(1)} %get-tuple-element.144), channel_id=1, source_target_pairs={{2,0},{4,2},{6,4},{0,6},{3,1},{5,3},{7,5},{1,7},{10,8},{12,10},{14... | collective-permute-start | bytes 2359304 | tf_op jit(solution)/shard_map/ppermute | solution.py:379
  40.3 44.9 %collective-permute-start.2 = (bf16[512,768]{1,0:T(8,128)(2,1)}, bf16[512,768]{1,0:T(8,128)(2,1)}, u32[]{:S(2)}, u32[]{:S(2)}) collective-permute-start(bf16[512,768]{1,0:T(8,128)(2,1)} %collective-permute-done.1), channel_id=1, source_target_pairs={{0,2},{2,4},{4,6},{6,0},{1,3},{3,5},{5,7},{7,1},{8,10},{10,12},{12... | collective-permute-start | bytes 2359304 | tf_op jit(solution)/shard_map/ppermute | solution.py:378
  63.3 43.3 %collective-permute-start.4 = (bf16[512,768]{1,0:T(8,128)(2,1)}, bf16[512,768]{1,0:T(8,128)(2,1)}, u32[]{:S(2)}, u32[]{:S(2)}) collective-permute-start(bf16[512,768]{1,0:T(8,128)(2,1)} %collective-permute-done.3), channel_id=1, source_target_pairs={{2,0},{4,2},{6,4},{0,6},{3,1},{5,3},{7,5},{1,7},{10,8},{12,10},{14... | collective-permute-start | bytes 2359304 | tf_op jit(solution)/shard_map/ppermute | solution.py:379
  85.2 44.0 %collective-permute-start.5 = (bf16[512,768]{1,0:T(8,128)(2,1)}, bf16[512,768]{1,0:T(8,128)(2,1)S(1)}, u32[]{:S(2)}, u32[]{:S(2)}) collective-permute-start(bf16[512,768]{1,0:T(8,128)(2,1)} %collective-permute-done.2), channel_id=1, source_target_pairs={{0,2},{2,4},{4,6},{6,0},{1,3},{3,5},{5,7},{7,1},{8,10},{10,12},{12... | collective-permute-start | bytes 2359304 | tf_op jit(solution)/shard_map/ppermute | solution.py:378
  106.7 39.9 %collective-permute-start.6 = (bf16[512,768]{1,0:T(8,128)(2,1)}, bf16[512,768]{1,0:T(8,128)(2,1)S(1)}, u32[]{:S(2)}, u32[]{:S(2)}) collective-permute-start(bf16[512,768]{1,0:T(8,128)(2,1)} %collective-permute-done.4), channel_id=1, source_target_pairs={{2,0},{4,2},{6,4},{0,6},{3,1},{5,3},{7,5},{1,7},{10,8},{12,10},{14... | collective-permute-start | bytes 2359304 | tf_op jit(solution)/shard_map/ppermute | solution.py:379
  342.1 367.4 %reduce-scatter.2.cloned.1.call-start = ((), (), s32[]{:S(2)}) async-start(), calls=%async_computation.4 | async-start | bytes 10948608 | tf_op jit(solution)/shard_map/reduce_scatter | solution.py:584
  421.9 36.7 %collective-permute-start.8 = (bf16[512,768]{1,0:T(8,128)(2,1)}, bf16[512,768]{1,0:T(8,128)(2,1)}, u32[]{:S(2)}, u32[]{:S(2)}) collective-permute-start(bf16[512,768]{1,0:T(8,128)(2,1)} %get-tuple-element.55), channel_id=1, source_target_pairs={{2,0},{4,2},{6,4},{0,6},{3,1},{5,3},{7,5},{1,7},{10,8},{12,10},{14... | collective-permute-start | bytes 2359304 | tf_op jit(solution)/shard_map/ppermute | solution.py:388
  423.9 34.7 %collective-permute-start.9 = (bf16[512,768]{1,0:T(8,128)(2,1)}, bf16[512,768]{1,0:T(8,128)(2,1)}, u32[]{:S(2)}, u32[]{:S(2)}) collective-permute-start(bf16[512,768]{1,0:T(8,128)(2,1)} %get-tuple-element.56), channel_id=1, source_target_pairs={{0,2},{2,4},{4,6},{6,0},{1,3},{3,5},{5,7},{7,1},{8,10},{10,12},{12... | collective-permute-start | bytes 2359304 | tf_op jit(solution)/shard_map/ppermute | solution.py:388
  425.1 82.3 %collective-permute-start.7 = (bf16[1,512,768]{2,1,0:T(8,128)(2,1)}, bf16[1,512,768]{2,1,0:T(8,128)(2,1)}, u32[]{:S(2)}, u32[]{:S(2)}) collective-permute-start(bf16[1,512,768]{2,1,0:T(8,128)(2,1)} %dynamic-slice_bitcast_fusion.4), channel_id=1, source_target_pairs={{0,1},{1,0},{2,3},{3,2},{4,5},{5,4},{6,7},{7,6},{8,9},{9,8},{10,11... | collective-permute-start | bytes 2359304 | tf_op jit(solution)/shard_map/ppermute | solution.py:453
  499.2 36.4 %collective-permute-start.10 = (bf16[512,768]{1,0:T(8,128)(2,1)S(1)}, bf16[512,768]{1,0:T(8,128)(2,1)S(1)}, u32[]{:S(2)}, u32[]{:S(2)}) collective-permute-start(bf16[512,768]{1,0:T(8,128)(2,1)S(1)} %get-tuple-element.60), channel_id=1, source_target_pairs={{2,0},{4,2},{6,4},{0,6},{3,1},{5,3},{7,5},{1,7},{10,8},{12,10},{14... | collective-permute-start | bytes 2359304 | tf_op jit(solution)/shard_map/ppermute | solution.py:388
  500.9 53.4 %collective-permute-start.11 = (bf16[512,768]{1,0:T(8,128)(2,1)S(1)}, bf16[512,768]{1,0:T(8,128)(2,1)S(1)}, u32[]{:S(2)}, u32[]{:S(2)}) collective-permute-start(bf16[512,768]{1,0:T(8,128)(2,1)S(1)} %get-tuple-element.61), channel_id=1, source_target_pairs={{0,2},{2,4},{4,6},{6,0},{1,3},{3,5},{5,7},{7,1},{8,10},{10,12},{12... | collective-permute-start | bytes 2359304 | tf_op jit(solution)/shard_map/ppermute | solution.py:388
  611.5 15.7 %collective-permute-start.20 = (bf16[771,512]{1,0:T(8,128)(2,1)}, bf16[771,512]{1,0:T(8,128)(2,1)}, u32[]{:S(2)}, u32[]{:S(2)}) collective-permute-start(bf16[771,512]{1,0:T(8,128)(2,1)} %pad_maximum_fusion), channel_id=1, source_target_pairs={{0,8},{8,0},{16,24},{24,16},{1,9},{9,1},{17,25},{25,17},{2,10},{10... | collective-permute-start | bytes 2368520 | tf_op jit(solution)/shard_map/ppermute | solution.py:418
  613.1 46.8 %collective-permute-start.15 = (bf16[2,2,2,2,48,640]{5,4,3,2,1,0:T(8,128)(2,1)}, bf16[2,2,2,2,48,640]{5,4,3,2,1,0:T(8,128)(2,1)}, u32[]{:S(2)}, u32[]{:S(2)}) collective-permute-start(bf16[2,2,2,2,48,640]{5,4,3,2,1,0:T(8,128)(2,1)} %dynamic-slice_bitcast_fusion), channel_id=1, source_target_pairs={{0,8},{8,0},{16,24},{24,16},{1,9},{9,1},{17,25},{25,17},{2,10},{10... | collective-permute-start | bytes 2949128 | tf_op jit(solution)/shard_map/ppermute | solution.py:412
  613.6 36.6 %collective-permute-start.12 = (bf16[512,768]{1,0:T(8,128)(2,1)}, bf16[512,768]{1,0:T(8,128)(2,1)}, u32[]{:S(2)}, u32[]{:S(2)}) collective-permute-start(bf16[512,768]{1,0:T(8,128)(2,1)} %get-tuple-element.66), channel_id=1, source_target_pairs={{2,0},{4,2},{6,4},{0,6},{3,1},{5,3},{7,5},{1,7},{10,8},{12,10},{14... | collective-permute-start | bytes 2359304 | tf_op jit(solution)/shard_map/ppermute | solution.py:388
  614.2 36.1 %collective-permute-start.13 = (bf16[512,768]{1,0:T(8,128)(2,1)}, bf16[512,768]{1,0:T(8,128)(2,1)}, u32[]{:S(2)}, u32[]{:S(2)}) collective-permute-start(bf16[512,768]{1,0:T(8,128)(2,1)} %get-tuple-element.67), channel_id=1, source_target_pairs={{0,2},{2,4},{4,6},{6,0},{1,3},{3,5},{5,7},{7,1},{8,10},{10,12},{12... | collective-permute-start | bytes 2359304 | tf_op jit(solution)/shard_map/ppermute | solution.py:388
  630.9 28.1 %collective-permute-start.21 = (bf16[387,512]{1,0:T(8,128)(2,1)S(1)}, bf16[387,512]{1,0:T(8,128)(2,1)S(1)}, u32[]{:S(2)}, u32[]{:S(2)}) collective-permute-start(bf16[387,512]{1,0:T(8,128)(2,1)S(1)} %pad_maximum_fusion.1), channel_id=1, source_target_pairs={{0,16},{8,24},{16,0},{24,8},{1,17},{9,25},{17,1},{25,9},{2,18},{10... | collective-permute-start | bytes 1188872 | tf_op jit(solution)/shard_map/ppermute | solution.py:418
  656.1 49.1 %collective-permute-start.14 = (bf16[1,512,768]{2,1,0:T(8,128)(2,1)}, bf16[1,512,768]{2,1,0:T(8,128)(2,1)}, u32[]{:S(2)}, u32[]{:S(2)}) collective-permute-start(bf16[1,512,768]{2,1,0:T(8,128)(2,1)} %dynamic-slice_bitcast_fusion.3), channel_id=1, source_target_pairs={{0,1},{1,0},{2,3},{3,2},{4,5},{5,4},{6,7},{7,6},{8,9},{9,8},{10,11... | collective-permute-start | bytes 2359304 | tf_op jit(solution)/shard_map/ppermute | solution.py:453
  659.3 21.8 %collective-permute-start.22 = (bf16[195,512]{1,0:T(8,128)(2,1)S(1)}, bf16[195,512]{1,0:T(8,128)(2,1)S(1)}, u32[]{:S(2)}, u32[]{:S(2)}) collective-permute-start(bf16[195,512]{1,0:T(8,128)(2,1)S(1)} %pad_maximum_fusion.4), channel_id=1, source_target_pairs={{0,1},{1,0},{2,3},{3,2},{4,5},{5,4},{6,7},{7,6},{8,9},{9,8},{10,11... | collective-permute-start | bytes 599048 | tf_op jit(solution)/shard_map/ppermute | solution.py:418
  661.4 28.4 %collective-permute-start.16 = (bf16[2,2,2,48,640]{4,3,2,1,0:T(8,128)(2,1)S(1)}, bf16[2,2,2,48,640]{4,3,2,1,0:T(8,128)(2,1)S(1)}, u32[]{:S(2)}, u32[]{:S(2)}) collective-permute-start(bf16[2,2,2,48,640]{4,3,2,1,0:T(8,128)(2,1)S(1)} %dynamic-slice_bitcast_fusion.6), channel_id=1, source_target_pairs={{0,1},{1,0},{2,3},{3,2},{4,5},{5,4},{6,7},{7,6},{8,9},{9,8},{10,11... | collective-permute-start | bytes 1474568 | tf_op jit(solution)/shard_map/ppermute | solution.py:412
  681.4 8.6 %collective-permute-start.23 = (bf16[99,512]{1,0:T(8,128)(2,1)S(1)}, bf16[99,512]{1,0:T(8,128)(2,1)S(1)}, u32[]{:S(2)}, u32[]{:S(2)}) collective-permute-start(bf16[99,512]{1,0:T(8,128)(2,1)S(1)} %pad_maximum_fusion.5), channel_id=1, source_target_pairs={{0,4},{2,6},{4,0},{6,2},{1,5},{3,7},{5,1},{7,3},{8,12},{10,14},{12... | collective-permute-start | bytes 304136 | tf_op jit(solution)/shard_map/ppermute | solution.py:418
  (55 other events, 595.2 us)
Sparse Core Ops, SparseCore 0:
  11.4 84.5 all-gather.3
  98.7 112.3 all-gather.5
  342.2 53.4 all-gather.7
  435.3 167.2 reduce-scatter.1
